TPU v7x, 32 devices: a whole 2x2x4 slice. The times are simulated.
32 devices in a mesh: row: 8 (over z, x), col: 4 (over y, core).
Axes of the slice: x: 2, y: 2, z: 4, core: 2. Of those that a mesh axis runs over, the one named last changes fastest.
Arguments:
- tokens: bfloat16 [512, 4096], P('row', 'col'), may hold values from -6 to 6
- gate_weight: bfloat16 [4096, 14336], P('col', 'row'), may hold values from -0.09375 to 0.09375
- up_weight: bfloat16 [4096, 14336], P('col', 'row'), may hold values from -0.09375 to 0.09375
- down_weight: bfloat16 [14336, 4096], P('row', 'col'), may hold values from -0.046875 to 0.046875
- gate_mask: int32 [32, 112], replicated, may hold values 0 or 1
- up_mask: int32 [32, 112], replicated, may hold values 0 or 1
- down_mask: int32 [112, 32], replicated, may hold values 0 or 1
- out_grad: bfloat16 [512, 4096], P('row', 'col'), may hold values from -6 to 6
Outputs:
- mixed: bfloat16 [512, 4096], P('row', 'col')
- input_grad: bfloat16 [512, 4096], P('row', 'col')
- gate_grad: float32 [4096, 14336], P('col', 'row')
- up_grad: float32 [4096, 14336], P('col', 'row')
- down_grad: float32 [14336, 4096], P('row', 'col')
All inputs are finite; a program needn't handle non-finite values.
Results may differ from a plain program's by a relative error of at most 0.0049.
Values may be sent and summed in bfloat16 or wider, within the bound.
No kernel may reach another device: no remote copies, remote signals or barrier semaphores. Data moves between devices by JAX's collectives and lax.ppermute only.
A program may use at most 128 MiB of HBM per device.

v0:
```python
import jax
import jax.numpy as jnp
from jax import lax
from jax.sharding import PartitionSpec as P

BLOCK = 128


def expand_mask(mask, row_start, row_count, col_start, col_count):
    row_block = (row_start + lax.broadcasted_iota(jnp.int32, (row_count, 1), 0)) // BLOCK
    left = (row_block == lax.broadcasted_iota(jnp.int32, (1, mask.shape[0]), 1)).astype(jnp.float32)
    col_block = (col_start + lax.broadcasted_iota(jnp.int32, (1, col_count), 1)) // BLOCK
    right = (lax.broadcasted_iota(jnp.int32, (mask.shape[1], 1), 0) == col_block).astype(
        jnp.float32
    )
    middle = jnp.dot(left, mask.astype(jnp.float32), precision=lax.Precision.HIGHEST)
    return jnp.dot(middle, right, precision=lax.Precision.HIGHEST)


def contract_first(left, right):
    return lax.dot_general(
        left, right, (((0,), (0,)), ((), ())), preferred_element_type=jnp.float32
    )


def contract_last(left, right):
    return lax.dot_general(
        left, right, (((1,), (1,)), ((), ())), preferred_element_type=jnp.float32
    )


def per_device(
    tokens, gate_weight, up_weight, down_weight, gate_mask, up_mask, down_mask, out_grad
):
    row_index = lax.axis_index("row")
    col_index = lax.axis_index("col")
    feat_cols = gate_weight.shape[0]
    unit_cols = gate_weight.shape[1]
    keep_gate = expand_mask(
        gate_mask, col_index * feat_cols, feat_cols, row_index * unit_cols, unit_cols
    )
    keep_up = expand_mask(
        up_mask, col_index * feat_cols, feat_cols, row_index * unit_cols, unit_cols
    )
    keep_down = expand_mask(
        down_mask, row_index * unit_cols, unit_cols, col_index * feat_cols, feat_cols
    )
    zero = jnp.zeros((), jnp.bfloat16)
    kept_both = jnp.concatenate(
        [jnp.where(keep_gate > 0, gate_weight, zero), jnp.where(keep_up > 0, up_weight, zero)],
        axis=1,
    )
    kept_down = jnp.where(keep_down > 0, down_weight, zero)
    gathered = lax.all_gather(tokens, "row", axis=0, tiled=True)
    block = gathered
    both = lax.psum_scatter(
        jnp.dot(block, kept_both, preferred_element_type=jnp.float32),
        "col",
        scatter_dimension=0,
        tiled=True,
    )
    gate = both[:, :unit_cols]
    up_part = both[:, unit_cols:]
    sig = jax.nn.sigmoid(gate)
    hidden = (gate * sig * up_part).astype(jnp.bfloat16)
    hidden_all = lax.all_gather(hidden, "col", axis=0, tiled=True)
    block = hidden_all
    mixed = lax.psum_scatter(
        jnp.dot(block, kept_down, preferred_element_type=jnp.float32),
        "row",
        scatter_dimension=0,
        tiled=True,
    ).astype(jnp.bfloat16)
    grad_all = lax.all_gather(out_grad, "row", axis=0, tiled=True)
    down_grad = keep_down * contract_first(hidden_all, grad_all)
    block = grad_all
    hidden_grad = lax.psum_scatter(
        contract_last(block, kept_down), "col", scatter_dimension=0, tiled=True
    )
    dgate = hidden_grad * up_part * sig * (1.0 + gate * (1.0 - sig))
    dup = hidden_grad * gate * sig
    pre_grad = jnp.concatenate([dgate.astype(jnp.bfloat16), dup.astype(jnp.bfloat16)], axis=1)
    pre_all = lax.all_gather(pre_grad, "col", axis=0, tiled=True)
    weight_both = contract_first(gathered, pre_all)
    gate_grad = keep_gate * weight_both[:, :unit_cols]
    up_grad = keep_up * weight_both[:, unit_cols:]
    block = pre_all
    input_grad = lax.psum_scatter(
        contract_last(block, kept_both), "row", scatter_dimension=0, tiled=True
    ).astype(jnp.bfloat16)
    return (mixed, input_grad, gate_grad, up_grad, down_grad)


def solution(mesh):
    return jax.shard_map(
        per_device,
        mesh=mesh,
        in_specs=(
            P("row", "col"),
            P("col", "row"),
            P("col", "row"),
            P("row", "col"),
            P(),
            P(),
            P(),
            P("row", "col"),
        ),
        out_specs=(
            P("row", "col"),
            P("row", "col"),
            P("col", "row"),
            P("col", "row"),
            P("row", "col"),
        ),
        check_vma=False,
    )
```

profile of v0, /device:TPU:0, one launch (start us, length us, event | category | flops | bytes accessed | tf_op | source)
XLA Modules:
  0.0 412.9 jit_solution(11120879040870394195)
XLA Ops:
  7.2 0.0 all-gather.9.cloned.1.call-start
  7.2 0.7 all-gather.9.cloned.1.call-update
  7.9 0.0 all-gather.5.cloned.1.call-start
  7.9 0.7 all-gather.5.cloned.1.call-update
  8.7 0.0 reduce-scatter.9.cloned.1.call-start
  8.7 1.4 fusion.1
  10.1 5.0 %fusion.11 = f32[1792,1024]{1,0:T(8,128)} fusion(f32[1792,32]{1,0:T(8,128)S(1)} %fusion.1, s32[1024]{0:T(1024)S(1)} %add_select_fusion.1), kind=kOutput, calls=%fused_computation.30 | convolution fusion | flops 704675840 | bytes 7573504 | tf_op jit(solution)/shard_map/dot_general | solution.py:17
  15.2 38.0 %all-gather.9.cloned.1.call-done = bf16[512,1024]{1,0:T(8,128)(2,1)} async-done(((bf16[64,1024]{1,0:T(8,128)(2,1)}), bf16[512,1024]{1,0:T(8,128)(2,1)}) %all-gather.9.cloned.1.call-update) | async-done | bytes 1048592 | tf_op jit(solution)/shard_map/all_gather | solution.py:74
  53.1 8.3 %convolution_bitcast_fusion.2 = f32[512,1792]{0,1:T(8,128)} fusion(bf16[512,1024]{1,0:T(8,128)(2,1)} %all-gather.9.cloned.1.call-done, bf16[1792,1024]{1,0:T(8,128)(2,1)} %param.11, f32[1792,1024]{1,0:T(8,128)} %fusion.11), kind=kOutput, calls=%fused_computation.10 | convolution fusion | flops 1882718208 | bytes 15728640 | tf_op jit(solution)/shard_map/dot_general | solution.py:27
  61.4 0.0 copy-start.1
  61.4 0.0 copy-start.2
  61.4 0.0 reduce-scatter.9.cloned.1.call-update
  61.4 0.2 reduce-scatter.5.cloned.1.call-start
  61.7 0.5 copy-done.1
  62.1 0.5 fusion.4
  62.6 0.0 copy-done.2
  62.6 0.5 fusion.5
  63.1 0.0 copy-start
  63.1 7.6 %compare_select_fusion.2 = (bf16[1024,1792]{1,0:T(8,128)(2,1)}, f32[1024,1792]{1,0:T(8,128)}) fusion(bf16[1024,1792]{1,0:T(8,128)(2,1)} %param.9, f32[1024,112]{1,0:T(8,128)S(1)} %fusion.5, s32[1792]{0:T(1024)S(1)} %add_select_fusion), kind=kOutput, calls=%fused_computation.6 | convolution fusion | flops 2470121472 | bytes 15145984 | tf_op jit(solution)/shard_map/dot_general | solution.py:17
  70.7 0.0 copy-done
  70.7 5.9 %compare_select_fusion.1 = (bf16[1024,1792]{1,0:T(8,128)(2,1)}, f32[1024,1792]{1,0:T(8,128)}) fusion(bf16[1024,1792]{1,0:T(8,128)(2,1)S(1)} %copy-done, f32[1024,112]{1,0:T(8,128)S(1)} %fusion.4, s32[1792]{0:T(1024)S(1)} %add_select_fusion), kind=kOutput, calls=%fused_computation.5 | convolution fusion | flops 2470121472 | bytes 15145984 | tf_op jit(solution)/shard_map/dot_general | solution.py:17
  76.6 17.7 %all-gather.5.cloned.1.call-done = bf16[512,1024]{1,0:T(8,128)(2,1)} async-done(((bf16[64,1024]{1,0:T(8,128)(2,1)}), bf16[512,1024]{1,0:T(8,128)(2,1)}) %all-gather.5.cloned.1.call-update) | async-done | bytes 1048592 | tf_op jit(solution)/shard_map/all_gather | solution.py:54
  94.3 11.0 %convolution_bitcast_fusion.1 = f32[512,3584]{0,1:T(8,128)} fusion(bf16[512,1024]{1,0:T(8,128)(2,1)} %all-gather.5.cloned.1.call-done, bf16[1024,1792]{1,0:T(8,128)(2,1)} %get-tuple-element.10, bf16[1024,1792]{1,0:T(8,128)(2,1)} %get-tuple-element.12), kind=kOutput, calls=%fused_computation.7 | convolution fusion | flops 3772776448 | bytes 15728640 | tf_op jit(solution)/shard_map/dot_general | solution.py:57
  105.2 0.0 reduce-scatter.5.cloned.1.call-update
  105.3 0.0 all-gather.7.cloned.1.call-start
  105.3 31.3 %reduce-scatter.9.cloned.1.call-done = f32[128,1792]{0,1:T(8,128)} async-done(((f32[512,1792]{0,1:T(8,128)}), f32[128,1792]{0,1:T(8,128)}) %reduce-scatter.9.cloned.1.call-update) | async-done | bytes 917520 | tf_op jit(solution)/shard_map/reduce_scatter | solution.py:77
  136.6 67.0 %reduce-scatter.5.cloned.1.call-done = f32[128,3584]{0,1:T(8,128)} async-done(((f32[512,3584]{0,1:T(8,128)}), f32[128,3584]{0,1:T(8,128)}) %reduce-scatter.5.cloned.1.call-update) | async-done | bytes 1835024 | tf_op jit(solution)/shard_map/reduce_scatter | solution.py:56
  203.7 3.1 multiply_convert_fusion.1
  206.7 0.0 all-gather.7.cloned.1.call-update
  206.8 0.0 all-gather.11.cloned.1.call-start
  206.8 1.0 pad_maximum_fusion.3
  207.8 0.0 all-gather.11.cloned.1.call-update
  207.9 0.0 reduce-scatter.7.cloned.1.call-start
  207.9 20.3 %all-gather.7.cloned.1.call-done = bf16[512,1792]{0,1:T(8,128)(2,1)} async-done(((bf16[128,1792]{0,1:T(8,128)(2,1)}), bf16[512,1792]{0,1:T(8,128)(2,1)}) %all-gather.7.cloned.1.call-update) | async-done | bytes 1835024 | tf_op jit(solution)/shard_map/all_gather | solution.py:66
  228.2 8.2 %fusion.24 = f32[512,1024]{1,0:T(8,128)} fusion(bf16[512,1792]{0,1:T(8,128)(2,1)} %all-gather.7.cloned.1.call-done, bf16[1792,1024]{1,0:T(8,128)(2,1)} %param.11, f32[1792,1024]{1,0:T(8,128)} %fusion.11), kind=kOutput, calls=%fused_computation.55 | convolution fusion | flops 1882718208 | bytes 14942208 | tf_op jit(solution)/shard_map/dot_general | solution.py:69
  236.4 0.0 reduce-scatter.7.cloned.1.call-update
  236.4 0.3 reduce-scatter.11.cloned.1.call-start
  236.7 24.9 %all-gather.11.cloned.1.call-done = bf16[512,3584]{0,1:T(8,128)(2,1)} async-done(((bf16[128,3584]{0,1:T(8,128)(2,1)}), bf16[512,3584]{0,1:T(8,128)(2,1)}) %all-gather.11.cloned.1.call-update) | async-done | bytes 3670032 | tf_op jit(solution)/shard_map/all_gather | solution.py:83
  261.6 9.5 %fusion = f32[512,1024]{1,0:T(8,128)} fusion(bf16[512,3584]{0,1:T(8,128)(2,1)} %all-gather.11.cloned.1.call-done, bf16[1024,1792]{1,0:T(8,128)(2,1)} %get-tuple-element.10, bf16[1024,1792]{1,0:T(8,128)(2,1)} %get-tuple-element.12), kind=kOutput, calls=%fused_computation.8 | convolution fusion | flops 3772776448 | bytes 13107200 | tf_op jit(solution)/shard_map/dot_general | solution.py:27
  271.2 0.0 slice-start
  271.2 0.0 reduce-scatter.11.cloned.1.call-update
  271.2 0.0 copy-start.3
  271.2 0.0 copy-start.4
  271.2 0.0 slice-start.1
  271.2 9.4 %convolution_multiply_fusion = f32[1792,1024]{1,0:T(8,128)} fusion(f32[1792,1024]{1,0:T(8,128)} %fusion.11, bf16[512,1792]{0,1:T(8,128)(2,1)} %all-gather.7.cloned.1.call-done, bf16[512,1024]{1,0:T(8,128)(2,1)} %all-gather.9.cloned.1.call-done), kind=kOutput, calls=%fused_computation.9 | convolution fusion | flops 1880883200 | bytes 17563648 | tf_op jit(solution)/shard_map/dot_general | solution.py:21
  280.6 0.0 copy-done.3
  280.6 0.0 copy-done.4
  280.6 7.6 %convolution_bitcast_fusion = f32[1024,3584]{1,0:T(8,128)} fusion(bf16[512,3584]{0,1:T(8,128)(2,1)S(1)} %copy-done.3, bf16[512,1024]{1,0:T(8,128)(2,1)S(1)} %copy-done.4), kind=kOutput, calls=%fused_computation | convolution fusion | flops 3758096384 | bytes 19398656 | tf_op jit(solution)/shard_map/dot_general | solution.py:21
  288.2 0.0 slice-done
  288.2 0.0 slice-done.1
  288.2 14.1 %slice_multiply_fusion = (f32[1024,1792]{1,0:T(8,128)}, f32[1024,1792]{1,0:T(8,128)}) fusion(f32[1024,1792]{1,0:T(8,128)} %get-tuple-element.11, f32[1024,3584]{1,0:T(8,128)} %convolution_bitcast_fusion, f32[1024,1792]{1,0:T(8,128)S(1)} %bitcast.18), kind=kLoop, calls=%fused_computation.1 | loop fusion | flops 3670016 | bytes 44040192 | tf_op jit(solution)/shard_map/mul | solution.py:86
  302.3 31.2 %reduce-scatter.7.cloned.1.call-done = f32[64,1024]{1,0:T(8,128)} async-done(((f32[512,1024]{1,0:T(8,128)}), f32[64,1024]{1,0:T(8,128)}) %reduce-scatter.7.cloned.1.call-update) | async-done | bytes 262160 | tf_op jit(solution)/shard_map/reduce_scatter | solution.py:68
  333.5 1.6 convert_element_type.34
  335.1 69.3 %reduce-scatter.11.cloned.1.call-done = f32[64,1024]{1,0:T(8,128)} async-done(((f32[512,1024]{1,0:T(8,128)}), f32[64,1024]{1,0:T(8,128)}) %reduce-scatter.11.cloned.1.call-update) | async-done | bytes 262160 | tf_op jit(solution)/shard_map/reduce_scatter | solution.py:88
  404.5 1.6 convert_element_type.37
  (3 shorter events, 0.0 us)
Async XLA Ops:
  7.2 46.0 %all-gather.9.cloned.1.call-start = ((), (), s32[]{:S(2)}) async-start(), calls=%async_computation.8 | async-start | bytes 1179648 | tf_op jit(solution)/shard_map/all_gather | solution.py:74
  7.9 86.4 %all-gather.5.cloned.1.call-start = ((), (), s32[]{:S(2)}) async-start(), calls=%async_computation.4 | async-start | bytes 1179648 | tf_op jit(solution)/shard_map/all_gather | solution.py:54
  8.7 128.0 %reduce-scatter.9.cloned.1.call-start = ((), (), s32[]{:S(2)}) async-start(), calls=%async_computation.9 | async-start | bytes 4587520 | tf_op jit(solution)/shard_map/reduce_scatter | solution.py:77
  61.4 0.7 copy-start.1
  61.4 1.2 copy-start.2
  61.4 142.2 %reduce-scatter.5.cloned.1.call-start = ((), (), s32[]{:S(2)}) async-start(), calls=%async_computation.5 | async-start | bytes 9175040 | tf_op jit(solution)/shard_map/reduce_scatter | solution.py:56
  63.1 7.6 %copy-start = (bf16[1024,1792]{1,0:T(8,128)(2,1)S(1)}, bf16[1024,1792]{1,0:T(8,128)(2,1)}, u32[]{:S(2)}) copy-start(bf16[1024,1792]{1,0:T(8,128)(2,1)} %param.10) | copy-start | bytes 11010052
  105.3 123.0 %all-gather.7.cloned.1.call-start = ((), (), s32[]{:S(2)}) async-start(), calls=%async_computation.6 | async-start | bytes 2293760 | tf_op jit(solution)/shard_map/all_gather | solution.py:66
  206.8 54.9 %all-gather.11.cloned.1.call-start = ((), (), s32[]{:S(2)}) async-start(), calls=%async_computation.10 | async-start | bytes 4587520 | tf_op jit(solution)/shard_map/all_gather | solution.py:83
  207.9 125.6 %reduce-scatter.7.cloned.1.call-start = ((), (), s32[]{:S(2)}) async-start(), calls=%async_computation.7 | async-start | bytes 2359296 | tf_op jit(solution)/shard_map/reduce_scatter | solution.py:68
  236.4 168.0 %reduce-scatter.11.cloned.1.call-start = ((), (), s32[]{:S(2)}) async-start(), calls=%async_computation.11 | async-start | bytes 2359296 | tf_op jit(solution)/shard_map/reduce_scatter | solution.py:88
  271.2 17.0 %slice-start = ((s8[7340032]{0:T(1024)(128)(4,1)}), s8[3145728]{0:T(1024)(128)(4,1)S(1)}, s32[]{:S(2)}) async-start(s8[7340032]{0:T(1024)(128)(4,1)} %bitcast.17), calls=%async_computation.12 | async-start | bytes 6291456
  271.2 9.4 %copy-start.3 = (bf16[512,3584]{0,1:T(8,128)(2,1)S(1)}, bf16[512,3584]{0,1:T(8,128)(2,1)}, u32[]{:S(2)}) copy-start(bf16[512,3584]{0,1:T(8,128)(2,1)} %all-gather.11.cloned.1.call-done) | copy-start | bytes 11010052
  271.2 9.4 %copy-start.4 = (bf16[512,1024]{1,0:T(8,128)(2,1)S(1)}, bf16[512,1024]{1,0:T(8,128)(2,1)}, u32[]{:S(2)}) copy-start(bf16[512,1024]{1,0:T(8,128)(2,1)} %all-gather.5.cloned.1.call-done) | copy-start | bytes 3145732
  271.2 17.0 %slice-start.1 = ((s8[7340032]{0:T(1024)(128)(4,1)}), s8[4194304]{0:T(1024)(128)(4,1)S(1)}, s32[]{:S(2)}) async-start(s8[7340032]{0:T(1024)(128)(4,1)} %bitcast.17), calls=%async_computation.13 | async-start | bytes 8388608
Sparse Core Ops, SparseCore 0:
  10.1 42.9 all-gather.8
  55.3 38.9 all-gather.4
  96.8 39.7 reduce-scatter.8
  139.0 64.6 reduce-scatter.4
  206.9 21.3 all-gather.6
  229.6 31.9 all-gather.10
  265.2 68.2 reduce-scatter.6
  337.0 67.3 reduce-scatter.10
where the time goes:
time: 413 us
  waiting for transfers between devices  301 us (73%)
  matrix products  74.7 us (18%)
  other arithmetic  21.4 us (5%)
  between operations  14.2 us (3%)
    reduce_scatter x1, waiting for transfers between devices, per_device(): lax.psum_scatter(contract_last(block, kept_both), 'row', scatter_dimensio...  69.3 us
    reduce_scatter x1, waiting for transfers between devices, per_device(): lax.psum_scatter(jnp.dot(block, kept_both, preferred_element_type=jnp.flo...  67 us
    all_gather x1, waiting for transfers between devices, per_device(): grad_all = lax.all_gather(out_grad, 'row', axis=0, tiled=True)  38 us
    reduce_scatter x1, waiting for transfers between devices, per_device(): lax.psum_scatter(contract_last(block, kept_down), 'col', scatter_dimensio...  31.3 us
    reduce_scatter x1, waiting for transfers between devices, per_device(): lax.psum_scatter(jnp.dot(block, kept_down, preferred_element_type=jnp.flo...  31.2 us
    all_gather x1, waiting for transfers between devices, per_device(): pre_all = lax.all_gather(pre_grad, 'col', axis=0, tiled=True)  24.9 us
    all_gather x1, waiting for transfers between devices, per_device(): hidden_all = lax.all_gather(hidden, 'col', axis=0, tiled=True)  20.3 us
    dot_general x3, matrix products, expand_mask(): return jnp.dot(middle, right, precision=lax.Precision.HIGHEST)  18.6 us
  transfers between devices with their start and end apart: 8, of which 8 were waited for; matrix products, arithmetic and copies ran while one was open for 22% of the time, Pallas kernels for 0%

commit v1 on v0

v1 whole, which is shorter than its diff:
```python
import jax
import jax.numpy as jnp
from jax import lax
from jax.experimental import pallas as pl
from jax.experimental.pallas import tpu as pltpu
from jax.sharding import PartitionSpec as P

BLOCK = 128
CORES = 2
BF16 = jnp.bfloat16
F32 = jnp.float32
MIB = 1 << 20
PARTIALS_MIB = 24
PRODUCTS_MIB = 24
HBM = pl.BlockSpec(memory_space=pltpu.HBM)
VMEM = pl.BlockSpec(memory_space=pltpu.VMEM)


def tile_of(units):
    return 256 if units % 256 == 0 else units


def keep_rows(weight, mask):
    mask = mask.astype(weight.dtype)
    parts = [
        weight[k * BLOCK : (k + 1) * BLOCK] * mask[k : k + 1] for k in range(mask.shape[0])
    ]
    return jnp.concatenate(parts, axis=0)


def keep_columns(weight, mask):
    parts = []
    for k in range(mask.shape[1]):
        wide = jnp.broadcast_to(mask[:, k : k + 1], (mask.shape[0], BLOCK))
        parts.append(weight[:, k * BLOCK : (k + 1) * BLOCK] * wide.astype(weight.dtype))
    return jnp.concatenate(parts, axis=1)


def dot_nn(left, right):
    return jnp.dot(left, right, preferred_element_type=F32)


def dot_nt(left, right):
    return lax.dot_general(
        left, right, (((1,), (1,)), ((), ())), preferred_element_type=F32
    )


def dot_tn(left, right):
    return lax.dot_general(
        left, right, (((0,), (0,)), ((), ())), preferred_element_type=F32
    )


def cost(flops, *arrays):
    return pl.CostEstimate(
        flops=flops,
        bytes_accessed=sum(a.size * a.dtype.itemsize for a in arrays),
        transcendentals=0,
    )


def params(mib):
    return pltpu.CompilerParams(vmem_limit_bytes=mib * MIB)


def tiles(units):
    tile = tile_of(units)
    return tile, units // tile, lambda j: pl.ds(pl.multiple_of(j * tile, tile), tile)


def for_steps(steps, body):
    if steps == 1:
        body(0)
    else:
        lax.fori_loop(0, steps, lambda j, c: (body(j), c)[1], 0)


def prepare(where, tokens, out_grad, gate_mask, up_mask, down_mask, units):
    rows, feats = tokens.shape
    half = rows // 2
    blocks = feats // BLOCK
    sources = (gate_mask, up_mask, down_mask, tokens, out_grad)

    def body(where_ref, *refs):
        srcs, (pair, kg, ku, kd), bufs, sems = refs[:5], refs[5:9], refs[9:14], refs[14]
        copies = [
            pltpu.make_async_copy(src, buf, sems.at[k])
            for k, (src, buf) in enumerate(zip(srcs, bufs))
        ]
        for copy in copies:
            copy.start()
        col, row, core = where_ref[0], where_ref[1], where_ref[2]
        count = gate_mask.shape[1]
        block = lax.div(
            row * units + lax.broadcasted_iota(jnp.int32, (count, units), 1), BLOCK
        )
        pick = (lax.broadcasted_iota(jnp.int32, (count, units), 0) == block).astype(F32)
        pick = pick.astype(BF16)
        shape = (blocks, gate_mask.shape[0])
        feature = col * blocks + lax.broadcasted_iota(jnp.int32, shape, 0)
        mine = (lax.broadcasted_iota(jnp.int32, shape, 1) == feature).astype(F32).astype(BF16)
        for k, out in enumerate((kg, ku, kd)):
            copies[k].wait()
            mask = dot_nn(mine, bufs[k][...].astype(F32).astype(BF16))
            if k < 2:
                out[...] = dot_nn(mask.astype(BF16), pick)
            else:
                out[...] = dot_tn(pick, mask.T.astype(BF16))
        for k in range(2):
            copies[3 + k].wait()
            low, high = bufs[3 + k][pl.ds(0, half), :], bufs[3 + k][pl.ds(half, half), :]
            pair[k, pl.ds(0, half), :] = jnp.where(core == 1, high, low)
            pair[k, pl.ds(half, half), :] = jnp.where(core == 1, low, high)

    return pl.pallas_call(
        body,
        in_specs=[pl.BlockSpec(memory_space=pltpu.SMEM)] + [HBM] * 5,
        out_specs=[VMEM] * 4,
        out_shape=[
            jax.ShapeDtypeStruct((2, rows, feats), BF16),
            jax.ShapeDtypeStruct((blocks, units), F32),
            jax.ShapeDtypeStruct((blocks, units), F32),
            jax.ShapeDtypeStruct((units, blocks), F32),
        ],
        scratch_shapes=[pltpu.VMEM(a.shape, a.dtype) for a in sources]
        + [pltpu.SemaphoreType.DMA((5,))],
        cost_estimate=pl.CostEstimate(flops=0, bytes_accessed=4 * MIB, transcendentals=0),
        compiler_params=params(16),
        name="prepare",
    )(where, *sources)


def partials(shards, weights, keeps=None):
    n = len(shards)
    m = 3 if keeps else 0
    _, rows, feats = shards[0].shape
    half = rows // 2
    own = n * half
    units = weights[0].shape[1]
    _, steps, at = tiles(units)

    def body(*refs):
        pairs = refs[:n]
        w_refs = refs[n : n + 3]
        masks = refs[n + 3 : n + 3 + m]
        keep_ref, send_ref = refs[n + 3 + m : n + 5 + m]
        bufs = refs[n + 5 + m : n + 5 + 2 * m] if keeps else w_refs
        lhs = refs[n + 5 + 2 * m]

        def copies(j):
            part = at(j)
            spots = [(slice(None), part), (slice(None), part), (part, slice(None))]
            return [
                pltpu.make_async_copy(src.at[spot], dst.at[spot], refs[-1].at[k, j])
                for k, (src, dst, spot) in enumerate(zip(w_refs, bufs, spots))
            ]

        def start(j):
            for copy in copies(j):
                copy.start()

        if keeps:
            for_steps(steps, start)
        for k in range(2):
            for i, pair in enumerate(pairs):
                lhs[k, pl.ds(i * half, half), :] = pair[k, pl.ds(0, half), :]
                lhs[k, pl.ds(own + i * half, half), :] = pair[k, pl.ds(half, half), :]

        def step(j):
            part = at(j)
            gate, up, down = (
                (lambda k=k: bufs[k][:, part] if k < 2 else bufs[k][part, :]) for k in range(3)
            )
            if keeps:
                for copy in copies(j):
                    copy.wait()
                bufs[0][:, part] = keep_rows(gate(), masks[0][:, part])
                bufs[1][:, part] = keep_rows(up(), masks[1][:, part])
                bufs[2][part, :] = keep_columns(down(), masks[2][part, :])
            outs = (dot_nn(lhs[0], gate()), dot_nn(lhs[0], up()), dot_nt(lhs[1], down()))
            for k, out in enumerate(outs):
                keep_ref[k, :, part] = out[:own]
                send_ref[k, :, part] = out[own:]

        for_steps(steps, step)

    out_shape = [jax.ShapeDtypeStruct((3, own, units), F32)] * 2
    if keeps:
        out_shape += [jax.ShapeDtypeStruct(w.shape, w.dtype) for w in weights]
    scratch = [pltpu.VMEM((2, 2 * own, feats), BF16)]
    if keeps:
        scratch.append(pltpu.SemaphoreType.DMA((3, steps)))
    return pl.pallas_call(
        body,
        in_specs=[VMEM] * n + [HBM if keeps else VMEM] * 3 + [VMEM] * m,
        out_specs=[VMEM] * (2 + m),
        out_shape=out_shape,
        scratch_shapes=scratch,
        cost_estimate=cost(12 * own * feats * units, *shards, *weights, *out_shape),
        compiler_params=params(PARTIALS_MIB),
        name="partials",
    )(*shards, *weights, *(keeps or ()))


def activate(keep, near, far):
    def body(*refs):
        keep_ref, near_ref = refs[:2]
        far_refs, out_ref = refs[2:-1], refs[-1]

        def total(k):
            value = keep_ref[k] + near_ref[k]
            for ref in far_refs:
                value = value + ref[k].astype(F32)
            return value

        gate, up, hidden_grad = total(0), total(1), total(2)
        sig = jax.nn.sigmoid(gate)
        act = gate * sig
        out_ref[0] = (act * up).astype(BF16)
        out_ref[1] = (hidden_grad * up * sig * (1.0 + gate * (1.0 - sig))).astype(BF16)
        out_ref[2] = (hidden_grad * act).astype(BF16)

    n = 3 + len(far)
    return pl.pallas_call(
        body,
        in_specs=[VMEM] * (n - 1),
        out_specs=VMEM,
        out_shape=jax.ShapeDtypeStruct(keep.shape, BF16),
        cost_estimate=cost(20 * keep.size, keep, near, *far),
        compiler_params=params(16),
        name="activate",
    )(keep, near, *far)


def products(parts, counts, slots, sizes, weights):
    pieces = [a for pair in parts for a in pair]
    n = len(pieces)
    units = pieces[0].shape[2]
    feats = weights[0].shape[0]
    half = pieces[0].shape[1] // counts[0]
    tokens = sum(p.shape[1] for p in pieces)
    _, steps, at = tiles(feats)
    outs_n = len(sizes)

    def body(*refs):
        piece_refs = refs[:n]
        gate_ref, up_ref, down_ref = refs[n : n + 3]
        outs, lhs = refs[n + 3 : n + 3 + outs_n], refs[n + 3 + outs_n]
        row = 0
        for piece in piece_refs:
            lhs[:, pl.ds(row, piece.shape[1]), :] = piece[...]
            row += piece.shape[1]

        def step(j):
            part = at(j)
            sums = (
                dot_nn(lhs[0], down_ref[:, part]),
                dot_nt(lhs[1], gate_ref[part, :]) + dot_nt(lhs[2], up_ref[part, :]),
            )
            row, shard = 0, 0
            for count in counts:
                for side in range(2):
                    for i in range(count):
                        out, place = slots[shard + i]
                        for k in range(2):
                            outs[out][place, k, pl.ds(side * half, half), part] = sums[k][
                                row : row + half
                            ].astype(outs[out].dtype)
                        row += half
                shard += count

        for_steps(steps, step)

    out_shape = [
        jax.ShapeDtypeStruct((size, 2, 2 * half, feats), BF16 if k else F32)
        for k, size in enumerate(sizes)
    ]
    return pl.pallas_call(
        body,
        in_specs=[VMEM] * (n + 3),
        out_specs=[VMEM] * outs_n,
        out_shape=out_shape,
        scratch_shapes=[pltpu.VMEM((3, tokens, units), BF16)],
        cost_estimate=cost(6 * tokens * feats * units, *pieces, *weights, *out_shape),
        compiler_params=params(PRODUCTS_MIB),
        name="products",
    )(*pieces, *weights)


def weight_grads(groups, parts, keeps):
    flat = [s for g in groups for s in g]
    pieces = [a for pair in parts for a in pair]
    n, m = len(flat), len(pieces)
    _, rows, feats = flat[0].shape
    half = rows // 2
    units = pieces[0].shape[2]
    tokens = n * rows
    tile, steps, at = tiles(units)

    def body(*refs):
        shards = list(refs[:n])
        piece_refs = refs[n : n + m]
        kg, ku, kd = refs[n + m : n + m + 3]
        grads = refs[n + m + 3 : n + m + 6]
        lhs, turned, rhs, gate_buf, up_buf, down_buf, sems = refs[n + m + 6 :]
        row, shard = 0, 0
        for group in groups:
            for side in range(2):
                for i in range(len(group)):
                    pair = shards[shard + i]
                    lhs[pl.ds(row, half), :] = pair[0, pl.ds(side * half, half), :]
                    rhs[pl.ds(row, half), :] = pair[1, pl.ds(side * half, half), :]
                    row += half
            shard += len(group)
        turned[...] = lhs[...].T

        def copies(j):
            part = at(j)
            return [
                pltpu.make_async_copy(src.at[j], dst, sems.at[k, j])
                for k, (src, dst) in enumerate(
                    (
                        (gate_buf, grads[0].at[:, part]),
                        (up_buf, grads[1].at[:, part]),
                        (down_buf, grads[2].at[part, :]),
                    )
                )
            ]

        def step(j):
            part = at(j)
            pre = [
                jnp.concatenate([p[k, :, part] for p in piece_refs], axis=0) for k in range(3)
            ]
            for buf, right, mask in ((gate_buf, pre[1], kg), (up_buf, pre[2], ku)):
                buf[j] = keep_rows(dot_nn(turned[...], right), mask[:, part])
            down_buf[j] = keep_columns(dot_tn(pre[0], rhs[...]), kd[part, :])
            for copy in copies(j):
                copy.start()

        def finish(j):
            for copy in copies(j):
                copy.wait()

        for_steps(steps, step)
        for_steps(steps, finish)

    out_shape = [
        jax.ShapeDtypeStruct((feats, units), F32),
        jax.ShapeDtypeStruct((feats, units), F32),
        jax.ShapeDtypeStruct((units, feats), F32),
    ]
    return pl.pallas_call(
        body,
        in_specs=[VMEM] * (n + m + 3),
        out_specs=[HBM] * 3,
        out_shape=out_shape,
        scratch_shapes=[
            pltpu.VMEM((tokens, feats), BF16),
            pltpu.VMEM((feats, tokens), BF16),
            pltpu.VMEM((tokens, feats), BF16),
            pltpu.VMEM((steps, feats, tile), F32),
            pltpu.VMEM((steps, feats, tile), F32),
            pltpu.VMEM((steps, tile, feats), F32),
            pltpu.SemaphoreType.DMA((3, steps)),
        ],
        cost_estimate=cost(6 * tokens * feats * units, *flat, *pieces, *out_shape),
        compiler_params=params(48),
        name="weight_grads",
    )(*flat, *pieces, *keeps)


def per_device(
    rows_n,
    cols_n,
    tokens,
    gate_weight,
    up_weight,
    down_weight,
    gate_mask,
    up_mask,
    down_mask,
    out_grad,
):
    cores = CORES if cols_n % CORES == 0 else 1
    ys = cols_n // cores
    xs = 1
    while (2 * xs) ** 2 <= rows_n and rows_n % (2 * xs) == 0:
        xs *= 2
    zs = rows_n // xs
    units = gate_weight.shape[1]
    row_index = lax.axis_index("row")
    col_index = lax.axis_index("col")
    core = col_index % cores
    half = tokens.shape[0] // 2

    def shift_z(value, by):
        pairs = [(i, ((i // xs + by) % zs) * xs + i % xs) for i in range(rows_n)]
        return lax.ppermute(value, "row", pairs)

    def shift_x(value, by):
        pairs = [(i, i // xs * xs + (i % xs + by) % xs) for i in range(rows_n)]
        return lax.ppermute(value, "row", pairs)

    def shift_y(value, by):
        pairs = [(i, (i // cores + by) % ys * cores + i % cores) for i in range(cols_n)]
        return lax.ppermute(value, "col", pairs)

    def swap_core(value):
        pairs = [(i, i // cores * cores + (i % cores + 1) % cores) for i in range(cols_n)]
        return lax.ppermute(value, "col", pairs)

    pair, *keeps = prepare(
        jnp.stack([col_index, row_index, core]),
        tokens,
        out_grad,
        gate_mask,
        up_mask,
        down_mask.T,
        units,
    )

    far_z = [d for k in range(1, zs // 2 + 1) for d in dict.fromkeys((k, zs - k))]
    held = {(0, 0): pair}
    for dz in far_z:
        held[dz, 0] = shift_z(pair, dz)
    for dx in range(1, xs):
        held[0, dx] = shift_x(pair, dx)
    for dz in far_z:
        for dx in range(1, xs):
            held[dz, dx] = shift_x(held[dz, 0], dx)

    z_groups = [far_z[k : k + 2] for k in range(0, len(far_z), 2)]
    chunks, groups = [[(0, 0)]], []
    for k, group in enumerate(z_groups):
        at = len(chunks)
        if k == 0:
            chunks.append([(dz, 0) for dz in group])
            chunks.append([(dz, dx) for dz in group for dx in range(1, xs)])
        else:
            chunks.append([(dz, dx) for dx in range(xs) for dz in group])
        groups.append([c for c in range(at, len(chunks)) if chunks[c]])
    chunks.append([(0, dx) for dx in range(1, xs)])
    groups.append([c for c in (0, len(chunks) - 1) if chunks[c]])

    parts = {}
    weights = (gate_weight, up_weight, down_weight)
    for k, chunk in enumerate(chunks):
        if not chunk:
            continue
        keep, send, *kept = partials([held[s] for s in chunk], weights, keeps if k == 0 else None)
        weights = kept or weights
        near = swap_core(send)
        out = (keep + near).astype(BF16)
        far = [shift_y(out, by) for by in range(1, ys)]
        own = activate(keep, near, far)
        parts[k] = (own, swap_core(own))

    total = None
    for group in groups:
        shards = [s for c in group for s in chunks[c]]
        dzs = list(dict.fromkeys(s[0] for s in shards))
        outs = products(
            [parts[c] for c in group],
            [len(chunks[c]) for c in group],
            [(dx, dzs.index(dz)) for dz, dx in shards],
            [len(dzs)] * xs,
            weights,
        )
        sums = outs[0]
        for dx in range(1, xs):
            sums = sums + shift_x(outs[dx], -dx)
        for k, dz in enumerate(dzs):
            value = sums[k]
            if dz:
                value = shift_z(value.astype(BF16), -dz)
            total = value.astype(F32) if total is None else total + value
    order = [k for k in range(len(chunks)) if chunks[k]]
    grads = weight_grads(
        [[held[s] for s in chunks[k]] for k in order], [parts[k] for k in order], keeps
    )
    total = total.astype(BF16)
    total = jnp.where(core == 1, jnp.roll(total, half, axis=1), total)
    return (total[0], total[1], *grads)


def solution(mesh):
    def whole(*args):
        return per_device(mesh.shape["row"], mesh.shape["col"], *args)

    return jax.shard_map(
        whole,
        mesh=mesh,
        in_specs=(
            P("row", "col"),
            P("col", "row"),
            P("col", "row"),
            P("row", "col"),
            P(),
            P(),
            P(),
            P("row", "col"),
        ),
        out_specs=(
            P("row", "col"),
            P("row", "col"),
            P("col", "row"),
            P("col", "row"),
            P("row", "col"),
        ),
        check_vma=False,
    )
```

time: 413 us -> 177 us (0.43)
  waiting for transfers between devices: 301 us -> 81.5 us
  matrix products: 74.7 us -> 0 us
  Pallas kernels: 0 us -> 45.8 us
  starting transfers between devices: 0.72 us -> 25.2 us
  other arithmetic: 21.4 us -> 2.24 us
  local copies, waits for them, and re-layouts: 0.49 us -> 17.9 us
  between operations: 14.2 us -> 1.27 us
    reduce_scatter x4 -> x0, waiting for transfers between devices: 199 us -> none  [the longest x1 69.3 us: per_device(): lax.psum_scatter(contract_last(block, kept_both), 'row', scatter_dimensio...]
    all_gather x4 -> x0, waiting for transfers between devices: 101 us -> none  [the longest x1 38 us: per_device(): grad_all = lax.all_gather(out_grad, 'row', axis=0, tiled=True)]
    ppermute x0 -> x28, waiting for transfers between devices: none -> 81.5 us  [the longest x5 46.8 us: shift_y(): return lax.ppermute(value, 'col', pairs)]
    dot_general x12 -> x0, matrix products: 74.7 us -> none  [the longest x3 18.6 us: expand_mask(): return jnp.dot(middle, right, precision=lax.Precision.HIGHEST)]
    pallas_call x0 -> x15, Pallas kernels: none -> 45.8 us  [the longest x5 18.4 us: partials(): pl.pallas_call(body, in_specs=[VMEM] * n + [HBM if keeps else VMEM] * 3 +...]
    ppermute x0 -> x28, starting transfers between devices: none -> 25.2 us  [the longest x6 9.7 us: shift_z(): return lax.ppermute(value, 'row', pairs)]
    unnamed x14 -> x80, local copies, waits for them, and re-layouts: 0.49 us -> 17.1 us
    mul x1 -> x0, other arithmetic: 14.1 us -> none  [per_device(): up_grad = keep_up * weight_both[:, unit_cols:]]
  transfers between devices with their start and end apart: 8 -> 28, of which waited for: 8 -> 14; matrix products, arithmetic and copies ran while one was open for 22% -> 1% of each run, Pallas kernels for 0% -> 25%
where the time goes in v1:
time: 177 us; the launch traced here: 174 us
  waiting for transfers between devices  81.5 us (46%)
  Pallas kernels  45.8 us (26%)
  starting transfers between devices  25.2 us (14%)
  local copies, waits for them, and re-layouts  17.9 us (10%)
  other arithmetic  2.24 us (1%)
    ppermute x5, waiting for transfers between devices, shift_y(): return lax.ppermute(value, 'col', pairs)  46.8 us
    ppermute x7, waiting for transfers between devices, shift_x(): return lax.ppermute(value, 'row', pairs)  23.1 us
    pallas_call x5, Pallas kernels, partials(): pl.pallas_call(body, in_specs=[VMEM] * n + [HBM if keeps else VMEM] * 3 +...  18.4 us
    unnamed x80, local copies, waits for them, and re-layouts  17.1 us
    pallas_call x3, Pallas kernels, products(): pl.pallas_call(body, in_specs=[VMEM] * (n + 3), out_specs=[VMEM] * outs_n...  13 us
    ppermute x6, waiting for transfers between devices, shift_z(): return lax.ppermute(value, 'row', pairs)  11.5 us
    pallas_call x1, Pallas kernels, weight_grads(): pl.pallas_call(body, in_specs=[VMEM] * (n + m + 3), out_specs=[HBM] * 3,...  10.8 us
    ppermute x6, starting transfers between devices, shift_z(): return lax.ppermute(value, 'row', pairs)  9.7 us
  transfers between devices with their start and end apart: 28, of which 14 were waited for; matrix products, arithmetic and copies ran while one was open for 1% of the time, Pallas kernels for 25%

profile of v1, /device:TPU:0, one launch (start us, length us, event | category | flops | bytes accessed | tf_op | source)
XLA Modules:
  0.0 173.8 jit_solution(10231200786848848656)
XLA Ops:
  0.6 0.1 pad_add_fusion.where_ref
  0.7 0.9 copy-done.35
  1.6 0.9 copy-done.36
  2.5 0.7 copy-done.37
  3.2 0.7 copy-done.38
  4.0 0.7 copy-done.39
  4.7 2.2 %prepare.1 = (bf16[2,64,1024]{2,1,0:T(8,128)(2,1)S(1)}, f32[8,1792]{1,0:T(8,128)S(1)}, f32[8,1792]{1,0:T(8,128)S(1)}, f32[1792,8]{1,0:T(8,128)S(1)}) custom-call(s32[3]{0:T(128)S(1)} %pad_add_fusion.where_ref, s32[32,112]{1,0:T(8,128)S(1)} %copy-done.37, s32[32,112]{1,0:T(8,128)S(1)} %copy-done.38, s32[32,112]{1,0:T(8,128)S(1)} %bitcast.18, ...), custom_call_target="tpu_custom_call" | custom-call | bytes 4194304 | tf_op jit(solution)/shard_map/prepare/pallas_call | solution.py:116
  6.9 5.1 %collective-permute-start.1 = (bf16[2,64,1024]{2,1,0:T(8,128)(2,1)S(1)}, bf16[2,64,1024]{2,1,0:T(8,128)(2,1)S(1)}, u32[]{:S(2)}, u32[]{:S(2)}) collective-permute-start(bf16[2,64,1024]{2,1,0:T(8,128)(2,1)S(1)} %get-tuple-element.31.refs_0_), channel_id=1, source_target_pairs={{0,24},{4,28},{8,0},{12,4},{16,8},{20,12},{24,16},{28,20},{1,25},{... | collective-permute-start | bytes 786440 | tf_op jit(solution)/shard_map/ppermute | solution.py:400
  12.1 1.0 collective-permute-start.13
  13.1 2.0 %copy-done.6 = bf16[1024,1792]{1,0:T(8,128)(2,1)S(1)} copy-done((bf16[1024,1792]{1,0:T(8,128)(2,1)S(1)}, bf16[1024,1792]{1,0:T(8,128)(2,1)}, u32[]{:S(2)}) %copy-start.6) | copy-done | bytes 3670040
  15.1 2.0 %copy-done.7 = bf16[1024,1792]{1,0:T(8,128)(2,1)S(1)} copy-done((bf16[1024,1792]{1,0:T(8,128)(2,1)S(1)}, bf16[1024,1792]{1,0:T(8,128)(2,1)}, u32[]{:S(2)}) %copy-start.7) | copy-done | bytes 3670040
  17.2 2.0 %copy-done.8 = bf16[1792,1024]{1,0:T(8,128)(2,1)S(1)} copy-done((bf16[1792,1024]{1,0:T(8,128)(2,1)S(1)}, bf16[1792,1024]{1,0:T(8,128)(2,1)}, u32[]{:S(2)}) %copy-start.8) | copy-done | bytes 3670040
  19.2 4.8 %partials.5 = (f32[3,32,1792]{2,1,0:T(8,128)S(1)}, f32[3,32,1792]{2,1,0:T(8,128)S(1)}, bf16[1024,1792]{1,0:T(8,128)(2,1)S(1)}, bf16[1024,1792]{1,0:T(8,128)(2,1)S(1)}, bf16[1792,1024]{1,0:T(8,128)(2,1)S(1)}) custom-call(bf16[2,64,1024]{2,1,0:T(8,128)(2,1)S(1)} %get-tuple-element.31.refs_0_, bf16[1024,1792]{1,0:T(8,128)(2,1)S(1)} %copy-done.6, ...), custom_call_target="tpu_custom_call" | custom-call | flops 704643072 | bytes 23658496 | tf_op jit(solution)/shard_map/partials/pallas_call | solution.py:194
  24.1 1.3 collective-permute-done.refs_0_.refs_1_
  25.4 3.4 %partials.6 = (f32[3,64,1792]{2,1,0:T(8,128)S(1)}, f32[3,64,1792]{2,1,0:T(8,128)S(1)}) custom-call(bf16[2,64,1024]{2,1,0:T(8,128)(2,1)S(1)} %collective-permute-done.refs_0_.refs_1_, bf16[2,64,1024]{2,1,0:T(8,128)(2,1)S(1)} %collective-permute-done.1.refs_1_.refs_2_, bf16[1024,1792]{1,0:T(8,128)(2,1)S(1)} %get-tuple-element.35.refs_2_.refs_4_.refs_1_, ...), custom_call_target="tpu_custom_call" | custom-call | flops 1409286144 | bytes 14286848 | tf_op jit(solution)/shard_map/partials/pallas_call | solution.py:194
  28.9 5.5 %collective-permute-done.13.refs_0_.refs_5_ = bf16[2,64,1024]{2,1,0:T(8,128)(2,1)S(1)} collective-permute-done((bf16[2,64,1024]{2,1,0:T(8,128)(2,1)S(1)}, bf16[2,64,1024]{2,1,0:T(8,128)(2,1)S(1)}, u32[]{:S(2)}, u32[]{:S(2)}) %collective-permute-start.13) | collective-permute-done | bytes 262176 | tf_op jit(solution)/shard_map/ppermute | solution.py:400
  34.4 1.5 collective-permute-start.14
  35.9 5.7 %collective-permute-done.14.refs_1_.refs_6_ = bf16[2,64,1024]{2,1,0:T(8,128)(2,1)S(1)} collective-permute-done((bf16[2,64,1024]{2,1,0:T(8,128)(2,1)S(1)}, bf16[2,64,1024]{2,1,0:T(8,128)(2,1)S(1)}, u32[]{:S(2)}, u32[]{:S(2)}) %collective-permute-start.14) | collective-permute-done | bytes 262176 | tf_op jit(solution)/shard_map/ppermute | solution.py:404
  41.6 3.4 %partials.8 = (f32[3,64,1792]{2,1,0:T(8,128)S(1)}, f32[3,64,1792]{2,1,0:T(8,128)S(1)}) custom-call(bf16[2,64,1024]{2,1,0:T(8,128)(2,1)S(1)} %collective-permute-done.13.refs_0_.refs_5_, bf16[2,64,1024]{2,1,0:T(8,128)(2,1)S(1)} %collective-permute-done.14.refs_1_.refs_6_, bf16[1024,1792]{1,0:T(8,128)(2,1)S(1)} %get-tuple-element.35.refs_2_.refs_4_.refs_1_, ...), custom_call_target="tpu_custom_call" | custom-call | flops 1409286144 | bytes 14286848 | tf_op jit(solution)/shard_map/partials/pallas_call | solution.py:194
  45.1 1.5 collective-permute-start.6
  46.6 0.5 collective-permute-start.5
  47.2 7.1 %collective-permute-done.6.refs_1_.refs_4_ = bf16[2,64,1024]{2,1,0:T(8,128)(2,1)S(1)} collective-permute-done((bf16[2,64,1024]{2,1,0:T(8,128)(2,1)S(1)}, bf16[2,64,1024]{2,1,0:T(8,128)(2,1)S(1)}, u32[]{:S(2)}, u32[]{:S(2)}) %collective-permute-start.6) | collective-permute-done | bytes 262176 | tf_op jit(solution)/shard_map/ppermute | solution.py:404
  54.3 5.1 %collective-permute-done.5.refs_0_.refs_3_ = bf16[2,64,1024]{2,1,0:T(8,128)(2,1)S(1)} collective-permute-done((bf16[2,64,1024]{2,1,0:T(8,128)(2,1)S(1)}, bf16[2,64,1024]{2,1,0:T(8,128)(2,1)S(1)}, u32[]{:S(2)}, u32[]{:S(2)}) %collective-permute-start.5) | collective-permute-done | bytes 262176 | tf_op jit(solution)/shard_map/ppermute | solution.py:404
  59.4 3.4 %partials.7 = (f32[3,64,1792]{2,1,0:T(8,128)S(1)}, f32[3,64,1792]{2,1,0:T(8,128)S(1)}) custom-call(bf16[2,64,1024]{2,1,0:T(8,128)(2,1)S(1)} %collective-permute-done.5.refs_0_.refs_3_, bf16[2,64,1024]{2,1,0:T(8,128)(2,1)S(1)} %collective-permute-done.6.refs_1_.refs_4_, bf16[1024,1792]{1,0:T(8,128)(2,1)S(1)} %get-tuple-element.35.refs_2_.refs_4_.refs_1_, ...), custom_call_target="tpu_custom_call" | custom-call | flops 1409286144 | bytes 14286848 | tf_op jit(solution)/shard_map/partials/pallas_call | solution.py:194
  62.9 1.5 collective-permute-start.23
  64.5 0.1 collective-permute-start.20
  64.6 0.1 add_convert_fusion.2
  64.8 1.6 collective-permute-start.3
  66.4 0.1 add_convert_fusion
  66.5 0.6 collective-permute-start.16
  67.1 0.1 add_convert_fusion.1
  67.2 1.6 collective-permute-start.8
  68.8 2.9 %collective-permute-done.23.refs_0_.refs_7_ = bf16[2,64,1024]{2,1,0:T(8,128)(2,1)S(1)} collective-permute-done((bf16[2,64,1024]{2,1,0:T(8,128)(2,1)S(1)}, bf16[2,64,1024]{2,1,0:T(8,128)(2,1)S(1)}, u32[]{:S(2)}, u32[]{:S(2)}) %collective-permute-start.23) | collective-permute-done | bytes 262176 | tf_op jit(solution)/shard_map/ppermute | solution.py:404
  71.6 3.3 %partials.9 = (f32[3,32,1792]{2,1,0:T(8,128)S(1)}, f32[3,32,1792]{2,1,0:T(8,128)S(1)}) custom-call(bf16[2,64,1024]{2,1,0:T(8,128)(2,1)S(1)} %collective-permute-done.23.refs_0_.refs_7_, bf16[1024,1792]{1,0:T(8,128)(2,1)S(1)} %get-tuple-element.35.refs_2_.refs_4_.refs_1_, bf16[1024,1792]{1,0:T(8,128)(2,1)S(1)} %get-tuple-element.36.refs_3_.refs_5_.refs_2_, ...), custom_call_target="tpu_custom_call" | custom-call | flops 704643072 | bytes 12648448 | tf_op jit(solution)/shard_map/partials/pallas_call | solution.py:194
  75.1 1.6 collective-permute-start.21
  76.7 6.4 %collective-permute-done.3.refs_2_ = bf16[3,64,1792]{2,1,0:T(8,128)(2,1)S(1)} collective-permute-done((bf16[3,64,1792]{2,1,0:T(8,128)(2,1)S(1)}, bf16[3,64,1792]{2,1,0:T(8,128)(2,1)S(1)}, u32[]{:S(2)}, u32[]{:S(2)}) %collective-permute-start.3) | collective-permute-done | bytes 688160 | tf_op jit(solution)/shard_map/ppermute | solution.py:408
  83.1 0.4 activate.5.refs_0_.refs_10_
  83.6 14.3 %collective-permute-done.16.refs_2_ = bf16[3,64,1792]{2,1,0:T(8,128)(2,1)S(1)} collective-permute-done((bf16[3,64,1792]{2,1,0:T(8,128)(2,1)S(1)}, bf16[3,64,1792]{2,1,0:T(8,128)(2,1)S(1)}, u32[]{:S(2)}, u32[]{:S(2)}) %collective-permute-start.16) | collective-permute-done | bytes 688160 | tf_op jit(solution)/shard_map/ppermute | solution.py:408
  97.9 0.4 activate.7.refs_0_.refs_14_
  98.3 14.3 %collective-permute-done.8.refs_2_ = bf16[3,64,1792]{2,1,0:T(8,128)(2,1)S(1)} collective-permute-done((bf16[3,64,1792]{2,1,0:T(8,128)(2,1)S(1)}, bf16[3,64,1792]{2,1,0:T(8,128)(2,1)S(1)}, u32[]{:S(2)}, u32[]{:S(2)}) %collective-permute-start.8) | collective-permute-done | bytes 688160 | tf_op jit(solution)/shard_map/ppermute | solution.py:408
  112.6 0.4 activate.6.refs_2_.refs_12_
  113.2 1.6 collective-permute-start.25
  114.7 5.2 %collective-permute-done.21.refs_2_ = bf16[3,32,1792]{2,1,0:T(8,128)(2,1)S(1)} collective-permute-done((bf16[3,32,1792]{2,1,0:T(8,128)(2,1)S(1)}, bf16[3,32,1792]{2,1,0:T(8,128)(2,1)S(1)}, u32[]{:S(2)}, u32[]{:S(2)}) %collective-permute-start.21) | collective-permute-done | bytes 344096 | tf_op jit(solution)/shard_map/ppermute | solution.py:408
  120.0 0.2 activate.8.refs_0_.refs_8_
  120.3 6.5 %collective-permute-done.25.refs_2_ = bf16[3,32,1792]{2,1,0:T(8,128)(2,1)S(1)} collective-permute-done((bf16[3,32,1792]{2,1,0:T(8,128)(2,1)S(1)}, bf16[3,32,1792]{2,1,0:T(8,128)(2,1)S(1)}, u32[]{:S(2)}, u32[]{:S(2)}) %collective-permute-start.25) | collective-permute-done | bytes 344096 | tf_op jit(solution)/shard_map/ppermute | solution.py:408
  126.8 0.2 activate.9.refs_2_.refs_16_
  127.1 4.6 %products.3 = (f32[2,2,64,1024]{3,2,1,0:T(8,128)S(1)}, bf16[2,2,64,1024]{3,2,1,0:T(8,128)(2,1)}) custom-call(bf16[3,64,1792]{2,1,0:T(8,128)(2,1)S(1)} %activate.5.refs_0_.refs_10_, bf16[3,64,1792]{2,1,0:T(8,128)(2,1)S(1)} %collective-permute-done.4.refs_1_.refs_11_, bf16[3,64,1792]{2,1,0:T(8,128)(2,1)S(1)} %activate.6.refs_2_.refs_12_, ...), custom_call_target="tpu_custom_call" | custom-call | flops 2818572288 | bytes 15335424 | tf_op jit(solution)/shard_map/products/pallas_call | solution.py:279
  131.7 0.5 collective-permute-start.10
  132.3 4.0 %products.4 = (f32[1,2,64,1024]{3,2,1,0:T(8,128)S(1)}, bf16[1,2,64,1024]{3,2,1,0:T(8,128)(2,1)}) custom-call(bf16[3,64,1792]{2,1,0:T(8,128)(2,1)S(1)} %activate.7.refs_0_.refs_14_, bf16[3,64,1792]{2,1,0:T(8,128)(2,1)S(1)} %collective-permute-done.17.refs_1_.refs_15_, bf16[1024,1792]{1,0:T(8,128)(2,1)S(1)} %get-tuple-element.35.refs_2_.refs_4_.refs_1_, ...), custom_call_target="tpu_custom_call" | custom-call | flops 1409286144 | bytes 13172736 | tf_op jit(solution)/shard_map/products/pallas_call | solution.py:279
  136.3 0.8 copy-done.17
  137.0 1.5 collective-permute-start.18
  138.5 2.0 %copy-done.1 = bf16[1024,1792]{1,0:T(8,128)(2,1)S(1)} copy-done((bf16[1024,1792]{1,0:T(8,128)(2,1)S(1)}, bf16[1024,1792]{1,0:T(8,128)(2,1)}, u32[]{:S(2)}) %copy-start.1) | copy-done | bytes 3670040
  140.6 2.0 %copy-done.3 = bf16[1024,1792]{1,0:T(8,128)(2,1)S(1)} copy-done((bf16[1024,1792]{1,0:T(8,128)(2,1)S(1)}, bf16[1024,1792]{1,0:T(8,128)(2,1)}, u32[]{:S(2)}) %copy-start.3) | copy-done | bytes 3670040
  142.6 2.0 %copy-done.5 = bf16[1792,1024]{1,0:T(8,128)(2,1)S(1)} copy-done((bf16[1792,1024]{1,0:T(8,128)(2,1)S(1)}, bf16[1792,1024]{1,0:T(8,128)(2,1)}, u32[]{:S(2)}) %copy-start.5) | copy-done | bytes 3670040
  144.6 4.4 %products.5 = (f32[1,2,64,1024]{3,2,1,0:T(8,128)S(1)}, bf16[1,2,64,1024]{3,2,1,0:T(8,128)(2,1)S(1)}) custom-call(bf16[3,32,1792]{2,1,0:T(8,128)(2,1)S(1)} %activate.8.refs_0_.refs_8_, bf16[3,32,1792]{2,1,0:T(8,128)(2,1)} %collective-permute-done.22.refs_1_.refs_9_, bf16[3,32,1792]{2,1,0:T(8,128)(2,1)S(1)} %activate.9.refs_2_.refs_16_, ...), custom_call_target="tpu_custom_call" | custom-call | flops 1409286144 | bytes 13172736 | tf_op jit(solution)/shard_map/products/pallas_call | solution.py:279
  149.0 0.6 collective-permute-start.27
  149.7 2.4 %collective-permute-done.18 = bf16[1,2,64,1024]{3,2,1,0:T(8,128)(2,1)S(1)} collective-permute-done((bf16[1,2,64,1024]{3,2,1,0:T(8,128)(2,1)}, bf16[1,2,64,1024]{3,2,1,0:T(8,128)(2,1)S(1)}, u32[]{:S(2)}, u32[]{:S(2)}) %collective-permute-start.18) | collective-permute-done | bytes 262176 | tf_op jit(solution)/shard_map/ppermute | solution.py:404
  152.3 1.3 add_convert_fusion.3
  153.6 3.5 %collective-permute-start.11 = (bf16[2,64,1024]{2,1,0:T(8,128)(2,1)S(1)}, bf16[2,64,1024]{2,1,0:T(8,128)(2,1)S(1)}, u32[]{:S(2)}, u32[]{:S(2)}) collective-permute-start(bf16[2,64,1024]{2,1,0:T(8,128)(2,1)S(1)} %get-tuple-element.57), channel_id=1, source_target_pairs={{0,24},{4,28},{8,0},{12,4},{16,8},{20,12},{24,16},{28,20},{1,25},{... | collective-permute-start | bytes 786440 | tf_op jit(solution)/shard_map/ppermute | solution.py:400
  157.2 10.8 %weight_grads.1 = (f32[1024,1792]{1,0:T(8,128)}, f32[1024,1792]{1,0:T(8,128)}, f32[1792,1024]{1,0:T(8,128)}) custom-call(bf16[2,64,1024]{2,1,0:T(8,128)(2,1)S(1)} %copy-done.20, bf16[2,64,1024]{2,1,0:T(8,128)(2,1)S(1)} %copy-done.24, bf16[2,64,1024]{2,1,0:T(8,128)(2,1)S(1)} %copy-done.22, bf16[2,64,1024]{2,1,0:T(8,128)(2,1)S(1)} %copy-done.32, ...), custom_call_target="tpu_custom_call" | custom-call | flops 5637144576 | bytes 29622272 | tf_op jit(solution)/shard_map/weight_grads/pallas_call | solution.py:354
  168.0 0.4 collective-permute-done.19
  168.5 4.3 %collective-permute-done.11 = bf16[2,64,1024]{2,1,0:T(8,128)(2,1)S(1)} collective-permute-done((bf16[2,64,1024]{2,1,0:T(8,128)(2,1)S(1)}, bf16[2,64,1024]{2,1,0:T(8,128)(2,1)S(1)}, u32[]{:S(2)}, u32[]{:S(2)}) %collective-permute-start.11) | collective-permute-done | bytes 262176 | tf_op jit(solution)/shard_map/ppermute | solution.py:400
  172.8 0.2 fusion
  173.1 0.7 slice_bitcast_fusion.2
  (100 shorter events, 1.2 us)
Async XLA Ops:
  0.7 0.9 copy-start.35
  1.6 0.9 copy-start.36
  6.9 17.1 %copy-start.12 = (f32[1792,8]{1,0:T(8,128)}, f32[1792,8]{1,0:T(8,128)S(1)}, u32[]{:S(2)}) copy-start(f32[1792,8]{1,0:T(8,128)S(1)} %get-tuple-element.34.refs_6_.refs_20_) | copy-start | bytes 172036
  6.9 56.0 %copy-start.19 = (bf16[2,64,1024]{2,1,0:T(8,128)(2,1)}, bf16[2,64,1024]{2,1,0:T(8,128)(2,1)S(1)}, u32[]{:S(2)}) copy-start(bf16[2,64,1024]{2,1,0:T(8,128)(2,1)S(1)} %get-tuple-element.31.refs_0_) | copy-start | bytes 786436
  6.9 17.2 %collective-permute-start.1 = (bf16[2,64,1024]{2,1,0:T(8,128)(2,1)S(1)}, bf16[2,64,1024]{2,1,0:T(8,128)(2,1)S(1)}, u32[]{:S(2)}, u32[]{:S(2)}) collective-permute-start(bf16[2,64,1024]{2,1,0:T(8,128)(2,1)S(1)} %get-tuple-element.31.refs_0_), channel_id=1, source_target_pairs={{0,24},{4,28},{8,0},{12,4},{16,8},{20,12},{24,16},{28,20},{1,25},{... | collective-permute-start | bytes 786440 | tf_op jit(solution)/shard_map/ppermute | solution.py:400
  12.1 13.3 %collective-permute-start = (bf16[2,64,1024]{2,1,0:T(8,128)(2,1)S(1)}, bf16[2,64,1024]{2,1,0:T(8,128)(2,1)S(1)}, u32[]{:S(2)}, u32[]{:S(2)}) collective-permute-start(bf16[2,64,1024]{2,1,0:T(8,128)(2,1)S(1)} %get-tuple-element.31.refs_0_), channel_id=1, source_target_pairs={{0,8},{4,12},{8,16},{12,20},{16,24},{20,28},{24,0},{28,4},{1,9},{5... | collective-permute-start | bytes 786440 | tf_op jit(solution)/shard_map/ppermute | solution.py:400
  12.1 22.3 %collective-permute-start.13 = (bf16[2,64,1024]{2,1,0:T(8,128)(2,1)S(1)}, bf16[2,64,1024]{2,1,0:T(8,128)(2,1)S(1)}, u32[]{:S(2)}, u32[]{:S(2)}) collective-permute-start(bf16[2,64,1024]{2,1,0:T(8,128)(2,1)S(1)} %get-tuple-element.31.refs_0_), channel_id=1, source_target_pairs={{0,16},{4,20},{8,24},{12,28},{16,0},{20,4},{24,8},{28,12},{1,17},{... | collective-permute-start | bytes 786440 | tf_op jit(solution)/shard_map/ppermute | solution.py:400
  13.1 2.0 %copy-start.6 = (bf16[1024,1792]{1,0:T(8,128)(2,1)S(1)}, bf16[1024,1792]{1,0:T(8,128)(2,1)}, u32[]{:S(2)}) copy-start(bf16[1024,1792]{1,0:T(8,128)(2,1)} %refs_1_.3) | copy-start | bytes 11010052
  15.1 2.0 %copy-start.7 = (bf16[1024,1792]{1,0:T(8,128)(2,1)S(1)}, bf16[1024,1792]{1,0:T(8,128)(2,1)}, u32[]{:S(2)}) copy-start(bf16[1024,1792]{1,0:T(8,128)(2,1)} %refs_2_.1) | copy-start | bytes 11010052
  17.1 2.0 %copy-start.8 = (bf16[1792,1024]{1,0:T(8,128)(2,1)S(1)}, bf16[1792,1024]{1,0:T(8,128)(2,1)}, u32[]{:S(2)}) copy-start(bf16[1792,1024]{1,0:T(8,128)(2,1)} %refs_3_.3) | copy-start | bytes 11010052
  24.1 108.2 %copy-start = (bf16[1024,1792]{1,0:T(8,128)(2,1)}, bf16[1024,1792]{1,0:T(8,128)(2,1)S(1)}, u32[]{:S(2)}) copy-start(bf16[1024,1792]{1,0:T(8,128)(2,1)S(1)} %get-tuple-element.35.refs_2_.refs_4_.refs_1_) | copy-start | bytes 11010052
  24.1 108.2 %copy-start.2 = (bf16[1024,1792]{1,0:T(8,128)(2,1)}, bf16[1024,1792]{1,0:T(8,128)(2,1)S(1)}, u32[]{:S(2)}) copy-start(bf16[1024,1792]{1,0:T(8,128)(2,1)S(1)} %get-tuple-element.36.refs_3_.refs_5_.refs_2_) | copy-start | bytes 11010052
  24.1 108.2 %copy-start.4 = (bf16[1792,1024]{1,0:T(8,128)(2,1)}, bf16[1792,1024]{1,0:T(8,128)(2,1)S(1)}, u32[]{:S(2)}) copy-start(bf16[1792,1024]{1,0:T(8,128)(2,1)S(1)} %get-tuple-element.37.refs_4_.refs_6_.refs_3_) | copy-start | bytes 11010052
  24.1 21.0 %copy-start.21 = (bf16[2,64,1024]{2,1,0:T(8,128)(2,1)}, bf16[2,64,1024]{2,1,0:T(8,128)(2,1)S(1)}, u32[]{:S(2)}) copy-start(bf16[2,64,1024]{2,1,0:T(8,128)(2,1)S(1)} %collective-permute-done.1.refs_1_.refs_2_) | copy-start | bytes 786436
  25.4 21.3 %copy-start.23 = (bf16[2,64,1024]{2,1,0:T(8,128)(2,1)}, bf16[2,64,1024]{2,1,0:T(8,128)(2,1)S(1)}, u32[]{:S(2)}) copy-start(bf16[2,64,1024]{2,1,0:T(8,128)(2,1)S(1)} %collective-permute-done.refs_0_.refs_1_) | copy-start | bytes 786436
  28.8 35.8 %collective-permute-start.2 = (f32[3,64,1792]{2,1,0:T(8,128)S(1)}, f32[3,64,1792]{2,1,0:T(8,128)S(1)}, u32[]{:S(2)}, u32[]{:S(2)}) collective-permute-start(f32[3,64,1792]{2,1,0:T(8,128)S(1)} %get-tuple-element.39), channel_id=1, source_target_pairs={{0,1},{1,0},{2,3},{3,2},{4,5},{5,4},{6,7},{7,6},{8,9},{9,8},{10,11... | collective-permute-start | bytes 4128776 | tf_op jit(solution)/shard_map/ppermute | solution.py:412
  34.4 10.6 %copy-start.25 = (bf16[2,64,1024]{2,1,0:T(8,128)(2,1)}, bf16[2,64,1024]{2,1,0:T(8,128)(2,1)S(1)}, u32[]{:S(2)}) copy-start(bf16[2,64,1024]{2,1,0:T(8,128)(2,1)S(1)} %collective-permute-done.13.refs_0_.refs_5_) | copy-start | bytes 786436
  34.4 7.2 %collective-permute-start.14 = (bf16[2,64,1024]{2,1,0:T(8,128)(2,1)S(1)}, bf16[2,64,1024]{2,1,0:T(8,128)(2,1)S(1)}, u32[]{:S(2)}, u32[]{:S(2)}) collective-permute-start(bf16[2,64,1024]{2,1,0:T(8,128)(2,1)S(1)} %collective-permute-done.13.refs_0_.refs_5_), channel_id=1, source_target_pairs={{0,4},{4,0},{8,12},{12,8},{16,20},{20,16},{24,28},{28,24},{1,5},{5... | collective-permute-start | bytes 786440 | tf_op jit(solution)/shard_map/ppermute | solution.py:404
  41.6 3.4 %copy-start.27 = (bf16[2,64,1024]{2,1,0:T(8,128)(2,1)}, bf16[2,64,1024]{2,1,0:T(8,128)(2,1)S(1)}, u32[]{:S(2)}) copy-start(bf16[2,64,1024]{2,1,0:T(8,128)(2,1)S(1)} %collective-permute-done.14.refs_1_.refs_6_) | copy-start | bytes 786436
  45.0 21.4 %collective-permute-start.15 = (f32[3,64,1792]{2,1,0:T(8,128)S(1)}, f32[3,64,1792]{2,1,0:T(8,128)S(1)}, u32[]{:S(2)}, u32[]{:S(2)}) collective-permute-start(f32[3,64,1792]{2,1,0:T(8,128)S(1)} %get-tuple-element.45), channel_id=1, source_target_pairs={{0,1},{1,0},{2,3},{3,2},{4,5},{5,4},{6,7},{7,6},{8,9},{9,8},{10,11... | collective-permute-start | bytes 4128776 | tf_op jit(solution)/shard_map/ppermute | solution.py:412
  45.1 9.2 %collective-permute-start.6 = (bf16[2,64,1024]{2,1,0:T(8,128)(2,1)S(1)}, bf16[2,64,1024]{2,1,0:T(8,128)(2,1)S(1)}, u32[]{:S(2)}, u32[]{:S(2)}) collective-permute-start(bf16[2,64,1024]{2,1,0:T(8,128)(2,1)S(1)} %collective-permute-done.1.refs_1_.refs_2_), channel_id=1, source_target_pairs={{0,4},{4,0},{8,12},{12,8},{16,20},{20,16},{24,28},{28,24},{1,5},{5... | collective-permute-start | bytes 786440 | tf_op jit(solution)/shard_map/ppermute | solution.py:404
  46.6 12.8 %collective-permute-start.5 = (bf16[2,64,1024]{2,1,0:T(8,128)(2,1)S(1)}, bf16[2,64,1024]{2,1,0:T(8,128)(2,1)S(1)}, u32[]{:S(2)}, u32[]{:S(2)}) collective-permute-start(bf16[2,64,1024]{2,1,0:T(8,128)(2,1)S(1)} %collective-permute-done.refs_0_.refs_1_), channel_id=1, source_target_pairs={{0,4},{4,0},{8,12},{12,8},{16,20},{20,16},{24,28},{28,24},{1,5},{5... | collective-permute-start | bytes 786440 | tf_op jit(solution)/shard_map/ppermute | solution.py:404
  54.3 8.5 %copy-start.29 = (bf16[2,64,1024]{2,1,0:T(8,128)(2,1)}, bf16[2,64,1024]{2,1,0:T(8,128)(2,1)S(1)}, u32[]{:S(2)}) copy-start(bf16[2,64,1024]{2,1,0:T(8,128)(2,1)S(1)} %collective-permute-done.6.refs_1_.refs_4_) | copy-start | bytes 786436
  59.4 3.4 %copy-start.31 = (bf16[2,64,1024]{2,1,0:T(8,128)(2,1)}, bf16[2,64,1024]{2,1,0:T(8,128)(2,1)S(1)}, u32[]{:S(2)}) copy-start(bf16[2,64,1024]{2,1,0:T(8,128)(2,1)S(1)} %collective-permute-done.5.refs_0_.refs_3_) | copy-start | bytes 786436
  62.8 4.2 %collective-permute-start.7 = (f32[3,64,1792]{2,1,0:T(8,128)S(1)}, f32[3,64,1792]{2,1,0:T(8,128)S(1)}, u32[]{:S(2)}, u32[]{:S(2)}) collective-permute-start(f32[3,64,1792]{2,1,0:T(8,128)S(1)} %get-tuple-element.41), channel_id=1, source_target_pairs={{0,1},{1,0},{2,3},{3,2},{4,5},{5,4},{6,7},{7,6},{8,9},{9,8},{10,11... | collective-permute-start | bytes 4128776 | tf_op jit(solution)/shard_map/ppermute | solution.py:412
  62.9 8.7 %collective-permute-start.23 = (bf16[2,64,1024]{2,1,0:T(8,128)(2,1)S(1)}, bf16[2,64,1024]{2,1,0:T(8,128)(2,1)S(1)}, u32[]{:S(2)}, u32[]{:S(2)}) collective-permute-start(bf16[2,64,1024]{2,1,0:T(8,128)(2,1)S(1)} %get-tuple-element.31.refs_0_), channel_id=1, source_target_pairs={{0,4},{4,0},{8,12},{12,8},{16,20},{20,16},{24,28},{28,24},{1,5},{5... | collective-permute-start | bytes 786440 | tf_op jit(solution)/shard_map/ppermute | solution.py:404
  64.5 10.6 %collective-permute-start.20 = (f32[3,32,1792]{2,1,0:T(8,128)S(1)}, f32[3,32,1792]{2,1,0:T(8,128)S(1)}, u32[]{:S(2)}, u32[]{:S(2)}) collective-permute-start(f32[3,32,1792]{2,1,0:T(8,128)S(1)} %get-tuple-element.49), channel_id=1, source_target_pairs={{0,1},{1,0},{2,3},{3,2},{4,5},{5,4},{6,7},{7,6},{8,9},{9,8},{10,11... | collective-permute-start | bytes 2064392 | tf_op jit(solution)/shard_map/ppermute | solution.py:412
  64.8 18.4 %collective-permute-start.3 = (bf16[3,64,1792]{2,1,0:T(8,128)(2,1)S(1)}, bf16[3,64,1792]{2,1,0:T(8,128)(2,1)S(1)}, u32[]{:S(2)}, u32[]{:S(2)}) collective-permute-start(bf16[3,64,1792]{2,1,0:T(8,128)(2,1)S(1)} %add_convert_fusion.2), channel_id=1, source_target_pairs={{0,2},{1,3},{2,0},{3,1},{4,6},{5,7},{6,4},{7,5},{8,10},{9,11},{10,... | collective-permute-start | bytes 2064392 | tf_op jit(solution)/shard_map/ppermute | solution.py:408
  66.5 31.4 %collective-permute-start.16 = (bf16[3,64,1792]{2,1,0:T(8,128)(2,1)S(1)}, bf16[3,64,1792]{2,1,0:T(8,128)(2,1)S(1)}, u32[]{:S(2)}, u32[]{:S(2)}) collective-permute-start(bf16[3,64,1792]{2,1,0:T(8,128)(2,1)S(1)} %add_convert_fusion), channel_id=1, source_target_pairs={{0,2},{1,3},{2,0},{3,1},{4,6},{5,7},{6,4},{7,5},{8,10},{9,11},{10,... | collective-permute-start | bytes 2064392 | tf_op jit(solution)/shard_map/ppermute | solution.py:408
  67.2 45.4 %collective-permute-start.8 = (bf16[3,64,1792]{2,1,0:T(8,128)(2,1)S(1)}, bf16[3,64,1792]{2,1,0:T(8,128)(2,1)S(1)}, u32[]{:S(2)}, u32[]{:S(2)}) collective-permute-start(bf16[3,64,1792]{2,1,0:T(8,128)(2,1)S(1)} %add_convert_fusion.1), channel_id=1, source_target_pairs={{0,2},{1,3},{2,0},{3,1},{4,6},{5,7},{6,4},{7,5},{8,10},{9,11},{10,... | collective-permute-start | bytes 2064392 | tf_op jit(solution)/shard_map/ppermute | solution.py:408
  71.6 3.3 %copy-start.33 = (bf16[2,64,1024]{2,1,0:T(8,128)(2,1)}, bf16[2,64,1024]{2,1,0:T(8,128)(2,1)S(1)}, u32[]{:S(2)}) copy-start(bf16[2,64,1024]{2,1,0:T(8,128)(2,1)S(1)} %collective-permute-done.23.refs_0_.refs_7_) | copy-start | bytes 786436
  75.0 38.1 %collective-permute-start.24 = (f32[3,32,1792]{2,1,0:T(8,128)S(1)}, f32[3,32,1792]{2,1,0:T(8,128)S(1)}, u32[]{:S(2)}, u32[]{:S(2)}) collective-permute-start(f32[3,32,1792]{2,1,0:T(8,128)S(1)} %get-tuple-element.51), channel_id=1, source_target_pairs={{0,1},{1,0},{2,3},{3,2},{4,5},{5,4},{6,7},{7,6},{8,9},{9,8},{10,11... | collective-permute-start | bytes 2064392 | tf_op jit(solution)/shard_map/ppermute | solution.py:412
  75.1 44.9 %collective-permute-start.21 = (bf16[3,32,1792]{2,1,0:T(8,128)(2,1)S(1)}, bf16[3,32,1792]{2,1,0:T(8,128)(2,1)S(1)}, u32[]{:S(2)}, u32[]{:S(2)}) collective-permute-start(bf16[3,32,1792]{2,1,0:T(8,128)(2,1)S(1)} %add_convert_fusion.5), channel_id=1, source_target_pairs={{0,2},{1,3},{2,0},{3,1},{4,6},{5,7},{6,4},{7,5},{8,10},{9,11},{10,... | collective-permute-start | bytes 1032200 | tf_op jit(solution)/shard_map/ppermute | solution.py:408
  83.5 43.5 %collective-permute-start.4 = (bf16[3,64,1792]{2,1,0:T(8,128)(2,1)S(1)}, bf16[3,64,1792]{2,1,0:T(8,128)(2,1)S(1)}, u32[]{:S(2)}, u32[]{:S(2)}) collective-permute-start(bf16[3,64,1792]{2,1,0:T(8,128)(2,1)S(1)} %activate.5.refs_0_.refs_10_), channel_id=1, source_target_pairs={{0,1},{1,0},{2,3},{3,2},{4,5},{5,4},{6,7},{7,6},{8,9},{9,8},{10,11... | collective-permute-start | bytes 2064392 | tf_op jit(solution)/shard_map/ppermute | solution.py:412
  98.2 34.0 %copy-start.9 = (bf16[3,64,1792]{2,1,0:T(8,128)(2,1)}, bf16[3,64,1792]{2,1,0:T(8,128)(2,1)S(1)}, u32[]{:S(2)}) copy-start(bf16[3,64,1792]{2,1,0:T(8,128)(2,1)S(1)} %activate.7.refs_0_.refs_14_) | copy-start | bytes 2064388
  98.3 34.0 %collective-permute-start.17 = (bf16[3,64,1792]{2,1,0:T(8,128)(2,1)S(1)}, bf16[3,64,1792]{2,1,0:T(8,128)(2,1)S(1)}, u32[]{:S(2)}, u32[]{:S(2)}) collective-permute-start(bf16[3,64,1792]{2,1,0:T(8,128)(2,1)S(1)} %activate.7.refs_0_.refs_14_), channel_id=1, source_target_pairs={{0,1},{1,0},{2,3},{3,2},{4,5},{5,4},{6,7},{7,6},{8,9},{9,8},{10,11... | collective-permute-start | bytes 2064392 | tf_op jit(solution)/shard_map/ppermute | solution.py:412
  113.0 14.1 %collective-permute-start.9 = (bf16[3,64,1792]{2,1,0:T(8,128)(2,1)S(1)}, bf16[3,64,1792]{2,1,0:T(8,128)(2,1)S(1)}, u32[]{:S(2)}, u32[]{:S(2)}) collective-permute-start(bf16[3,64,1792]{2,1,0:T(8,128)(2,1)S(1)} %activate.6.refs_2_.refs_12_), channel_id=1, source_target_pairs={{0,1},{1,0},{2,3},{3,2},{4,5},{5,4},{6,7},{7,6},{8,9},{9,8},{10,11... | collective-permute-start | bytes 2064392 | tf_op jit(solution)/shard_map/ppermute | solution.py:412
  113.2 13.6 %collective-permute-start.25 = (bf16[3,32,1792]{2,1,0:T(8,128)(2,1)S(1)}, bf16[3,32,1792]{2,1,0:T(8,128)(2,1)S(1)}, u32[]{:S(2)}, u32[]{:S(2)}) collective-permute-start(bf16[3,32,1792]{2,1,0:T(8,128)(2,1)S(1)} %add_convert_fusion.4), channel_id=1, source_target_pairs={{0,2},{1,3},{2,0},{3,1},{4,6},{5,7},{6,4},{7,5},{8,10},{9,11},{10,... | collective-permute-start | bytes 1032200 | tf_op jit(solution)/shard_map/ppermute | solution.py:408
  120.2 18.3 %collective-permute-start.22 = (bf16[3,32,1792]{2,1,0:T(8,128)(2,1)S(1)}, bf16[3,32,1792]{2,1,0:T(8,128)(2,1)}, u32[]{:S(2)}, u32[]{:S(2)}) collective-permute-start(bf16[3,32,1792]{2,1,0:T(8,128)(2,1)S(1)} %activate.8.refs_0_.refs_8_), channel_id=1, source_target_pairs={{0,1},{1,0},{2,3},{3,2},{4,5},{5,4},{6,7},{7,6},{8,9},{9,8},{10,11... | collective-permute-start | bytes 1032200 | tf_op jit(solution)/shard_map/ppermute | solution.py:412
  127.0 11.6 %collective-permute-start.26 = (bf16[3,32,1792]{2,1,0:T(8,128)(2,1)S(1)}, bf16[3,32,1792]{2,1,0:T(8,128)(2,1)}, u32[]{:S(2)}, u32[]{:S(2)}) collective-permute-start(bf16[3,32,1792]{2,1,0:T(8,128)(2,1)S(1)} %activate.9.refs_2_.refs_16_), channel_id=1, source_target_pairs={{0,1},{1,0},{2,3},{3,2},{4,5},{5,4},{6,7},{7,6},{8,9},{9,8},{10,11... | collective-permute-start | bytes 1032200 | tf_op jit(solution)/shard_map/ppermute | solution.py:412
  127.0 4.6 %copy-start.14 = (bf16[3,64,1792]{2,1,0:T(8,128)(2,1)}, bf16[3,64,1792]{2,1,0:T(8,128)(2,1)S(1)}, u32[]{:S(2)}) copy-start(bf16[3,64,1792]{2,1,0:T(8,128)(2,1)S(1)} %collective-permute-done.4.refs_1_.refs_11_) | copy-start | bytes 2064388
  127.1 4.6 %copy-start.16 = (bf16[3,64,1792]{2,1,0:T(8,128)(2,1)}, bf16[3,64,1792]{2,1,0:T(8,128)(2,1)S(1)}, u32[]{:S(2)}) copy-start(bf16[3,64,1792]{2,1,0:T(8,128)(2,1)S(1)} %collective-permute-done.9.refs_3_.refs_13_) | copy-start | bytes 2064388
  131.7 4.6 %copy-start.10 = (f32[2,2,64,1024]{3,2,1,0:T(8,128)}, f32[2,2,64,1024]{3,2,1,0:T(8,128)S(1)}, u32[]{:S(2)}) copy-start(f32[2,2,64,1024]{3,2,1,0:T(8,128)S(1)} %get-tuple-element.42) | copy-start | bytes 3145732
  131.7 20.5 %collective-permute-start.10 = (bf16[2,2,64,1024]{3,2,1,0:T(8,128)(2,1)}, bf16[2,2,64,1024]{3,2,1,0:T(8,128)(2,1)}, u32[]{:S(2)}, u32[]{:S(2)}) collective-permute-start(bf16[2,2,64,1024]{3,2,1,0:T(8,128)(2,1)} %get-tuple-element.43), channel_id=1, source_target_pairs={{0,4},{4,0},{8,12},{12,8},{16,20},{20,16},{24,28},{28,24},{1,5},{5... | collective-permute-start | bytes 1572872 | tf_op jit(solution)/shard_map/ppermute | solution.py:404
  132.3 4.0 %copy-start.13 = (bf16[3,64,1792]{2,1,0:T(8,128)(2,1)}, bf16[3,64,1792]{2,1,0:T(8,128)(2,1)S(1)}, u32[]{:S(2)}) copy-start(bf16[3,64,1792]{2,1,0:T(8,128)(2,1)S(1)} %collective-permute-done.17.refs_1_.refs_15_) | copy-start | bytes 2064388
  137.0 15.0 %collective-permute-start.18 = (bf16[1,2,64,1024]{3,2,1,0:T(8,128)(2,1)}, bf16[1,2,64,1024]{3,2,1,0:T(8,128)(2,1)S(1)}, u32[]{:S(2)}, u32[]{:S(2)}) collective-permute-start(bf16[1,2,64,1024]{3,2,1,0:T(8,128)(2,1)} %get-tuple-element.47), channel_id=1, source_target_pairs={{0,4},{4,0},{8,12},{12,8},{16,20},{20,16},{24,28},{28,24},{1,5},{5... | collective-permute-start | bytes 786440 | tf_op jit(solution)/shard_map/ppermute | solution.py:404
  138.5 2.0 %copy-start.1 = (bf16[1024,1792]{1,0:T(8,128)(2,1)S(1)}, bf16[1024,1792]{1,0:T(8,128)(2,1)}, u32[]{:S(2)}) copy-start(bf16[1024,1792]{1,0:T(8,128)(2,1)} %copy-done) | copy-start | bytes 11010052
  140.6 2.0 %copy-start.3 = (bf16[1024,1792]{1,0:T(8,128)(2,1)S(1)}, bf16[1024,1792]{1,0:T(8,128)(2,1)}, u32[]{:S(2)}) copy-start(bf16[1024,1792]{1,0:T(8,128)(2,1)} %copy-done.2) | copy-start | bytes 11010052
  142.6 2.0 %copy-start.5 = (bf16[1792,1024]{1,0:T(8,128)(2,1)S(1)}, bf16[1792,1024]{1,0:T(8,128)(2,1)}, u32[]{:S(2)}) copy-start(bf16[1792,1024]{1,0:T(8,128)(2,1)} %copy-done.4) | copy-start | bytes 11010052
  144.6 7.4 %copy-start.18 = (f32[1,2,64,1024]{3,2,1,0:T(8,128)S(1)}, f32[1,2,64,1024]{3,2,1,0:T(8,128)}, u32[]{:S(2)}) copy-start(f32[1,2,64,1024]{3,2,1,0:T(8,128)} %copy-done.17) | copy-start | bytes 1572868
  149.0 3.1 %copy-start.11 = (f32[2,2,64,1024]{3,2,1,0:T(8,128)S(1)}, f32[2,2,64,1024]{3,2,1,0:T(8,128)}, u32[]{:S(2)}) copy-start(f32[2,2,64,1024]{3,2,1,0:T(8,128)} %copy-done.10) | copy-start | bytes 3145732
  149.0 19.0 %collective-permute-start.27 = (bf16[1,2,64,1024]{3,2,1,0:T(8,128)(2,1)S(1)}, bf16[1,2,64,1024]{3,2,1,0:T(8,128)(2,1)S(1)}, u32[]{:S(2)}, u32[]{:S(2)}) collective-permute-start(bf16[1,2,64,1024]{3,2,1,0:T(8,128)(2,1)S(1)} %get-tuple-element.53), channel_id=1, source_target_pairs={{0,4},{4,0},{8,12},{12,8},{16,20},{20,16},{24,28},{28,24},{1,5},{5... | collective-permute-start | bytes 786440 | tf_op jit(solution)/shard_map/ppermute | solution.py:404
  152.1 16.4 %collective-permute-start.19 = (bf16[2,64,1024]{2,1,0:T(8,128)(2,1)S(1)}, bf16[2,64,1024]{2,1,0:T(8,128)(2,1)S(1)}, u32[]{:S(2)}, u32[]{:S(2)}) collective-permute-start(bf16[2,64,1024]{2,1,0:T(8,128)(2,1)S(1)} %fusion.1), channel_id=1, source_target_pairs={{0,16},{4,20},{8,24},{12,28},{16,0},{20,4},{24,8},{28,12},{1,17},{... | collective-permute-start | bytes 786440 | tf_op jit(solution)/shard_map/ppermute | solution.py:400
  152.2 5.0 %copy-start.15 = (bf16[3,64,1792]{2,1,0:T(8,128)(2,1)S(1)}, bf16[3,64,1792]{2,1,0:T(8,128)(2,1)}, u32[]{:S(2)}) copy-start(bf16[3,64,1792]{2,1,0:T(8,128)(2,1)} %copy-done.14) | copy-start | bytes 2064388
  152.2 5.0 %copy-start.20 = (bf16[2,64,1024]{2,1,0:T(8,128)(2,1)S(1)}, bf16[2,64,1024]{2,1,0:T(8,128)(2,1)}, u32[]{:S(2)}) copy-start(bf16[2,64,1024]{2,1,0:T(8,128)(2,1)} %copy-done.19) | copy-start | bytes 786436
  152.2 4.9 %copy-start.22 = (bf16[2,64,1024]{2,1,0:T(8,128)(2,1)S(1)}, bf16[2,64,1024]{2,1,0:T(8,128)(2,1)}, u32[]{:S(2)}) copy-start(bf16[2,64,1024]{2,1,0:T(8,128)(2,1)} %copy-done.21) | copy-start | bytes 786436
  152.2 4.9 %copy-start.24 = (bf16[2,64,1024]{2,1,0:T(8,128)(2,1)S(1)}, bf16[2,64,1024]{2,1,0:T(8,128)(2,1)}, u32[]{:S(2)}) copy-start(bf16[2,64,1024]{2,1,0:T(8,128)(2,1)} %copy-done.23) | copy-start | bytes 786436
  152.2 4.9 %copy-start.26 = (bf16[2,64,1024]{2,1,0:T(8,128)(2,1)S(1)}, bf16[2,64,1024]{2,1,0:T(8,128)(2,1)}, u32[]{:S(2)}) copy-start(bf16[2,64,1024]{2,1,0:T(8,128)(2,1)} %copy-done.25) | copy-start | bytes 786436
  152.2 4.9 %copy-start.28 = (bf16[2,64,1024]{2,1,0:T(8,128)(2,1)S(1)}, bf16[2,64,1024]{2,1,0:T(8,128)(2,1)}, u32[]{:S(2)}) copy-start(bf16[2,64,1024]{2,1,0:T(8,128)(2,1)} %copy-done.27) | copy-start | bytes 786436
  152.2 4.9 %copy-start.30 = (bf16[2,64,1024]{2,1,0:T(8,128)(2,1)S(1)}, bf16[2,64,1024]{2,1,0:T(8,128)(2,1)}, u32[]{:S(2)}) copy-start(bf16[2,64,1024]{2,1,0:T(8,128)(2,1)} %copy-done.29) | copy-start | bytes 786436
  152.2 4.9 %copy-start.32 = (bf16[2,64,1024]{2,1,0:T(8,128)(2,1)S(1)}, bf16[2,64,1024]{2,1,0:T(8,128)(2,1)}, u32[]{:S(2)}) copy-start(bf16[2,64,1024]{2,1,0:T(8,128)(2,1)} %copy-done.31) | copy-start | bytes 786436
  152.3 4.9 %copy-start.34 = (bf16[2,64,1024]{2,1,0:T(8,128)(2,1)S(1)}, bf16[2,64,1024]{2,1,0:T(8,128)(2,1)}, u32[]{:S(2)}) copy-start(bf16[2,64,1024]{2,1,0:T(8,128)(2,1)} %copy-done.33) | copy-start | bytes 786436
  153.6 19.1 %collective-permute-start.11 = (bf16[2,64,1024]{2,1,0:T(8,128)(2,1)S(1)}, bf16[2,64,1024]{2,1,0:T(8,128)(2,1)S(1)}, u32[]{:S(2)}, u32[]{:S(2)}) collective-permute-start(bf16[2,64,1024]{2,1,0:T(8,128)(2,1)S(1)} %get-tuple-element.57), channel_id=1, source_target_pairs={{0,24},{4,28},{8,0},{12,4},{16,8},{20,12},{24,16},{28,20},{1,25},{... | collective-permute-start | bytes 786440 | tf_op jit(solution)/shard_map/ppermute | solution.py:400
  157.1 15.7 %collective-permute-start.12 = (bf16[2,64,1024]{2,1,0:T(8,128)(2,1)S(1)}, bf16[2,64,1024]{2,1,0:T(8,128)(2,1)S(1)}, u32[]{:S(2)}, u32[]{:S(2)}) collective-permute-start(bf16[2,64,1024]{2,1,0:T(8,128)(2,1)S(1)} %get-tuple-element.58), channel_id=1, source_target_pairs={{0,8},{4,12},{8,16},{12,20},{16,24},{20,28},{24,0},{28,4},{1,9},{5... | collective-permute-start | bytes 786440 | tf_op jit(solution)/shard_map/ppermute | solution.py:400
  (4 other events, 2.9 us)

commit v2 on v1

--- a/solution.py
+++ b/solution.py
@@ -10,10 +10,12 @@
 BF16 = jnp.bfloat16
 F32 = jnp.float32
 MIB = 1 << 20
-PARTIALS_MIB = 24
-PRODUCTS_MIB = 24
+FIRST_MIB = 39
+PARTIALS_MIB = 8
+PRODUCTS_MIB = 10
 HBM = pl.BlockSpec(memory_space=pltpu.HBM)
 VMEM = pl.BlockSpec(memory_space=pltpu.VMEM)
+SMEM = pl.BlockSpec(memory_space=pltpu.SMEM)
 
 
 def tile_of(units):
@@ -76,109 +78,120 @@
         lax.fori_loop(0, steps, lambda j, c: (body(j), c)[1], 0)
 
 
-def prepare(where, tokens, out_grad, gate_mask, up_mask, down_mask, units):
-    rows, feats = tokens.shape
+def load_half(pair, k, half, core, second):
+    first = pl.multiple_of(half * (1 - core if second else core), half)
+    return pair[k, pl.ds(first, half), :]
+
+
+def first_partials(where, shard, weights, masks):
+    _, rows, feats = shard.shape
     half = rows // 2
+    units = weights[0].shape[1]
     blocks = feats // BLOCK
-    sources = (gate_mask, up_mask, down_mask, tokens, out_grad)
-
-    def body(where_ref, *refs):
-        srcs, (pair, kg, ku, kd), bufs, sems = refs[:5], refs[5:9], refs[9:14], refs[14]
-        copies = [
-            pltpu.make_async_copy(src, buf, sems.at[k])
-            for k, (src, buf) in enumerate(zip(srcs, bufs))
-        ]
-        for copy in copies:
-            copy.start()
+    _, steps, at = tiles(units)
+
+    def body(where_ref, pair, masks_ref, *refs):
+        w_refs, (keep_ref, send_ref), bufs = refs[:3], refs[3:5], refs[5:8]
+        expanded, lhs, sems = refs[8:11], refs[11], refs[12]
         col, row, core = where_ref[0], where_ref[1], where_ref[2]
-        count = gate_mask.shape[1]
+
+        def copies(j):
+            part = at(j)
+            spots = [(slice(None), part), (slice(None), part), (part, slice(None))]
+            return [
+                pltpu.make_async_copy(src.at[spot], dst.at[spot], sems.at[k, j])
+                for k, (src, dst, spot) in enumerate(zip(w_refs, bufs, spots))
+            ]
+
+        def start(j):
+            for copy in copies(j):
+                copy.start()
+
+        for_steps(steps, start)
+        count = masks_ref.shape[1]
         block = lax.div(
             row * units + lax.broadcasted_iota(jnp.int32, (count, units), 1), BLOCK
         )
         pick = (lax.broadcasted_iota(jnp.int32, (count, units), 0) == block).astype(F32)
         pick = pick.astype(BF16)
-        shape = (blocks, gate_mask.shape[0])
-        feature = col * blocks + lax.broadcasted_iota(jnp.int32, shape, 0)
-        mine = (lax.broadcasted_iota(jnp.int32, shape, 1) == feature).astype(F32).astype(BF16)
-        for k, out in enumerate((kg, ku, kd)):
-            copies[k].wait()
-            mask = dot_nn(mine, bufs[k][...].astype(F32).astype(BF16))
+        total = masks_ref.shape[0] // 3
+        feature = col * blocks + lax.broadcasted_iota(jnp.int32, (blocks, total), 0)
+        mine = (
+            (lax.broadcasted_iota(jnp.int32, (blocks, total), 1) == feature)
+            .astype(F32)
+            .astype(BF16)
+        )
+        for k, out in enumerate(expanded):
+            mask = dot_nn(mine, masks_ref[pl.ds(k * total, total), :])
             if k < 2:
                 out[...] = dot_nn(mask.astype(BF16), pick)
             else:
                 out[...] = dot_tn(pick, mask.T.astype(BF16))
         for k in range(2):
-            copies[3 + k].wait()
-            low, high = bufs[3 + k][pl.ds(0, half), :], bufs[3 + k][pl.ds(half, half), :]
-            pair[k, pl.ds(0, half), :] = jnp.where(core == 1, high, low)
-            pair[k, pl.ds(half, half), :] = jnp.where(core == 1, low, high)
-
+            for second in range(2):
+                lhs[k, pl.ds(second * half, half), :] = load_half(pair, k, half, core, second)
+
+        def step(j):
+            part = at(j)
+            for copy in copies(j):
+                copy.wait()
+            gate = keep_rows(bufs[0][:, part], expanded[0][:, part])
+            up = keep_rows(bufs[1][:, part], expanded[1][:, part])
+            down = keep_columns(bufs[2][part, :], expanded[2][part, :])
+            bufs[0][:, part] = gate
+            bufs[1][:, part] = up
+            bufs[2][part, :] = down
+            for k, out in enumerate((dot_nn(lhs[0], gate), dot_nn(lhs[0], up), dot_nt(lhs[1], down))):
+                keep_ref[k, :, part] = out[:half]
+                send_ref[k, :, part] = out[half:]
+
+        for_steps(steps, step)
+
+    out_shape = [jax.ShapeDtypeStruct((3, half, units), F32)] * 2
+    out_shape += [jax.ShapeDtypeStruct(w.shape, w.dtype) for w in weights]
+    out_shape += [jax.ShapeDtypeStruct((blocks, units), F32)] * 2
+    out_shape.append(jax.ShapeDtypeStruct((units, blocks), F32))
     return pl.pallas_call(
         body,
-        in_specs=[pl.BlockSpec(memory_space=pltpu.SMEM)] + [HBM] * 5,
-        out_specs=[VMEM] * 4,
-        out_shape=[
-            jax.ShapeDtypeStruct((2, rows, feats), BF16),
-            jax.ShapeDtypeStruct((blocks, units), F32),
-            jax.ShapeDtypeStruct((blocks, units), F32),
-            jax.ShapeDtypeStruct((units, blocks), F32),
+        in_specs=[SMEM, VMEM, VMEM] + [HBM] * 3,
+        out_specs=[VMEM] * 8,
+        out_shape=out_shape,
+        scratch_shapes=[
+            pltpu.VMEM((2, rows, feats), BF16),
+            pltpu.SemaphoreType.DMA((3, steps)),
         ],
-        scratch_shapes=[pltpu.VMEM(a.shape, a.dtype) for a in sources]
-        + [pltpu.SemaphoreType.DMA((5,))],
-        cost_estimate=pl.CostEstimate(flops=0, bytes_accessed=4 * MIB, transcendentals=0),
-        compiler_params=params(16),
-        name="prepare",
-    )(where, *sources)
-
-
-def partials(shards, weights, keeps=None):
+        cost_estimate=cost(12 * half * feats * units, shard, *weights, *out_shape),
+        compiler_params=params(FIRST_MIB),
+        name="first_partials",
+    )(where, shard, masks, *weights)
+
+
+def partials(where, shards, weights):
     n = len(shards)
-    m = 3 if keeps else 0
     _, rows, feats = shards[0].shape
     half = rows // 2
     own = n * half
     units = weights[0].shape[1]
     _, steps, at = tiles(units)
 
-    def body(*refs):
+    def body(where_ref, *refs):
         pairs = refs[:n]
-        w_refs = refs[n : n + 3]
-        masks = refs[n + 3 : n + 3 + m]
-        keep_ref, send_ref = refs[n + 3 + m : n + 5 + m]
-        bufs = refs[n + 5 + m : n + 5 + 2 * m] if keeps else w_refs
-        lhs = refs[n + 5 + 2 * m]
-
-        def copies(j):
-            part = at(j)
-            spots = [(slice(None), part), (slice(None), part), (part, slice(None))]
-            return [
-                pltpu.make_async_copy(src.at[spot], dst.at[spot], refs[-1].at[k, j])
-                for k, (src, dst, spot) in enumerate(zip(w_refs, bufs, spots))
-            ]
-
-        def start(j):
-            for copy in copies(j):
-                copy.start()
-
-        if keeps:
-            for_steps(steps, start)
+        gate_ref, up_ref, down_ref, keep_ref, send_ref, lhs = refs[n:]
+        core = where_ref[2]
         for k in range(2):
             for i, pair in enumerate(pairs):
-                lhs[k, pl.ds(i * half, half), :] = pair[k, pl.ds(0, half), :]
-                lhs[k, pl.ds(own + i * half, half), :] = pair[k, pl.ds(half, half), :]
+                for second in range(2):
+                    lhs[k, pl.ds(second * own + i * half, half), :] = load_half(
+                        pair, k, half, core, second
+                    )
 
         def step(j):
             part = at(j)
-            gate, up, down = (
-                (lambda k=k: bufs[k][:, part] if k < 2 else bufs[k][part, :]) for k in range(3)
+            outs = (
+                dot_nn(lhs[0], gate_ref[:, part]),
+                dot_nn(lhs[0], up_ref[:, part]),
+                dot_nt(lhs[1], down_ref[part, :]),
             )
-            if keeps:
-                for copy in copies(j):
-                    copy.wait()
-                bufs[0][:, part] = keep_rows(gate(), masks[0][:, part])
-                bufs[1][:, part] = keep_rows(up(), masks[1][:, part])
-                bufs[2][part, :] = keep_columns(down(), masks[2][part, :])
-            outs = (dot_nn(lhs[0], gate()), dot_nn(lhs[0], up()), dot_nt(lhs[1], down()))
             for k, out in enumerate(outs):
                 keep_ref[k, :, part] = out[:own]
                 send_ref[k, :, part] = out[own:]
@@ -186,21 +199,44 @@
         for_steps(steps, step)
 
     out_shape = [jax.ShapeDtypeStruct((3, own, units), F32)] * 2
-    if keeps:
-        out_shape += [jax.ShapeDtypeStruct(w.shape, w.dtype) for w in weights]
-    scratch = [pltpu.VMEM((2, 2 * own, feats), BF16)]
-    if keeps:
-        scratch.append(pltpu.SemaphoreType.DMA((3, steps)))
     return pl.pallas_call(
         body,
-        in_specs=[VMEM] * n + [HBM if keeps else VMEM] * 3 + [VMEM] * m,
-        out_specs=[VMEM] * (2 + m),
+        in_specs=[SMEM] + [VMEM] * (n + 3),
+        out_specs=[VMEM] * 2,
         out_shape=out_shape,
-        scratch_shapes=scratch,
+        scratch_shapes=[pltpu.VMEM((2, 2 * own, feats), BF16)],
         cost_estimate=cost(12 * own * feats * units, *shards, *weights, *out_shape),
         compiler_params=params(PARTIALS_MIB),
         name="partials",
-    )(*shards, *weights, *(keeps or ()))
+    )(where, *shards, *weights)
+
+
+def finish(where, parts):
+    _, rows, feats = parts[0].shape
+    half = rows // 2
+
+    def body(where_ref, *refs):
+        part_refs, outs = refs[:-2], refs[-2:]
+        core = where_ref[2]
+        for k, out in enumerate(outs):
+            total = part_refs[0][k].astype(F32)
+            for ref in part_refs[1:]:
+                total = total + ref[k].astype(F32)
+            total = total.astype(BF16)
+            low, high = total[:half], total[half:]
+            out[pl.ds(0, half), :] = jnp.where(core == 1, high, low)
+            out[pl.ds(half, half), :] = jnp.where(core == 1, low, high)
+
+    out_shape = [jax.ShapeDtypeStruct((rows, feats), BF16)] * 2
+    return pl.pallas_call(
+        body,
+        in_specs=[SMEM] + [VMEM] * len(parts),
+        out_specs=[VMEM] * 2,
+        out_shape=out_shape,
+        cost_estimate=cost(2 * rows * feats * len(parts), *parts, *out_shape),
+        compiler_params=params(8),
+        name="finish",
+    )(where, *parts)
 
 
 def activate(keep, near, far):
@@ -228,7 +264,7 @@
         out_specs=VMEM,
         out_shape=jax.ShapeDtypeStruct(keep.shape, BF16),
         cost_estimate=cost(20 * keep.size, keep, near, *far),
-        compiler_params=params(16),
+        compiler_params=params(8),
         name="activate",
     )(keep, near, *far)
 
@@ -288,7 +324,7 @@
     )(*pieces, *weights)
 
 
-def weight_grads(groups, parts, keeps):
+def weight_grads(where, groups, parts, keeps):
     flat = [s for g in groups for s in g]
     pieces = [a for pair in parts for a in pair]
     n, m = len(flat), len(pieces)
@@ -298,8 +334,9 @@
     tokens = n * rows
     tile, steps, at = tiles(units)
 
-    def body(*refs):
+    def body(where_ref, *refs):
         shards = list(refs[:n])
+        core = where_ref[2]
         piece_refs = refs[n : n + m]
         kg, ku, kd = refs[n + m : n + m + 3]
         grads = refs[n + m + 3 : n + m + 6]
@@ -309,8 +346,8 @@
             for side in range(2):
                 for i in range(len(group)):
                     pair = shards[shard + i]
-                    lhs[pl.ds(row, half), :] = pair[0, pl.ds(side * half, half), :]
-                    rhs[pl.ds(row, half), :] = pair[1, pl.ds(side * half, half), :]
+                    lhs[pl.ds(row, half), :] = load_half(pair, 0, half, core, side)
+                    rhs[pl.ds(row, half), :] = load_half(pair, 1, half, core, side)
                     row += half
             shard += len(group)
         turned[...] = lhs[...].T
@@ -353,7 +390,7 @@
     ]
     return pl.pallas_call(
         body,
-        in_specs=[VMEM] * (n + m + 3),
+        in_specs=[SMEM] + [VMEM] * (n + m + 3),
         out_specs=[HBM] * 3,
         out_shape=out_shape,
         scratch_shapes=[
@@ -366,9 +403,9 @@
             pltpu.SemaphoreType.DMA((3, steps)),
         ],
         cost_estimate=cost(6 * tokens * feats * units, *flat, *pieces, *out_shape),
-        compiler_params=params(48),
+        compiler_params=params(32),
         name="weight_grads",
-    )(*flat, *pieces, *keeps)
+    )(where, *flat, *pieces, *keeps)
 
 
 def per_device(
@@ -389,11 +426,9 @@
     while (2 * xs) ** 2 <= rows_n and rows_n % (2 * xs) == 0:
         xs *= 2
     zs = rows_n // xs
-    units = gate_weight.shape[1]
     row_index = lax.axis_index("row")
     col_index = lax.axis_index("col")
     core = col_index % cores
-    half = tokens.shape[0] // 2
 
     def shift_z(value, by):
         pairs = [(i, ((i // xs + by) % zs) * xs + i % xs) for i in range(rows_n)]
@@ -411,15 +446,9 @@
         pairs = [(i, i // cores * cores + (i % cores + 1) % cores) for i in range(cols_n)]
         return lax.ppermute(value, "col", pairs)
 
-    pair, *keeps = prepare(
-        jnp.stack([col_index, row_index, core]),
-        tokens,
-        out_grad,
-        gate_mask,
-        up_mask,
-        down_mask.T,
-        units,
-    )
+    where = jnp.stack([col_index, row_index, core])
+    pair = jnp.stack([tokens, out_grad])
+    masks = jnp.concatenate([gate_mask, up_mask, down_mask.T]).astype(BF16)
 
     far_z = [d for k in range(1, zs // 2 + 1) for d in dict.fromkeys((k, zs - k))]
     held = {(0, 0): pair}
@@ -449,15 +478,20 @@
     for k, chunk in enumerate(chunks):
         if not chunk:
             continue
-        keep, send, *kept = partials([held[s] for s in chunk], weights, keeps if k == 0 else None)
-        weights = kept or weights
+        at = "last" if k == len(chunks) - 1 else k
+        shards = [held[s] for s in chunk]
+        if k == 0:
+            keep, send, *rest = first_partials(where, *shards, weights, masks)
+            weights, keeps = rest[:3], rest[3:]
+        else:
+            keep, send = partials(where, shards, weights)
         near = swap_core(send)
         out = (keep + near).astype(BF16)
         far = [shift_y(out, by) for by in range(1, ys)]
         own = activate(keep, near, far)
         parts[k] = (own, swap_core(own))
 
-    total = None
+    terms = []
     for group in groups:
         shards = [s for c in group for s in chunks[c]]
         dzs = list(dict.fromkeys(s[0] for s in shards))
@@ -475,14 +509,12 @@
             value = sums[k]
             if dz:
                 value = shift_z(value.astype(BF16), -dz)
-            total = value.astype(F32) if total is None else total + value
+            terms.append(value)
     order = [k for k in range(len(chunks)) if chunks[k]]
     grads = weight_grads(
-        [[held[s] for s in chunks[k]] for k in order], [parts[k] for k in order], keeps
+        where, [[held[s] for s in chunks[k]] for k in order], [parts[k] for k in order], keeps
     )
-    total = total.astype(BF16)
-    total = jnp.where(core == 1, jnp.roll(total, half, axis=1), total)
-    return (total[0], total[1], *grads)
+    return (*finish(where, terms), *grads)
 
 
 def solution(mesh):

time: 177 us -> 173 us (0.977)
  local copies, waits for them, and re-layouts: 17.9 us -> 0.04 us
  waiting for transfers between devices: 81.5 us -> 96.4 us
  other arithmetic: 2.24 us -> 4.03 us
    unnamed x80 -> x0, local copies, waits for them, and re-layouts: 17.1 us -> none
    ppermute x6, waiting for transfers between devices: 11.5 us -> 24.1 us  [shift_z(): return lax.ppermute(value, 'row', pairs)]
    ppermute x5, waiting for transfers between devices: 46.8 us -> 53.8 us  [shift_y(): return lax.ppermute(value, 'col', pairs)]
    ppermute x7, waiting for transfers between devices: 23.1 us -> 17.8 us  [shift_x(): return lax.ppermute(value, 'row', pairs)]
    pallas_call x3, Pallas kernels: 13 us -> 10.3 us  [products(): pl.pallas_call(body, in_specs=[VMEM] * (n + 3), out_specs=[VMEM] * outs_n...]
  transfers between devices with their start and end apart: 28 -> 28, of which waited for: 14 -> 11; matrix products, arithmetic and copies ran while one was open for 1% -> 2% of each run, Pallas kernels for 25% -> 23%
where the time goes in v2:
time: 173 us; the launch traced here: 171 us
  waiting for transfers between devices  96.4 us (56%)
  Pallas kernels  44.3 us (26%)
  starting transfers between devices  25.4 us (15%)
  other arithmetic  4.03 us (2%)
    ppermute x5, waiting for transfers between devices, shift_y(): return lax.ppermute(value, 'col', pairs)  53.8 us
    ppermute x6, waiting for transfers between devices, shift_z(): return lax.ppermute(value, 'row', pairs)  24.1 us
    ppermute x7, waiting for transfers between devices, shift_x(): return lax.ppermute(value, 'row', pairs)  17.8 us
    pallas_call x4, Pallas kernels, partials(): pl.pallas_call(body, in_specs=[SMEM] + [VMEM] * (n + 3), out_specs=[VMEM]...  15.8 us
    pallas_call x3, Pallas kernels, products(): pl.pallas_call(body, in_specs=[VMEM] * (n + 3), out_specs=[VMEM] * outs_n...  10.3 us
    ppermute x6, starting transfers between devices, shift_z(): return lax.ppermute(value, 'row', pairs)  9.88 us
    pallas_call x1, Pallas kernels, weight_grads(): pl.pallas_call(body, in_specs=[SMEM] + [VMEM] * (n + m + 3), out_specs=[H...  9.3 us
    ppermute x7, starting transfers between devices, shift_x(): return lax.ppermute(value, 'row', pairs)  7.76 us
  transfers between devices with their start and end apart: 28, of which 11 were waited for; matrix products, arithmetic and copies ran while one was open for 2% of the time, Pallas kernels for 23%

profile of v2, /device:TPU:0, one launch (start us, length us, event | category | flops | bytes accessed | tf_op | source)
XLA Modules:
  0.0 171.0 jit_solution(7574988148644741741)
XLA Ops:
  0.6 1.0 pad_maximum_fusion.pair.refs_0_
  1.6 5.1 %collective-permute-start.1 = (bf16[2,64,1024]{2,1,0:T(8,128)(2,1)S(1)}, bf16[2,64,1024]{2,1,0:T(8,128)(2,1)S(1)}, u32[]{:S(2)}, u32[]{:S(2)}) collective-permute-start(bf16[2,64,1024]{2,1,0:T(8,128)(2,1)S(1)} %pad_maximum_fusion.pair.refs_0_), channel_id=1, source_target_pairs={{0,24},{4,28},{8,0},{12,4},{16,8},{20,12},{24,16},{28,20},{1,25},{... | collective-permute-start | bytes 786440 | tf_op jit(solution)/shard_map/ppermute | solution.py:435
  6.8 0.7 convert.14
  7.5 0.7 convert.15
  8.2 0.7 convert_bitcast_fusion
  8.9 0.1 pad_add_fusion.where_ref
  9.0 5.9 %first_partials.1 = (f32[3,32,1792]{2,1,0:T(8,128)S(1)}, f32[3,32,1792]{2,1,0:T(8,128)S(1)}, bf16[1024,1792]{1,0:T(8,128)(2,1)S(1)}, bf16[1024,1792]{1,0:T(8,128...) custom-call(s32[3]{0:T(128)S(1)} %pad_add_fusion.where_ref, ...), custom_call_target="tpu_custom_call" | custom-call | flops 704643072 | bytes 23830528 | tf_op jit(solution)/shard_map/first_partials/pallas_call | solution.py:154
  15.0 3.9 %collective-permute-done.refs_0_.refs_1_ = bf16[2,64,1024]{2,1,0:T(8,128)(2,1)S(1)} collective-permute-done((bf16[2,64,1024]{2,1,0:T(8,128)(2,1)S(1)}, bf16[2,64,1024]{2,1,0:T(8,128)(2,1)S(1)}, u32[]{:S(2)}, u32[]{:S(2)}) %collective-permute-start) | collective-permute-done | bytes 262176 | tf_op jit(solution)/shard_map/ppermute | solution.py:435
  18.8 4.0 %partials.4 = (f32[3,64,1792]{2,1,0:T(8,128)S(1)}, f32[3,64,1792]{2,1,0:T(8,128)S(1)}) custom-call(s32[3]{0:T(128)S(1)} %pad_add_fusion.where_ref, bf16[2,64,1024]{2,1,0:T(8,128)(2,1)S(1)} %collective-permute-done.refs_0_.refs_1_, bf16[2,64,1024]{2,1,0:T(8,128)(2,1)S(1)} %collective-permute-done.1.refs_1_.refs_2_, ...), custom_call_target="tpu_custom_call" | custom-call | flops 1409286144 | bytes 14286848 | tf_op jit(solution)/shard_map/partials/pallas_call | solution.py:202
  22.8 0.1 collective-permute-start.2
  22.9 0.8 collective-permute-start.13
  23.7 1.5 collective-permute-start.6
  25.2 0.5 collective-permute-start.5
  25.7 12.4 %collective-permute-done.13.refs_0_.refs_5_ = bf16[2,64,1024]{2,1,0:T(8,128)(2,1)S(1)} collective-permute-done((bf16[2,64,1024]{2,1,0:T(8,128)(2,1)S(1)}, bf16[2,64,1024]{2,1,0:T(8,128)(2,1)S(1)}, u32[]{:S(2)}, u32[]{:S(2)}) %collective-permute-start.13) | collective-permute-done | bytes 262176 | tf_op jit(solution)/shard_map/ppermute | solution.py:435
  38.1 1.5 collective-permute-start.23
  39.6 0.5 collective-permute-start.14
  40.2 4.0 %partials.5 = (f32[3,64,1792]{2,1,0:T(8,128)S(1)}, f32[3,64,1792]{2,1,0:T(8,128)S(1)}) custom-call(s32[3]{0:T(128)S(1)} %pad_add_fusion.where_ref, bf16[2,64,1024]{2,1,0:T(8,128)(2,1)S(1)} %collective-permute-done.5.refs_0_.refs_3_, bf16[2,64,1024]{2,1,0:T(8,128)(2,1)S(1)} %collective-permute-done.6.refs_1_.refs_4_, ...), custom_call_target="tpu_custom_call" | custom-call | flops 1409286144 | bytes 14286848 | tf_op jit(solution)/shard_map/partials/pallas_call | solution.py:202
  44.1 0.1 collective-permute-start.7
  44.2 3.1 %collective-permute-done.23.refs_0_.refs_7_ = bf16[2,64,1024]{2,1,0:T(8,128)(2,1)S(1)} collective-permute-done((bf16[2,64,1024]{2,1,0:T(8,128)(2,1)S(1)}, bf16[2,64,1024]{2,1,0:T(8,128)(2,1)S(1)}, u32[]{:S(2)}, u32[]{:S(2)}) %collective-permute-start.23) | collective-permute-done | bytes 262176 | tf_op jit(solution)/shard_map/ppermute | solution.py:439
  47.3 3.9 %partials.7 = (f32[3,32,1792]{2,1,0:T(8,128)S(1)}, f32[3,32,1792]{2,1,0:T(8,128)S(1)}) custom-call(s32[3]{0:T(128)S(1)} %pad_add_fusion.where_ref, bf16[2,64,1024]{2,1,0:T(8,128)(2,1)S(1)} %collective-permute-done.23.refs_0_.refs_7_, bf16[1024,1792]{1,0:T(8,128)(2,1)S(1)} %get-tuple-element.32.refs_2_.refs_4_.refs_1_, ...), custom_call_target="tpu_custom_call" | custom-call | flops 704643072 | bytes 12648448 | tf_op jit(solution)/shard_map/partials/pallas_call | solution.py:202
  51.2 0.1 collective-permute-start.24
  51.2 0.3 collective-permute-done.14.refs_1_.refs_6_
  51.5 4.0 %partials.6 = (f32[3,64,1792]{2,1,0:T(8,128)S(1)}, f32[3,64,1792]{2,1,0:T(8,128)S(1)}) custom-call(s32[3]{0:T(128)S(1)} %pad_add_fusion.where_ref, bf16[2,64,1024]{2,1,0:T(8,128)(2,1)S(1)} %collective-permute-done.13.refs_0_.refs_5_, bf16[2,64,1024]{2,1,0:T(8,128)(2,1)S(1)} %collective-permute-done.14.refs_1_.refs_6_, ...), custom_call_target="tpu_custom_call" | custom-call | flops 1409286144 | bytes 14286848 | tf_op jit(solution)/shard_map/partials/pallas_call | solution.py:202
  55.5 0.3 collective-permute-start.15
  55.8 0.1 add_convert_fusion.5
  55.9 1.6 collective-permute-start.21
  57.4 0.1 add_convert_fusion.2
  57.6 0.6 collective-permute-start.3
  58.1 0.1 add_convert_fusion.1
  58.3 1.6 collective-permute-start.8
  59.9 0.1 add_convert_fusion
  60.0 0.6 collective-permute-start.16
  60.6 0.1 add_convert_fusion.4
  60.6 1.6 collective-permute-start.25
  62.2 19.4 %collective-permute-done.3.refs_2_ = bf16[3,64,1792]{2,1,0:T(8,128)(2,1)S(1)} collective-permute-done((bf16[3,64,1792]{2,1,0:T(8,128)(2,1)S(1)}, bf16[3,64,1792]{2,1,0:T(8,128)(2,1)S(1)}, u32[]{:S(2)}, u32[]{:S(2)}) %collective-permute-start.3) | collective-permute-done | bytes 688160 | tf_op jit(solution)/shard_map/ppermute | solution.py:443
  81.6 0.4 activate.5.refs_0_.refs_10_
  82.0 0.1 collective-permute-start.4
  82.1 14.3 %collective-permute-done.8.refs_2_ = bf16[3,64,1792]{2,1,0:T(8,128)(2,1)S(1)} collective-permute-done((bf16[3,64,1792]{2,1,0:T(8,128)(2,1)S(1)}, bf16[3,64,1792]{2,1,0:T(8,128)(2,1)S(1)}, u32[]{:S(2)}, u32[]{:S(2)}) %collective-permute-start.8) | collective-permute-done | bytes 688160 | tf_op jit(solution)/shard_map/ppermute | solution.py:443
  96.3 0.4 activate.6.refs_2_.refs_12_
  96.8 0.1 collective-permute-start.9
  96.9 0.2 activate.8.refs_0_.refs_8_
  97.1 0.6 collective-permute-start.22
  97.6 20.2 %collective-permute-done.25.refs_2_ = bf16[3,32,1792]{2,1,0:T(8,128)(2,1)S(1)} collective-permute-done((bf16[3,32,1792]{2,1,0:T(8,128)(2,1)S(1)}, bf16[3,32,1792]{2,1,0:T(8,128)(2,1)S(1)}, u32[]{:S(2)}, u32[]{:S(2)}) %collective-permute-start.25) | collective-permute-done | bytes 344096 | tf_op jit(solution)/shard_map/ppermute | solution.py:443
  117.8 0.2 activate.9.refs_2_.refs_16_
  118.0 0.1 collective-permute-start.26
  118.1 0.4 activate.7.refs_0_.refs_14_
  118.5 0.6 collective-permute-start.17
  119.1 0.7 collective-permute-done.26.refs_3_.refs_17_
  119.7 3.3 %products.5 = (f32[1,2,64,1024]{3,2,1,0:T(8,128)S(1)}, bf16[1,2,64,1024]{3,2,1,0:T(8,128)(2,1)S(1)}) custom-call(bf16[3,32,1792]{2,1,0:T(8,128)(2,1)S(1)} %activate.8.refs_0_.refs_8_, bf16[3,32,1792]{2,1,0:T(8,128)(2,1)S(1)} %collective-permute-done.22.refs_1_.refs_9_, bf16[3,32,1792]{2,1,0:T(8,128)(2,1)S(1)} %activate.9.refs_2_.refs_16_, ...), custom_call_target="tpu_custom_call" | custom-call | flops 1409286144 | bytes 13172736 | tf_op jit(solution)/shard_map/products/pallas_call | solution.py:315
  123.0 1.6 collective-permute-start.27
  124.5 3.8 %products.3 = (f32[2,2,64,1024]{3,2,1,0:T(8,128)S(1)}, bf16[2,2,64,1024]{3,2,1,0:T(8,128)(2,1)S(1)}) custom-call(bf16[3,64,1792]{2,1,0:T(8,128)(2,1)S(1)} %activate.5.refs_0_.refs_10_, bf16[3,64,1792]{2,1,0:T(8,128)(2,1)S(1)} %collective-permute-done.4.refs_1_.refs_11_, bf16[3,64,1792]{2,1,0:T(8,128)(2,1)S(1)} %activate.6.refs_2_.refs_12_, ...), custom_call_target="tpu_custom_call" | custom-call | flops 2818572288 | bytes 15335424 | tf_op jit(solution)/shard_map/products/pallas_call | solution.py:315
  128.3 0.6 collective-permute-start.10
  129.0 3.3 %products.4 = (f32[1,2,64,1024]{3,2,1,0:T(8,128)S(1)}, bf16[1,2,64,1024]{3,2,1,0:T(8,128)(2,1)S(1)}) custom-call(bf16[3,64,1792]{2,1,0:T(8,128)(2,1)S(1)} %activate.7.refs_0_.refs_14_, bf16[3,64,1792]{2,1,0:T(8,128)(2,1)S(1)} %collective-permute-done.17.refs_1_.refs_15_, bf16[1024,1792]{1,0:T(8,128)(2,1)S(1)} %get-tuple-element.32.refs_2_.refs_4_.refs_1_, ...), custom_call_target="tpu_custom_call" | custom-call | flops 1409286144 | bytes 13172736 | tf_op jit(solution)/shard_map/products/pallas_call | solution.py:315
  132.2 1.6 collective-permute-start.18
  133.8 14.4 %collective-permute-done.18 = bf16[1,2,64,1024]{3,2,1,0:T(8,128)(2,1)S(1)} collective-permute-done((bf16[1,2,64,1024]{3,2,1,0:T(8,128)(2,1)S(1)}, bf16[1,2,64,1024]{3,2,1,0:T(8,128)(2,1)S(1)}, u32[]{:S(2)}, u32[]{:S(2)}) %collective-permute-start.18) | collective-permute-done | bytes 262176 | tf_op jit(solution)/shard_map/ppermute | solution.py:439
  148.2 0.1 fusion
  148.3 0.1 collective-permute-start.19
  148.4 0.2 add_convert_fusion.3
  148.6 2.7 %collective-permute-start.12 = (bf16[2,64,1024]{2,1,0:T(8,128)(2,1)S(1)}, bf16[2,64,1024]{2,1,0:T(8,128)(2,1)S(1)}, u32[]{:S(2)}, u32[]{:S(2)}) collective-permute-start(bf16[2,64,1024]{2,1,0:T(8,128)(2,1)S(1)} %get-tuple-element.59), channel_id=1, source_target_pairs={{0,8},{4,12},{8,16},{12,20},{16,24},{20,28},{24,0},{28,4},{1,9},{5... | collective-permute-start | bytes 786440 | tf_op jit(solution)/shard_map/ppermute | solution.py:435
  151.3 1.2 collective-permute-start.11
  152.5 9.3 %weight_grads.1 = (f32[1024,1792]{1,0:T(8,128)}, f32[1024,1792]{1,0:T(8,128)}, f32[1792,1024]{1,0:T(8,128)}) custom-call(s32[3]{0:T(128)S(1)} %pad_add_fusion.where_ref, bf16[2,64,1024]{2,1,0:T(8,128)(2,1)S(1)} %pad_maximum_fusion.pair.refs_0_, bf16[2,64,1024]{2,1,0:T(8,128)(2,1)S(1)} %collective-permute-done.refs_0_.refs_1_, ...), custom_call_target="tpu_custom_call" | custom-call | flops 5637144576 | bytes 29622272 | tf_op jit(solution)/shard_map/weight_grads/pallas_call | solution.py:391
  161.8 6.1 %collective-permute-done.19.refs_2_ = bf16[2,64,1024]{2,1,0:T(8,128)(2,1)S(1)} collective-permute-done((bf16[2,64,1024]{2,1,0:T(8,128)(2,1)S(1)}, bf16[2,64,1024]{2,1,0:T(8,128)(2,1)S(1)}, u32[]{:S(2)}, u32[]{:S(2)}) %collective-permute-start.19) | collective-permute-done | bytes 262176 | tf_op jit(solution)/shard_map/ppermute | solution.py:435
  167.9 1.8 %collective-permute-done.11.refs_0_ = bf16[2,64,1024]{2,1,0:T(8,128)(2,1)S(1)} collective-permute-done((bf16[2,64,1024]{2,1,0:T(8,128)(2,1)S(1)}, bf16[2,64,1024]{2,1,0:T(8,128)(2,1)S(1)}, u32[]{:S(2)}, u32[]{:S(2)}) %collective-permute-start.11) | collective-permute-done | bytes 262176 | tf_op jit(solution)/shard_map/ppermute | solution.py:435
  169.6 1.3 finish.1
  (22 shorter events, 0.1 us)
Async XLA Ops:
  1.6 13.3 %collective-permute-start.1 = (bf16[2,64,1024]{2,1,0:T(8,128)(2,1)S(1)}, bf16[2,64,1024]{2,1,0:T(8,128)(2,1)S(1)}, u32[]{:S(2)}, u32[]{:S(2)}) collective-permute-start(bf16[2,64,1024]{2,1,0:T(8,128)(2,1)S(1)} %pad_maximum_fusion.pair.refs_0_), channel_id=1, source_target_pairs={{0,24},{4,28},{8,0},{12,4},{16,8},{20,12},{24,16},{28,20},{1,25},{... | collective-permute-start | bytes 786440 | tf_op jit(solution)/shard_map/ppermute | solution.py:435
  6.8 12.1 %collective-permute-start = (bf16[2,64,1024]{2,1,0:T(8,128)(2,1)S(1)}, bf16[2,64,1024]{2,1,0:T(8,128)(2,1)S(1)}, u32[]{:S(2)}, u32[]{:S(2)}) collective-permute-start(bf16[2,64,1024]{2,1,0:T(8,128)(2,1)S(1)} %pad_maximum_fusion.pair.refs_0_), channel_id=1, source_target_pairs={{0,8},{4,12},{8,16},{12,20},{16,24},{20,28},{24,0},{28,4},{1,9},{5... | collective-permute-start | bytes 786440 | tf_op jit(solution)/shard_map/ppermute | solution.py:435
  22.8 34.6 %collective-permute-start.2 = (f32[3,64,1792]{2,1,0:T(8,128)S(1)}, f32[3,64,1792]{2,1,0:T(8,128)S(1)}, u32[]{:S(2)}, u32[]{:S(2)}) collective-permute-start(f32[3,64,1792]{2,1,0:T(8,128)S(1)} %get-tuple-element.36), channel_id=1, source_target_pairs={{0,1},{1,0},{2,3},{3,2},{4,5},{5,4},{6,7},{7,6},{8,9},{9,8},{10,11... | collective-permute-start | bytes 4128776 | tf_op jit(solution)/shard_map/ppermute | solution.py:447
  22.9 15.2 %collective-permute-start.13 = (bf16[2,64,1024]{2,1,0:T(8,128)(2,1)S(1)}, bf16[2,64,1024]{2,1,0:T(8,128)(2,1)S(1)}, u32[]{:S(2)}, u32[]{:S(2)}) collective-permute-start(bf16[2,64,1024]{2,1,0:T(8,128)(2,1)S(1)} %pad_maximum_fusion.pair.refs_0_), channel_id=1, source_target_pairs={{0,16},{4,20},{8,24},{12,28},{16,0},{20,4},{24,8},{28,12},{1,17},{... | collective-permute-start | bytes 786440 | tf_op jit(solution)/shard_map/ppermute | solution.py:435
  23.7 15.9 %collective-permute-start.6 = (bf16[2,64,1024]{2,1,0:T(8,128)(2,1)S(1)}, bf16[2,64,1024]{2,1,0:T(8,128)(2,1)S(1)}, u32[]{:S(2)}, u32[]{:S(2)}) collective-permute-start(bf16[2,64,1024]{2,1,0:T(8,128)(2,1)S(1)} %collective-permute-done.1.refs_1_.refs_2_), channel_id=1, source_target_pairs={{0,4},{4,0},{8,12},{12,8},{16,20},{20,16},{24,28},{28,24},{1,5},{5... | collective-permute-start | bytes 786440 | tf_op jit(solution)/shard_map/ppermute | solution.py:439
  25.2 15.0 %collective-permute-start.5 = (bf16[2,64,1024]{2,1,0:T(8,128)(2,1)S(1)}, bf16[2,64,1024]{2,1,0:T(8,128)(2,1)S(1)}, u32[]{:S(2)}, u32[]{:S(2)}) collective-permute-start(bf16[2,64,1024]{2,1,0:T(8,128)(2,1)S(1)} %collective-permute-done.refs_0_.refs_1_), channel_id=1, source_target_pairs={{0,4},{4,0},{8,12},{12,8},{16,20},{20,16},{24,28},{28,24},{1,5},{5... | collective-permute-start | bytes 786440 | tf_op jit(solution)/shard_map/ppermute | solution.py:439
  25.7 30.1 %collective-permute-start.20 = (f32[3,32,1792]{2,1,0:T(8,128)S(1)}, f32[3,32,1792]{2,1,0:T(8,128)S(1)}, u32[]{:S(2)}, u32[]{:S(2)}) collective-permute-start(f32[3,32,1792]{2,1,0:T(8,128)S(1)} %get-tuple-element.46), channel_id=1, source_target_pairs={{0,1},{1,0},{2,3},{3,2},{4,5},{5,4},{6,7},{7,6},{8,9},{9,8},{10,11... | collective-permute-start | bytes 2064392 | tf_op jit(solution)/shard_map/ppermute | solution.py:447
  38.1 9.2 %collective-permute-start.23 = (bf16[2,64,1024]{2,1,0:T(8,128)(2,1)S(1)}, bf16[2,64,1024]{2,1,0:T(8,128)(2,1)S(1)}, u32[]{:S(2)}, u32[]{:S(2)}) collective-permute-start(bf16[2,64,1024]{2,1,0:T(8,128)(2,1)S(1)} %pad_maximum_fusion.pair.refs_0_), channel_id=1, source_target_pairs={{0,4},{4,0},{8,12},{12,8},{16,20},{20,16},{24,28},{28,24},{1,5},{5... | collective-permute-start | bytes 786440 | tf_op jit(solution)/shard_map/ppermute | solution.py:439
  39.6 11.9 %collective-permute-start.14 = (bf16[2,64,1024]{2,1,0:T(8,128)(2,1)S(1)}, bf16[2,64,1024]{2,1,0:T(8,128)(2,1)S(1)}, u32[]{:S(2)}, u32[]{:S(2)}) collective-permute-start(bf16[2,64,1024]{2,1,0:T(8,128)(2,1)S(1)} %collective-permute-done.13.refs_0_.refs_5_), channel_id=1, source_target_pairs={{0,4},{4,0},{8,12},{12,8},{16,20},{20,16},{24,28},{28,24},{1,5},{5... | collective-permute-start | bytes 786440 | tf_op jit(solution)/shard_map/ppermute | solution.py:439
  44.1 14.0 %collective-permute-start.7 = (f32[3,64,1792]{2,1,0:T(8,128)S(1)}, f32[3,64,1792]{2,1,0:T(8,128)S(1)}, u32[]{:S(2)}, u32[]{:S(2)}) collective-permute-start(f32[3,64,1792]{2,1,0:T(8,128)S(1)} %get-tuple-element.38), channel_id=1, source_target_pairs={{0,1},{1,0},{2,3},{3,2},{4,5},{5,4},{6,7},{7,6},{8,9},{9,8},{10,11... | collective-permute-start | bytes 4128776 | tf_op jit(solution)/shard_map/ppermute | solution.py:447
  51.2 9.4 %collective-permute-start.24 = (f32[3,32,1792]{2,1,0:T(8,128)S(1)}, f32[3,32,1792]{2,1,0:T(8,128)S(1)}, u32[]{:S(2)}, u32[]{:S(2)}) collective-permute-start(f32[3,32,1792]{2,1,0:T(8,128)S(1)} %get-tuple-element.48), channel_id=1, source_target_pairs={{0,1},{1,0},{2,3},{3,2},{4,5},{5,4},{6,7},{7,6},{8,9},{9,8},{10,11... | collective-permute-start | bytes 2064392 | tf_op jit(solution)/shard_map/ppermute | solution.py:447
  55.5 4.4 %collective-permute-start.15 = (f32[3,64,1792]{2,1,0:T(8,128)S(1)}, f32[3,64,1792]{2,1,0:T(8,128)S(1)}, u32[]{:S(2)}, u32[]{:S(2)}) collective-permute-start(f32[3,64,1792]{2,1,0:T(8,128)S(1)} %get-tuple-element.42), channel_id=1, source_target_pairs={{0,1},{1,0},{2,3},{3,2},{4,5},{5,4},{6,7},{7,6},{8,9},{9,8},{10,11... | collective-permute-start | bytes 4128776 | tf_op jit(solution)/shard_map/ppermute | solution.py:447
  55.9 41.0 %collective-permute-start.21 = (bf16[3,32,1792]{2,1,0:T(8,128)(2,1)S(1)}, bf16[3,32,1792]{2,1,0:T(8,128)(2,1)S(1)}, u32[]{:S(2)}, u32[]{:S(2)}) collective-permute-start(bf16[3,32,1792]{2,1,0:T(8,128)(2,1)S(1)} %add_convert_fusion.5), channel_id=1, source_target_pairs={{0,2},{1,3},{2,0},{3,1},{4,6},{5,7},{6,4},{7,5},{8,10},{9,11},{10,... | collective-permute-start | bytes 1032200 | tf_op jit(solution)/shard_map/ppermute | solution.py:443
  57.6 24.0 %collective-permute-start.3 = (bf16[3,64,1792]{2,1,0:T(8,128)(2,1)S(1)}, bf16[3,64,1792]{2,1,0:T(8,128)(2,1)S(1)}, u32[]{:S(2)}, u32[]{:S(2)}) collective-permute-start(bf16[3,64,1792]{2,1,0:T(8,128)(2,1)S(1)} %add_convert_fusion.2), channel_id=1, source_target_pairs={{0,2},{1,3},{2,0},{3,1},{4,6},{5,7},{6,4},{7,5},{8,10},{9,11},{10,... | collective-permute-start | bytes 2064392 | tf_op jit(solution)/shard_map/ppermute | solution.py:443
  58.3 38.1 %collective-permute-start.8 = (bf16[3,64,1792]{2,1,0:T(8,128)(2,1)S(1)}, bf16[3,64,1792]{2,1,0:T(8,128)(2,1)S(1)}, u32[]{:S(2)}, u32[]{:S(2)}) collective-permute-start(bf16[3,64,1792]{2,1,0:T(8,128)(2,1)S(1)} %add_convert_fusion.1), channel_id=1, source_target_pairs={{0,2},{1,3},{2,0},{3,1},{4,6},{5,7},{6,4},{7,5},{8,10},{9,11},{10,... | collective-permute-start | bytes 2064392 | tf_op jit(solution)/shard_map/ppermute | solution.py:443
  60.0 58.1 %collective-permute-start.16 = (bf16[3,64,1792]{2,1,0:T(8,128)(2,1)S(1)}, bf16[3,64,1792]{2,1,0:T(8,128)(2,1)S(1)}, u32[]{:S(2)}, u32[]{:S(2)}) collective-permute-start(bf16[3,64,1792]{2,1,0:T(8,128)(2,1)S(1)} %add_convert_fusion), channel_id=1, source_target_pairs={{0,2},{1,3},{2,0},{3,1},{4,6},{5,7},{6,4},{7,5},{8,10},{9,11},{10,... | collective-permute-start | bytes 2064392 | tf_op jit(solution)/shard_map/ppermute | solution.py:443
  60.6 57.1 %collective-permute-start.25 = (bf16[3,32,1792]{2,1,0:T(8,128)(2,1)S(1)}, bf16[3,32,1792]{2,1,0:T(8,128)(2,1)S(1)}, u32[]{:S(2)}, u32[]{:S(2)}) collective-permute-start(bf16[3,32,1792]{2,1,0:T(8,128)(2,1)S(1)} %add_convert_fusion.4), channel_id=1, source_target_pairs={{0,2},{1,3},{2,0},{3,1},{4,6},{5,7},{6,4},{7,5},{8,10},{9,11},{10,... | collective-permute-start | bytes 1032200 | tf_op jit(solution)/shard_map/ppermute | solution.py:443
  82.0 42.5 %collective-permute-start.4 = (bf16[3,64,1792]{2,1,0:T(8,128)(2,1)S(1)}, bf16[3,64,1792]{2,1,0:T(8,128)(2,1)S(1)}, u32[]{:S(2)}, u32[]{:S(2)}) collective-permute-start(bf16[3,64,1792]{2,1,0:T(8,128)(2,1)S(1)} %activate.5.refs_0_.refs_10_), channel_id=1, source_target_pairs={{0,1},{1,0},{2,3},{3,2},{4,5},{5,4},{6,7},{7,6},{8,9},{9,8},{10,11... | collective-permute-start | bytes 2064392 | tf_op jit(solution)/shard_map/ppermute | solution.py:447
  96.8 27.8 %collective-permute-start.9 = (bf16[3,64,1792]{2,1,0:T(8,128)(2,1)S(1)}, bf16[3,64,1792]{2,1,0:T(8,128)(2,1)S(1)}, u32[]{:S(2)}, u32[]{:S(2)}) collective-permute-start(bf16[3,64,1792]{2,1,0:T(8,128)(2,1)S(1)} %activate.6.refs_2_.refs_12_), channel_id=1, source_target_pairs={{0,1},{1,0},{2,3},{3,2},{4,5},{5,4},{6,7},{7,6},{8,9},{9,8},{10,11... | collective-permute-start | bytes 2064392 | tf_op jit(solution)/shard_map/ppermute | solution.py:447
  97.1 22.0 %collective-permute-start.22 = (bf16[3,32,1792]{2,1,0:T(8,128)(2,1)S(1)}, bf16[3,32,1792]{2,1,0:T(8,128)(2,1)S(1)}, u32[]{:S(2)}, u32[]{:S(2)}) collective-permute-start(bf16[3,32,1792]{2,1,0:T(8,128)(2,1)S(1)} %activate.8.refs_0_.refs_8_), channel_id=1, source_target_pairs={{0,1},{1,0},{2,3},{3,2},{4,5},{5,4},{6,7},{7,6},{8,9},{9,8},{10,11... | collective-permute-start | bytes 1032200 | tf_op jit(solution)/shard_map/ppermute | solution.py:447
  118.0 1.7 %collective-permute-start.26 = (bf16[3,32,1792]{2,1,0:T(8,128)(2,1)S(1)}, bf16[3,32,1792]{2,1,0:T(8,128)(2,1)S(1)}, u32[]{:S(2)}, u32[]{:S(2)}) collective-permute-start(bf16[3,32,1792]{2,1,0:T(8,128)(2,1)S(1)} %activate.9.refs_2_.refs_16_), channel_id=1, source_target_pairs={{0,1},{1,0},{2,3},{3,2},{4,5},{5,4},{6,7},{7,6},{8,9},{9,8},{10,11... | collective-permute-start | bytes 1032200 | tf_op jit(solution)/shard_map/ppermute | solution.py:447
  118.5 10.5 %collective-permute-start.17 = (bf16[3,64,1792]{2,1,0:T(8,128)(2,1)S(1)}, bf16[3,64,1792]{2,1,0:T(8,128)(2,1)S(1)}, u32[]{:S(2)}, u32[]{:S(2)}) collective-permute-start(bf16[3,64,1792]{2,1,0:T(8,128)(2,1)S(1)} %activate.7.refs_0_.refs_14_), channel_id=1, source_target_pairs={{0,1},{1,0},{2,3},{3,2},{4,5},{5,4},{6,7},{7,6},{8,9},{9,8},{10,11... | collective-permute-start | bytes 2064392 | tf_op jit(solution)/shard_map/ppermute | solution.py:447
  123.0 10.8 %collective-permute-start.27 = (bf16[1,2,64,1024]{3,2,1,0:T(8,128)(2,1)S(1)}, bf16[1,2,64,1024]{3,2,1,0:T(8,128)(2,1)S(1)}, u32[]{:S(2)}, u32[]{:S(2)}) collective-permute-start(bf16[1,2,64,1024]{3,2,1,0:T(8,128)(2,1)S(1)} %get-tuple-element.50), channel_id=1, source_target_pairs={{0,4},{4,0},{8,12},{12,8},{16,20},{20,16},{24,28},{28,24},{1,5},{5... | collective-permute-start | bytes 786440 | tf_op jit(solution)/shard_map/ppermute | solution.py:439
  128.3 20.0 %collective-permute-start.10 = (bf16[2,2,64,1024]{3,2,1,0:T(8,128)(2,1)S(1)}, bf16[2,2,64,1024]{3,2,1,0:T(8,128)(2,1)S(1)}, u32[]{:S(2)}, u32[]{:S(2)}) collective-permute-start(bf16[2,2,64,1024]{3,2,1,0:T(8,128)(2,1)S(1)} %get-tuple-element.40), channel_id=1, source_target_pairs={{0,4},{4,0},{8,12},{12,8},{16,20},{20,16},{24,28},{28,24},{1,5},{5... | collective-permute-start | bytes 1572872 | tf_op jit(solution)/shard_map/ppermute | solution.py:439
  132.2 16.0 %collective-permute-start.18 = (bf16[1,2,64,1024]{3,2,1,0:T(8,128)(2,1)S(1)}, bf16[1,2,64,1024]{3,2,1,0:T(8,128)(2,1)S(1)}, u32[]{:S(2)}, u32[]{:S(2)}) collective-permute-start(bf16[1,2,64,1024]{3,2,1,0:T(8,128)(2,1)S(1)} %get-tuple-element.44), channel_id=1, source_target_pairs={{0,4},{4,0},{8,12},{12,8},{16,20},{20,16},{24,28},{28,24},{1,5},{5... | collective-permute-start | bytes 786440 | tf_op jit(solution)/shard_map/ppermute | solution.py:439
  148.3 19.6 %collective-permute-start.19 = (bf16[2,64,1024]{2,1,0:T(8,128)(2,1)S(1)}, bf16[2,64,1024]{2,1,0:T(8,128)(2,1)S(1)}, u32[]{:S(2)}, u32[]{:S(2)}) collective-permute-start(bf16[2,64,1024]{2,1,0:T(8,128)(2,1)S(1)} %fusion), channel_id=1, source_target_pairs={{0,16},{4,20},{8,24},{12,28},{16,0},{20,4},{24,8},{28,12},{1,17},{... | collective-permute-start | bytes 786440 | tf_op jit(solution)/shard_map/ppermute | solution.py:435
  148.6 19.3 %collective-permute-start.12 = (bf16[2,64,1024]{2,1,0:T(8,128)(2,1)S(1)}, bf16[2,64,1024]{2,1,0:T(8,128)(2,1)S(1)}, u32[]{:S(2)}, u32[]{:S(2)}) collective-permute-start(bf16[2,64,1024]{2,1,0:T(8,128)(2,1)S(1)} %get-tuple-element.59), channel_id=1, source_target_pairs={{0,8},{4,12},{8,16},{12,20},{16,24},{20,28},{24,0},{28,4},{1,9},{5... | collective-permute-start | bytes 786440 | tf_op jit(solution)/shard_map/ppermute | solution.py:435
  151.3 18.3 %collective-permute-start.11 = (bf16[2,64,1024]{2,1,0:T(8,128)(2,1)S(1)}, bf16[2,64,1024]{2,1,0:T(8,128)(2,1)S(1)}, u32[]{:S(2)}, u32[]{:S(2)}) collective-permute-start(bf16[2,64,1024]{2,1,0:T(8,128)(2,1)S(1)} %get-tuple-element.60), channel_id=1, source_target_pairs={{0,24},{4,28},{8,0},{12,4},{16,8},{20,12},{24,16},{28,20},{1,25},{... | collective-permute-start | bytes 786440 | tf_op jit(solution)/shard_map/ppermute | solution.py:435

commit v3 on v2

--- a/solution.py
+++ b/solution.py
@@ -71,16 +71,20 @@
     return tile, units // tile, lambda j: pl.ds(pl.multiple_of(j * tile, tile), tile)
 
 
-def for_steps(steps, body):
+def for_steps(steps, body, unroll=False):
     if steps == 1:
         body(0)
     else:
-        lax.fori_loop(0, steps, lambda j, c: (body(j), c)[1], 0)
-
-
-def load_half(pair, k, half, core, second):
-    first = pl.multiple_of(half * (1 - core if second else core), half)
-    return pair[k, pl.ds(first, half), :]
+        lax.fori_loop(0, steps, lambda j, c: (body(j), c)[1], 0, unroll=unroll)
+
+
+def split_halves(core, store):
+    for c in range(CORES):
+
+        @pl.when(core == c)
+        def _():
+            for second in range(2):
+                store(second, (c + second) % 2)
 
 
 def first_partials(where, shard, weights, masks):
@@ -122,14 +126,17 @@
             .astype(BF16)
         )
         for k, out in enumerate(expanded):
-            mask = dot_nn(mine, masks_ref[pl.ds(k * total, total), :])
+            mask = masks_ref[pl.ds(k * total, total), :].astype(F32).astype(BF16)
+            mask = dot_nn(mine, mask)
             if k < 2:
                 out[...] = dot_nn(mask.astype(BF16), pick)
             else:
                 out[...] = dot_tn(pick, mask.T.astype(BF16))
-        for k in range(2):
-            for second in range(2):
-                lhs[k, pl.ds(second * half, half), :] = load_half(pair, k, half, core, second)
+
+        def store(second, side):
+            lhs[:, pl.ds(second * half, half), :] = pair[:, pl.ds(side * half, half), :]
+
+        split_halves(core, store)
 
         def step(j):
             part = at(j)
@@ -178,12 +185,14 @@
         pairs = refs[:n]
         gate_ref, up_ref, down_ref, keep_ref, send_ref, lhs = refs[n:]
         core = where_ref[2]
-        for k in range(2):
+
+        def store(second, side):
             for i, pair in enumerate(pairs):
-                for second in range(2):
-                    lhs[k, pl.ds(second * own + i * half, half), :] = load_half(
-                        pair, k, half, core, second
-                    )
+                lhs[:, pl.ds(second * own + i * half, half), :] = pair[
+                    :, pl.ds(side * half, half), :
+                ]
+
+        split_halves(core, store)
 
         def step(j):
             part = at(j)
@@ -196,7 +205,7 @@
                 keep_ref[k, :, part] = out[:own]
                 send_ref[k, :, part] = out[own:]
 
-        for_steps(steps, step)
+        for_steps(steps, step, True)
 
     out_shape = [jax.ShapeDtypeStruct((3, own, units), F32)] * 2
     return pl.pallas_call(
@@ -269,24 +278,26 @@
     )(keep, near, *far)
 
 
-def products(parts, counts, slots, sizes, weights):
-    pieces = [a for pair in parts for a in pair]
+def products(shards, slots, sizes, weights):
+    pieces, spots = [], []
+    for own, other, place, half in shards:
+        for piece in (own, other):
+            known = [k for k, p in enumerate(pieces) if p is piece]
+            if not known:
+                pieces.append(piece)
+            spots.append((known[0] if known else len(pieces) - 1, place * half))
     n = len(pieces)
     units = pieces[0].shape[2]
     feats = weights[0].shape[0]
-    half = pieces[0].shape[1] // counts[0]
-    tokens = sum(p.shape[1] for p in pieces)
+    tokens = 2 * half * len(shards)
     _, steps, at = tiles(feats)
     outs_n = len(sizes)
 
     def body(*refs):
-        piece_refs = refs[:n]
         gate_ref, up_ref, down_ref = refs[n : n + 3]
         outs, lhs = refs[n + 3 : n + 3 + outs_n], refs[n + 3 + outs_n]
-        row = 0
-        for piece in piece_refs:
-            lhs[:, pl.ds(row, piece.shape[1]), :] = piece[...]
-            row += piece.shape[1]
+        for k, (piece, row) in enumerate(spots):
+            lhs[:, pl.ds(k * half, half), :] = refs[piece][:, pl.ds(row, half), :]
 
         def step(j):
             part = at(j)
@@ -294,19 +305,13 @@
                 dot_nn(lhs[0], down_ref[:, part]),
                 dot_nt(lhs[1], gate_ref[part, :]) + dot_nt(lhs[2], up_ref[part, :]),
             )
-            row, shard = 0, 0
-            for count in counts:
-                for side in range(2):
-                    for i in range(count):
-                        out, place = slots[shard + i]
-                        for k in range(2):
-                            outs[out][place, k, pl.ds(side * half, half), part] = sums[k][
-                                row : row + half
-                            ].astype(outs[out].dtype)
-                        row += half
-                shard += count
-
-        for_steps(steps, step)
+            for i, (out, place) in enumerate(slots):
+                for k in range(2):
+                    outs[out][place, k, :, part] = sums[k][
+                        2 * half * i : 2 * half * (i + 1)
+                    ].astype(outs[out].dtype)
+
+        for_steps(steps, step, True)
 
     out_shape = [
         jax.ShapeDtypeStruct((size, 2, 2 * half, feats), BF16 if k else F32)
@@ -341,15 +346,19 @@
         kg, ku, kd = refs[n + m : n + m + 3]
         grads = refs[n + m + 3 : n + m + 6]
         lhs, turned, rhs, gate_buf, up_buf, down_buf, sems = refs[n + m + 6 :]
-        row, shard = 0, 0
-        for group in groups:
-            for side in range(2):
+
+        def store(second, side):
+            row, shard = 0, 0
+            for group in groups:
+                size = len(group) * half
                 for i in range(len(group)):
-                    pair = shards[shard + i]
-                    lhs[pl.ds(row, half), :] = load_half(pair, 0, half, core, side)
-                    rhs[pl.ds(row, half), :] = load_half(pair, 1, half, core, side)
-                    row += half
-            shard += len(group)
+                    at_row = pl.ds(row + second * size + i * half, half)
+                    lhs[at_row, :] = shards[shard + i][0, pl.ds(side * half, half), :]
+                    rhs[at_row, :] = shards[shard + i][1, pl.ds(side * half, half), :]
+                row += 2 * size
+                shard += len(group)
+
+        split_halves(core, store)
         turned[...] = lhs[...].T
 
         def copies(j):
@@ -448,7 +457,7 @@
 
     where = jnp.stack([col_index, row_index, core])
     pair = jnp.stack([tokens, out_grad])
-    masks = jnp.concatenate([gate_mask, up_mask, down_mask.T]).astype(BF16)
+    masks = jnp.concatenate([gate_mask, up_mask, down_mask.T])
 
     far_z = [d for k in range(1, zs // 2 + 1) for d in dict.fromkeys((k, zs - k))]
     held = {(0, 0): pair}
@@ -460,27 +469,27 @@
         for dx in range(1, xs):
             held[dz, dx] = shift_x(held[dz, 0], dx)
 
-    z_groups = [far_z[k : k + 2] for k in range(0, len(far_z), 2)]
-    chunks, groups = [[(0, 0)]], []
-    for k, group in enumerate(z_groups):
-        at = len(chunks)
-        if k == 0:
-            chunks.append([(dz, 0) for dz in group])
-            chunks.append([(dz, dx) for dz in group for dx in range(1, xs)])
-        else:
-            chunks.append([(dz, dx) for dx in range(xs) for dz in group])
-        groups.append([c for c in range(at, len(chunks)) if chunks[c]])
-    chunks.append([(0, dx) for dx in range(1, xs)])
-    groups.append([c for c in (0, len(chunks) - 1) if chunks[c]])
+    far_x = range(1, xs)
+    near_z = far_z[:2]
+    chunks = {"own": [(0, 0)], "a": [(dz, 0) for dz in near_z]}
+    chunks["b"] = [(dz, dx) for dz in near_z[:1] for dx in far_x]
+    for k in range(2, len(far_z), 2):
+        chunks[f"m{k}"] = [(dz, dx) for dx in range(xs) for dz in far_z[k : k + 2]]
+    chunks["c"] = [(dz, dx) for dz in near_z[1:] for dx in far_x]
+    chunks["x"] = [(0, dx) for dx in far_x]
+    groups = {"b": near_z[:1]}
+    for k in range(2, len(far_z), 2):
+        groups[f"m{k}"] = far_z[k : k + 2]
+    groups["c"] = near_z[1:]
+    groups["x"] = [0]
+    chunks = {name: chunk for name, chunk in chunks.items() if chunk}
+    groups = {name: group for name, group in groups.items() if group}
 
     parts = {}
     weights = (gate_weight, up_weight, down_weight)
-    for k, chunk in enumerate(chunks):
-        if not chunk:
-            continue
-        at = "last" if k == len(chunks) - 1 else k
+    for name, chunk in chunks.items():
         shards = [held[s] for s in chunk]
-        if k == 0:
+        if name == "own":
             keep, send, *rest = first_partials(where, *shards, weights, masks)
             weights, keeps = rest[:3], rest[3:]
         else:
@@ -489,32 +498,36 @@
         out = (keep + near).astype(BF16)
         far = [shift_y(out, by) for by in range(1, ys)]
         own = activate(keep, near, far)
-        parts[k] = (own, swap_core(own))
-
+        parts[name] = (own, swap_core(own))
+
+    half = tokens.shape[0] // 2
+    homes = {
+        s: (*parts[name], k, half) for name, chunk in chunks.items() for k, s in enumerate(chunk)
+    }
     terms = []
-    for group in groups:
-        shards = [s for c in group for s in chunks[c]]
-        dzs = list(dict.fromkeys(s[0] for s in shards))
+    for group in groups.values():
+        shards = [(dz, dx) for dx in range(xs) for dz in group]
         outs = products(
-            [parts[c] for c in group],
-            [len(chunks[c]) for c in group],
-            [(dx, dzs.index(dz)) for dz, dx in shards],
-            [len(dzs)] * xs,
+            [homes[s] for s in shards],
+            [(dx, group.index(dz)) for dz, dx in shards],
+            [len(group)] * xs,
             weights,
         )
         sums = outs[0]
-        for dx in range(1, xs):
+        for dx in far_x:
             sums = sums + shift_x(outs[dx], -dx)
-        for k, dz in enumerate(dzs):
+        for k, dz in enumerate(group):
             value = sums[k]
             if dz:
                 value = shift_z(value.astype(BF16), -dz)
             terms.append(value)
-    order = [k for k in range(len(chunks)) if chunks[k]]
     grads = weight_grads(
-        where, [[held[s] for s in chunks[k]] for k in order], [parts[k] for k in order], keeps
+        where,
+        [[held[s] for s in chunk] for chunk in chunks.values()],
+        [parts[name] for name in chunks],
+        keeps,
     )
-    return (*finish(where, terms), *grads)
+    return (*finish(where, terms[::-1]), *grads)
 
 
 def solution(mesh):

time: 173 us -> 161 us (0.931); the launches traced: 171 us -> 161 us
  waiting for transfers between devices: 96.4 us -> 72.2 us
  starting transfers between devices: 25.4 us -> 40 us
    ppermute x6, waiting for transfers between devices: 24.1 us -> 12.8 us  [shift_z(): return lax.ppermute(value, 'row', pairs)]
    ppermute x6, starting transfers between devices: 9.88 us -> 20.1 us  [shift_z(): return lax.ppermute(value, 'row', pairs)]
    ppermute x7 -> x8, waiting for transfers between devices: 17.8 us -> 9.66 us  [shift_x(): return lax.ppermute(value, 'row', pairs)]
    ppermute x5 -> x6, waiting for transfers between devices: 53.8 us -> 49.7 us  [shift_y(): return lax.ppermute(value, 'col', pairs)]
    ppermute x7 -> x8, starting transfers between devices: 7.76 us -> 10.4 us  [shift_x(): return lax.ppermute(value, 'row', pairs)]
    pallas_call x3 -> x4, Pallas kernels: 10.3 us -> 12 us  [products(): pl.pallas_call(body, in_specs=[VMEM] * (n + 3), out_specs=[VMEM] * outs_n...]
    ppermute x5 -> x6, starting transfers between devices: 5.9 us -> 7.28 us  [shift_y(): return lax.ppermute(value, 'col', pairs)]
    pallas_call x4 -> x5, Pallas kernels: 15.8 us -> 14.9 us  [partials(): pl.pallas_call(body, in_specs=[SMEM] + [VMEM] * (n + 3), out_specs=[VMEM]...]
  transfers between devices with their start and end apart: 28 -> 32, of which waited for: 11 -> 9; matrix products, arithmetic and copies ran while one was open for 2% -> 1% of each run, Pallas kernels for 23% -> 27%
where the time goes in v3:
time: 161 us
  waiting for transfers between devices  72.2 us (45%)
  Pallas kernels  45.2 us (28%)
  starting transfers between devices  40 us (25%)
  other arithmetic  2.59 us (2%)
    ppermute x6, waiting for transfers between devices, shift_y(): return lax.ppermute(value, 'col', pairs)  49.7 us
    ppermute x6, starting transfers between devices, shift_z(): return lax.ppermute(value, 'row', pairs)  20.1 us
    pallas_call x5, Pallas kernels, partials(): pl.pallas_call(body, in_specs=[SMEM] + [VMEM] * (n + 3), out_specs=[VMEM]...  14.9 us
    ppermute x6, waiting for transfers between devices, shift_z(): return lax.ppermute(value, 'row', pairs)  12.8 us
    pallas_call x4, Pallas kernels, products(): pl.pallas_call(body, in_specs=[VMEM] * (n + 3), out_specs=[VMEM] * outs_n...  12 us
    ppermute x8, starting transfers between devices, shift_x(): return lax.ppermute(value, 'row', pairs)  10.4 us
    ppermute x8, waiting for transfers between devices, shift_x(): return lax.ppermute(value, 'row', pairs)  9.66 us
    pallas_call x1, Pallas kernels, weight_grads(): pl.pallas_call(body, in_specs=[SMEM] + [VMEM] * (n + m + 3), out_specs=[H...  9.46 us
  transfers between devices with their start and end apart: 32, of which 9 were waited for; matrix products, arithmetic and copies ran while one was open for 1% of the time, Pallas kernels for 27%

profile of v3, /device:TPU:0, one launch (start us, length us, event | category | flops | bytes accessed | tf_op | source)
XLA Modules:
  0.0 161.0 jit_solution(11957405037889287030)
XLA Ops:
  0.6 1.0 pad_maximum_fusion.pair.refs_0_
  1.6 4.1 %collective-permute-start.19 = (bf16[2,64,1024]{2,1,0:T(8,128)(2,1)S(1)}, bf16[2,64,1024]{2,1,0:T(8,128)(2,1)S(1)}, u32[]{:S(2)}, u32[]{:S(2)}) collective-permute-start(bf16[2,64,1024]{2,1,0:T(8,128)(2,1)S(1)} %pad_maximum_fusion.pair.refs_0_), channel_id=1, source_target_pairs={{0,16},{4,20},{8,24},{12,28},{16,0},{20,4},{24,8},{28,12},{1,17},{... | collective-permute-start | bytes 786440 | tf_op jit(solution)/shard_map/ppermute | solution.py:444
  5.8 1.3 collective-permute-start.9
  7.1 0.7 collective-permute-start.8
  7.8 0.8 pad_add_fusion.masks_ref
  8.5 0.1 pad_add_fusion.1.where_ref
  8.6 5.9 %first_partials.1 = (f32[3,32,1792]{2,1,0:T(8,128)S(1)}, f32[3,32,1792]{2,1,0:T(8,128)S(1)}, bf16[1024,1792]{1,0:T(8,128)(2,1)S(1)}, bf16[1024,1792]{1,0:T(8,128...) custom-call(s32[3]{0:T(128)S(1)} %pad_add_fusion.1.where_ref, ...), custom_call_target="tpu_custom_call" | custom-call | flops 704643072 | bytes 23830528 | tf_op jit(solution)/shard_map/first_partials/pallas_call | solution.py:161
  14.6 0.1 collective-permute-start
  14.7 1.6 collective-permute-start.3
  16.2 8.3 %collective-permute-done.8.refs_0_.refs_1_ = bf16[2,64,1024]{2,1,0:T(8,128)(2,1)S(1)} collective-permute-done((bf16[2,64,1024]{2,1,0:T(8,128)(2,1)S(1)}, bf16[2,64,1024]{2,1,0:T(8,128)(2,1)S(1)}, u32[]{:S(2)}, u32[]{:S(2)}) %collective-permute-start.8) | collective-permute-done | bytes 262176 | tf_op jit(solution)/shard_map/ppermute | solution.py:444
  24.5 1.5 collective-permute-start.26
  26.0 0.5 collective-permute-start.20
  26.5 1.5 collective-permute-start.13
  28.0 2.8 %partials.6 = (f32[3,64,1792]{2,1,0:T(8,128)S(1)}, f32[3,64,1792]{2,1,0:T(8,128)S(1)}) custom-call(s32[3]{0:T(128)S(1)} %pad_add_fusion.1.where_ref, bf16[2,64,1024]{2,1,0:T(8,128)(2,1)S(1)} %collective-permute-done.8.refs_0_.refs_1_, bf16[2,64,1024]{2,1,0:T(8,128)(2,1)S(1)} %collective-permute-done.9.refs_1_.refs_2_, ...), custom_call_target="tpu_custom_call" | custom-call | flops 1409286144 | bytes 14286848 | tf_op jit(solution)/shard_map/partials/pallas_call | solution.py:211
  30.9 0.1 collective-permute-start.10
  30.9 3.0 %partials.5 = (f32[3,32,1792]{2,1,0:T(8,128)S(1)}, f32[3,32,1792]{2,1,0:T(8,128)S(1)}) custom-call(s32[3]{0:T(128)S(1)} %pad_add_fusion.1.where_ref, bf16[2,64,1024]{2,1,0:T(8,128)(2,1)S(1)} %collective-permute-done.3.refs_0_.refs_7_, bf16[1024,1792]{1,0:T(8,128)(2,1)S(1)} %get-tuple-element.38.refs_1_.refs_4_.refs_2_, ...), custom_call_target="tpu_custom_call" | custom-call | flops 704643072 | bytes 12648448 | tf_op jit(solution)/shard_map/partials/pallas_call | solution.py:211
  34.0 0.6 collective-permute-start.4
  34.5 3.0 %partials.9 = (f32[3,32,1792]{2,1,0:T(8,128)S(1)}, f32[3,32,1792]{2,1,0:T(8,128)S(1)}) custom-call(s32[3]{0:T(128)S(1)} %pad_add_fusion.1.where_ref, bf16[2,64,1024]{2,1,0:T(8,128)(2,1)S(1)} %collective-permute-done.26.refs_0_.refs_3_, bf16[1024,1792]{1,0:T(8,128)(2,1)S(1)} %get-tuple-element.38.refs_1_.refs_4_.refs_2_, ...), custom_call_target="tpu_custom_call" | custom-call | flops 704643072 | bytes 12648448 | tf_op jit(solution)/shard_map/partials/pallas_call | solution.py:211
  37.6 5.3 %collective-permute-done.13.refs_0_.refs_6_ = bf16[2,64,1024]{2,1,0:T(8,128)(2,1)S(1)} collective-permute-done((bf16[2,64,1024]{2,1,0:T(8,128)(2,1)S(1)}, bf16[2,64,1024]{2,1,0:T(8,128)(2,1)S(1)}, u32[]{:S(2)}, u32[]{:S(2)}) %collective-permute-start.13) | collective-permute-done | bytes 262176 | tf_op jit(solution)/shard_map/ppermute | solution.py:448
  42.9 3.0 %partials.7 = (f32[3,32,1792]{2,1,0:T(8,128)S(1)}, f32[3,32,1792]{2,1,0:T(8,128)S(1)}) custom-call(s32[3]{0:T(128)S(1)} %pad_add_fusion.1.where_ref, bf16[2,64,1024]{2,1,0:T(8,128)(2,1)S(1)} %collective-permute-done.13.refs_0_.refs_6_, bf16[1024,1792]{1,0:T(8,128)(2,1)S(1)} %get-tuple-element.38.refs_1_.refs_4_.refs_2_, ...), custom_call_target="tpu_custom_call" | custom-call | flops 704643072 | bytes 12648448 | tf_op jit(solution)/shard_map/partials/pallas_call | solution.py:211
  46.0 0.6 collective-permute-start.14
  46.5 3.0 %partials.8 = (f32[3,64,1792]{2,1,0:T(8,128)S(1)}, f32[3,64,1792]{2,1,0:T(8,128)S(1)}) custom-call(s32[3]{0:T(128)S(1)} %pad_add_fusion.1.where_ref, bf16[2,64,1024]{2,1,0:T(8,128)(2,1)S(1)} %collective-permute-done.19.refs_0_.refs_4_, bf16[2,64,1024]{2,1,0:T(8,128)(2,1)S(1)} %collective-permute-done.20.refs_1_.refs_5_, ...), custom_call_target="tpu_custom_call" | custom-call | flops 1409286144 | bytes 14286848 | tf_op jit(solution)/shard_map/partials/pallas_call | solution.py:211
  49.6 0.1 collective-permute-start.21
  49.7 1.6 collective-permute-start.1
  51.4 8.9 %collective-permute-done.1.refs_2_ = bf16[3,32,1792]{2,1,0:T(8,128)(2,1)S(1)} collective-permute-done((bf16[3,32,1792]{2,1,0:T(8,128)(2,1)S(1)}, bf16[3,32,1792]{2,1,0:T(8,128)(2,1)S(1)}, u32[]{:S(2)}, u32[]{:S(2)}) %collective-permute-start.1) | collective-permute-done | bytes 344096 | tf_op jit(solution)/shard_map/ppermute | solution.py:452
  60.2 1.5 collective-permute-start.5
  61.8 0.2 activate.6.refs_0_.refs_8_
  62.0 0.1 collective-permute-start.2
  62.0 0.1 add_convert_fusion.1
  62.2 0.6 collective-permute-start.11
  62.8 8.3 %collective-permute-done.5.refs_2_ = bf16[3,32,1792]{2,1,0:T(8,128)(2,1)S(1)} collective-permute-done((bf16[3,32,1792]{2,1,0:T(8,128)(2,1)S(1)}, bf16[3,32,1792]{2,1,0:T(8,128)(2,1)S(1)}, u32[]{:S(2)}, u32[]{:S(2)}) %collective-permute-start.5) | collective-permute-done | bytes 344096 | tf_op jit(solution)/shard_map/ppermute | solution.py:452
  71.2 1.5 collective-permute-start.28
  72.7 0.2 activate.7.refs_2_.refs_18_
  72.9 0.1 collective-permute-start.6
  73.0 0.1 add_convert_fusion
  73.1 12.8 %collective-permute-done.11.refs_2_ = bf16[3,64,1792]{2,1,0:T(8,128)(2,1)S(1)} collective-permute-done((bf16[3,64,1792]{2,1,0:T(8,128)(2,1)S(1)}, bf16[3,64,1792]{2,1,0:T(8,128)(2,1)S(1)}, u32[]{:S(2)}, u32[]{:S(2)}) %collective-permute-start.11) | collective-permute-done | bytes 688160 | tf_op jit(solution)/shard_map/ppermute | solution.py:452
  85.9 1.5 collective-permute-start.22
  87.4 0.4 activate.8.refs_0_.refs_10_
  87.9 0.1 collective-permute-start.12
  88.0 0.6 collective-permute-start.15
  88.6 2.9 %products.4 = (f32[1,2,64,1024]{3,2,1,0:T(8,128)S(1)}, bf16[1,2,64,1024]{3,2,1,0:T(8,128)(2,1)S(1)}) custom-call(bf16[3,32,1792]{2,1,0:T(8,128)(2,1)S(1)} %activate.6.refs_0_.refs_8_, bf16[3,32,1792]{2,1,0:T(8,128)(2,1)S(1)} %collective-permute-done.2.refs_1_.refs_9_, bf16[3,32,1792]{2,1,0:T(8,128)(2,1)S(1)} %activate.7.refs_2_.refs_18_, ...), custom_call_target="tpu_custom_call" | custom-call | flops 1409286144 | bytes 13172736 | tf_op jit(solution)/shard_map/products/pallas_call | solution.py:320
  91.6 1.6 collective-permute-start.7
  93.1 14.9 %collective-permute-done.22.refs_2_ = bf16[3,64,1792]{2,1,0:T(8,128)(2,1)S(1)} collective-permute-done((bf16[3,64,1792]{2,1,0:T(8,128)(2,1)S(1)}, bf16[3,64,1792]{2,1,0:T(8,128)(2,1)S(1)}, u32[]{:S(2)}, u32[]{:S(2)}) %collective-permute-start.22) | collective-permute-done | bytes 688160 | tf_op jit(solution)/shard_map/ppermute | solution.py:452
  108.0 0.4 activate.10.refs_0_.refs_14_
  108.5 0.1 collective-permute-start.23
  108.5 0.2 activate.11.refs_2_.refs_12_
  108.7 0.6 collective-permute-start.29
  109.3 4.8 %collective-permute-done.15.refs_2_ = bf16[3,32,1792]{2,1,0:T(8,128)(2,1)S(1)} collective-permute-done((bf16[3,32,1792]{2,1,0:T(8,128)(2,1)S(1)}, bf16[3,32,1792]{2,1,0:T(8,128)(2,1)S(1)}, u32[]{:S(2)}, u32[]{:S(2)}) %collective-permute-start.15) | collective-permute-done | bytes 344096 | tf_op jit(solution)/shard_map/ppermute | solution.py:452
  114.1 0.2 activate.9.refs_2_.refs_16_
  114.3 0.1 collective-permute-start.16
  114.4 0.1 add_bitcast_fusion.refs_0_
  114.5 2.9 %products.7 = (f32[1,2,64,1024]{3,2,1,0:T(8,128)S(1)}, bf16[1,2,64,1024]{3,2,1,0:T(8,128)(2,1)S(1)}) custom-call(bf16[3,64,1792]{2,1,0:T(8,128)(2,1)S(1)} %activate.8.refs_0_.refs_10_, bf16[3,64,1792]{2,1,0:T(8,128)(2,1)S(1)} %collective-permute-done.12.refs_1_.refs_11_, bf16[3,32,1792]{2,1,0:T(8,128)(2,1)S(1)} %activate.11.refs_2_.refs_12_, ...), custom_call_target="tpu_custom_call" | custom-call | flops 1409286144 | bytes 13860864 | tf_op jit(solution)/shard_map/products/pallas_call | solution.py:320
  117.4 1.6 collective-permute-start.30
  119.0 2.9 %products.5 = (f32[1,2,64,1024]{3,2,1,0:T(8,128)S(1)}, bf16[1,2,64,1024]{3,2,1,0:T(8,128)(2,1)S(1)}) custom-call(bf16[3,64,1792]{2,1,0:T(8,128)(2,1)S(1)} %activate.8.refs_0_.refs_10_, bf16[3,64,1792]{2,1,0:T(8,128)(2,1)S(1)} %collective-permute-done.12.refs_1_.refs_11_, bf16[3,32,1792]{2,1,0:T(8,128)(2,1)S(1)} %activate.9.refs_2_.refs_16_, ...), custom_call_target="tpu_custom_call" | custom-call | flops 1409286144 | bytes 13860864 | tf_op jit(solution)/shard_map/products/pallas_call | solution.py:320
  121.9 0.6 collective-permute-start.17
  122.5 3.1 %products.6 = (f32[1,2,64,1024]{3,2,1,0:T(8,128)S(1)}, bf16[1,2,64,1024]{3,2,1,0:T(8,128)(2,1)S(1)}) custom-call(bf16[3,64,1792]{2,1,0:T(8,128)(2,1)S(1)} %activate.10.refs_0_.refs_14_, bf16[3,64,1792]{2,1,0:T(8,128)(2,1)S(1)} %collective-permute-done.23.refs_1_.refs_15_, bf16[1024,1792]{1,0:T(8,128)(2,1)S(1)} %get-tuple-element.38.refs_1_.refs_4_.refs_2_, ...), custom_call_target="tpu_custom_call" | custom-call | flops 1409286144 | bytes 13172736 | tf_op jit(solution)/shard_map/products/pallas_call | solution.py:320
  125.7 1.6 collective-permute-start.24
  127.3 0.7 collective-permute-start.31
  128.0 4.3 %collective-permute-done.17 = bf16[1,2,64,1024]{3,2,1,0:T(8,128)(2,1)S(1)} collective-permute-done((bf16[1,2,64,1024]{3,2,1,0:T(8,128)(2,1)S(1)}, bf16[1,2,64,1024]{3,2,1,0:T(8,128)(2,1)S(1)}, u32[]{:S(2)}, u32[]{:S(2)}) %collective-permute-start.17) | collective-permute-done | bytes 262176 | tf_op jit(solution)/shard_map/ppermute | solution.py:448
  132.3 6.3 %collective-permute-start.18 = (bf16[2,64,1024]{2,1,0:T(8,128)(2,1)S(1)}, bf16[2,64,1024]{2,1,0:T(8,128)(2,1)S(1)}, u32[]{:S(2)}, u32[]{:S(2)}) collective-permute-start(bf16[2,64,1024]{2,1,0:T(8,128)(2,1)S(1)} %fusion), channel_id=1, source_target_pairs={{0,8},{4,12},{8,16},{12,20},{16,24},{20,28},{24,0},{28,4},{1,9},{5... | collective-permute-start | bytes 786440 | tf_op jit(solution)/shard_map/ppermute | solution.py:444
  138.7 7.0 %collective-permute-start.25 = (bf16[2,64,1024]{2,1,0:T(8,128)(2,1)S(1)}, bf16[2,64,1024]{2,1,0:T(8,128)(2,1)S(1)}, u32[]{:S(2)}, u32[]{:S(2)}) collective-permute-start(bf16[2,64,1024]{2,1,0:T(8,128)(2,1)S(1)} %fusion.1), channel_id=1, source_target_pairs={{0,16},{4,20},{8,24},{12,28},{16,0},{20,4},{24,8},{28,12},{1,17},{... | collective-permute-start | bytes 786440 | tf_op jit(solution)/shard_map/ppermute | solution.py:444
  145.7 9.5 %weight_grads.1 = (f32[1024,1792]{1,0:T(8,128)}, f32[1024,1792]{1,0:T(8,128)}, f32[1792,1024]{1,0:T(8,128)}) custom-call(s32[3]{0:T(128)S(1)} %pad_add_fusion.1.where_ref, bf16[2,64,1024]{2,1,0:T(8,128)(2,1)S(1)} %pad_maximum_fusion.pair.refs_0_, bf16[2,64,1024]{2,1,0:T(8,128)(2,1)S(1)} %collective-permute-done.8.refs_0_.refs_1_, ...), custom_call_target="tpu_custom_call" | custom-call | flops 5637144576 | bytes 29622272 | tf_op jit(solution)/shard_map/weight_grads/pallas_call | solution.py:400
  155.2 4.5 %collective-permute-done.25.refs_2_ = bf16[2,64,1024]{2,1,0:T(8,128)(2,1)S(1)} collective-permute-done((bf16[2,64,1024]{2,1,0:T(8,128)(2,1)S(1)}, bf16[2,64,1024]{2,1,0:T(8,128)(2,1)S(1)}, u32[]{:S(2)}, u32[]{:S(2)}) %collective-permute-start.25) | collective-permute-done | bytes 262176 | tf_op jit(solution)/shard_map/ppermute | solution.py:444
  159.6 1.3 finish.1
  (31 shorter events, 0.5 us)
Async XLA Ops:
  1.6 24.4 %collective-permute-start.19 = (bf16[2,64,1024]{2,1,0:T(8,128)(2,1)S(1)}, bf16[2,64,1024]{2,1,0:T(8,128)(2,1)S(1)}, u32[]{:S(2)}, u32[]{:S(2)}) collective-permute-start(bf16[2,64,1024]{2,1,0:T(8,128)(2,1)S(1)} %pad_maximum_fusion.pair.refs_0_), channel_id=1, source_target_pairs={{0,16},{4,20},{8,24},{12,28},{16,0},{20,4},{24,8},{28,12},{1,17},{... | collective-permute-start | bytes 786440 | tf_op jit(solution)/shard_map/ppermute | solution.py:444
  5.8 20.8 %collective-permute-start.9 = (bf16[2,64,1024]{2,1,0:T(8,128)(2,1)S(1)}, bf16[2,64,1024]{2,1,0:T(8,128)(2,1)S(1)}, u32[]{:S(2)}, u32[]{:S(2)}) collective-permute-start(bf16[2,64,1024]{2,1,0:T(8,128)(2,1)S(1)} %pad_maximum_fusion.pair.refs_0_), channel_id=1, source_target_pairs={{0,24},{4,28},{8,0},{12,4},{16,8},{20,12},{24,16},{28,20},{1,25},{... | collective-permute-start | bytes 786440 | tf_op jit(solution)/shard_map/ppermute | solution.py:444
  7.1 17.4 %collective-permute-start.8 = (bf16[2,64,1024]{2,1,0:T(8,128)(2,1)S(1)}, bf16[2,64,1024]{2,1,0:T(8,128)(2,1)S(1)}, u32[]{:S(2)}, u32[]{:S(2)}) collective-permute-start(bf16[2,64,1024]{2,1,0:T(8,128)(2,1)S(1)} %pad_maximum_fusion.pair.refs_0_), channel_id=1, source_target_pairs={{0,8},{4,12},{8,16},{12,20},{16,24},{20,28},{24,0},{28,4},{1,9},{5... | collective-permute-start | bytes 786440 | tf_op jit(solution)/shard_map/ppermute | solution.py:444
  14.6 35.0 %collective-permute-start = (f32[3,32,1792]{2,1,0:T(8,128)S(1)}, f32[3,32,1792]{2,1,0:T(8,128)S(1)}, u32[]{:S(2)}, u32[]{:S(2)}) collective-permute-start(f32[3,32,1792]{2,1,0:T(8,128)S(1)} %get-tuple-element.37), channel_id=1, source_target_pairs={{0,1},{1,0},{2,3},{3,2},{4,5},{5,4},{6,7},{7,6},{8,9},{9,8},{10,11... | collective-permute-start | bytes 2064392 | tf_op jit(solution)/shard_map/ppermute | solution.py:456
  14.7 16.2 %collective-permute-start.3 = (bf16[2,64,1024]{2,1,0:T(8,128)(2,1)S(1)}, bf16[2,64,1024]{2,1,0:T(8,128)(2,1)S(1)}, u32[]{:S(2)}, u32[]{:S(2)}) collective-permute-start(bf16[2,64,1024]{2,1,0:T(8,128)(2,1)S(1)} %pad_maximum_fusion.pair.refs_0_), channel_id=1, source_target_pairs={{0,4},{4,0},{8,12},{12,8},{16,20},{20,16},{24,28},{28,24},{1,5},{5... | collective-permute-start | bytes 786440 | tf_op jit(solution)/shard_map/ppermute | solution.py:448
  24.5 9.5 %collective-permute-start.26 = (bf16[2,64,1024]{2,1,0:T(8,128)(2,1)S(1)}, bf16[2,64,1024]{2,1,0:T(8,128)(2,1)S(1)}, u32[]{:S(2)}, u32[]{:S(2)}) collective-permute-start(bf16[2,64,1024]{2,1,0:T(8,128)(2,1)S(1)} %collective-permute-done.8.refs_0_.refs_1_), channel_id=1, source_target_pairs={{0,4},{4,0},{8,12},{12,8},{16,20},{20,16},{24,28},{28,24},{1,5},{5... | collective-permute-start | bytes 786440 | tf_op jit(solution)/shard_map/ppermute | solution.py:448
  26.0 20.0 %collective-permute-start.20 = (bf16[2,64,1024]{2,1,0:T(8,128)(2,1)S(1)}, bf16[2,64,1024]{2,1,0:T(8,128)(2,1)S(1)}, u32[]{:S(2)}, u32[]{:S(2)}) collective-permute-start(bf16[2,64,1024]{2,1,0:T(8,128)(2,1)S(1)} %collective-permute-done.19.refs_0_.refs_4_), channel_id=1, source_target_pairs={{0,4},{4,0},{8,12},{12,8},{16,20},{20,16},{24,28},{28,24},{1,5},{5... | collective-permute-start | bytes 786440 | tf_op jit(solution)/shard_map/ppermute | solution.py:448
  26.5 16.4 %collective-permute-start.13 = (bf16[2,64,1024]{2,1,0:T(8,128)(2,1)S(1)}, bf16[2,64,1024]{2,1,0:T(8,128)(2,1)S(1)}, u32[]{:S(2)}, u32[]{:S(2)}) collective-permute-start(bf16[2,64,1024]{2,1,0:T(8,128)(2,1)S(1)} %collective-permute-done.9.refs_1_.refs_2_), channel_id=1, source_target_pairs={{0,4},{4,0},{8,12},{12,8},{16,20},{20,16},{24,28},{28,24},{1,5},{5... | collective-permute-start | bytes 786440 | tf_op jit(solution)/shard_map/ppermute | solution.py:448
  30.9 31.1 %collective-permute-start.10 = (f32[3,64,1792]{2,1,0:T(8,128)S(1)}, f32[3,64,1792]{2,1,0:T(8,128)S(1)}, u32[]{:S(2)}, u32[]{:S(2)}) collective-permute-start(f32[3,64,1792]{2,1,0:T(8,128)S(1)} %get-tuple-element.46), channel_id=1, source_target_pairs={{0,1},{1,0},{2,3},{3,2},{4,5},{5,4},{6,7},{7,6},{8,9},{9,8},{10,11... | collective-permute-start | bytes 4128776 | tf_op jit(solution)/shard_map/ppermute | solution.py:456
  34.0 15.7 %collective-permute-start.4 = (f32[3,32,1792]{2,1,0:T(8,128)S(1)}, f32[3,32,1792]{2,1,0:T(8,128)S(1)}, u32[]{:S(2)}, u32[]{:S(2)}) collective-permute-start(f32[3,32,1792]{2,1,0:T(8,128)S(1)} %get-tuple-element.42), channel_id=1, source_target_pairs={{0,1},{1,0},{2,3},{3,2},{4,5},{5,4},{6,7},{7,6},{8,9},{9,8},{10,11... | collective-permute-start | bytes 2064392 | tf_op jit(solution)/shard_map/ppermute | solution.py:456
  42.9 19.3 %collective-permute-start.27 = (f32[3,32,1792]{2,1,0:T(8,128)S(1)}, f32[3,32,1792]{2,1,0:T(8,128)S(1)}, u32[]{:S(2)}, u32[]{:S(2)}) collective-permute-start(f32[3,32,1792]{2,1,0:T(8,128)S(1)} %get-tuple-element.56), channel_id=1, source_target_pairs={{0,1},{1,0},{2,3},{3,2},{4,5},{5,4},{6,7},{7,6},{8,9},{9,8},{10,11... | collective-permute-start | bytes 2064392 | tf_op jit(solution)/shard_map/ppermute | solution.py:456
  46.0 41.9 %collective-permute-start.14 = (f32[3,32,1792]{2,1,0:T(8,128)S(1)}, f32[3,32,1792]{2,1,0:T(8,128)S(1)}, u32[]{:S(2)}, u32[]{:S(2)}) collective-permute-start(f32[3,32,1792]{2,1,0:T(8,128)S(1)} %get-tuple-element.48), channel_id=1, source_target_pairs={{0,1},{1,0},{2,3},{3,2},{4,5},{5,4},{6,7},{7,6},{8,9},{9,8},{10,11... | collective-permute-start | bytes 2064392 | tf_op jit(solution)/shard_map/ppermute | solution.py:456
  49.6 23.3 %collective-permute-start.21 = (f32[3,64,1792]{2,1,0:T(8,128)S(1)}, f32[3,64,1792]{2,1,0:T(8,128)S(1)}, u32[]{:S(2)}, u32[]{:S(2)}) collective-permute-start(f32[3,64,1792]{2,1,0:T(8,128)S(1)} %get-tuple-element.52), channel_id=1, source_target_pairs={{0,1},{1,0},{2,3},{3,2},{4,5},{5,4},{6,7},{7,6},{8,9},{9,8},{10,11... | collective-permute-start | bytes 4128776 | tf_op jit(solution)/shard_map/ppermute | solution.py:456
  49.7 10.5 %collective-permute-start.1 = (bf16[3,32,1792]{2,1,0:T(8,128)(2,1)S(1)}, bf16[3,32,1792]{2,1,0:T(8,128)(2,1)S(1)}, u32[]{:S(2)}, u32[]{:S(2)}) collective-permute-start(bf16[3,32,1792]{2,1,0:T(8,128)(2,1)S(1)} %add_convert_fusion.5), channel_id=1, source_target_pairs={{0,2},{1,3},{2,0},{3,1},{4,6},{5,7},{6,4},{7,5},{8,10},{9,11},{10,... | collective-permute-start | bytes 1032200 | tf_op jit(solution)/shard_map/ppermute | solution.py:452
  60.2 10.9 %collective-permute-start.5 = (bf16[3,32,1792]{2,1,0:T(8,128)(2,1)S(1)}, bf16[3,32,1792]{2,1,0:T(8,128)(2,1)S(1)}, u32[]{:S(2)}, u32[]{:S(2)}) collective-permute-start(bf16[3,32,1792]{2,1,0:T(8,128)(2,1)S(1)} %add_convert_fusion.4), channel_id=1, source_target_pairs={{0,2},{1,3},{2,0},{3,1},{4,6},{5,7},{6,4},{7,5},{8,10},{9,11},{10,... | collective-permute-start | bytes 1032200 | tf_op jit(solution)/shard_map/ppermute | solution.py:452
  62.0 26.0 %collective-permute-start.2 = (bf16[3,32,1792]{2,1,0:T(8,128)(2,1)S(1)}, bf16[3,32,1792]{2,1,0:T(8,128)(2,1)S(1)}, u32[]{:S(2)}, u32[]{:S(2)}) collective-permute-start(bf16[3,32,1792]{2,1,0:T(8,128)(2,1)S(1)} %activate.6.refs_0_.refs_8_), channel_id=1, source_target_pairs={{0,1},{1,0},{2,3},{3,2},{4,5},{5,4},{6,7},{7,6},{8,9},{9,8},{10,11... | collective-permute-start | bytes 1032200 | tf_op jit(solution)/shard_map/ppermute | solution.py:456
  62.2 23.7 %collective-permute-start.11 = (bf16[3,64,1792]{2,1,0:T(8,128)(2,1)S(1)}, bf16[3,64,1792]{2,1,0:T(8,128)(2,1)S(1)}, u32[]{:S(2)}, u32[]{:S(2)}) collective-permute-start(bf16[3,64,1792]{2,1,0:T(8,128)(2,1)S(1)} %add_convert_fusion.1), channel_id=1, source_target_pairs={{0,2},{1,3},{2,0},{3,1},{4,6},{5,7},{6,4},{7,5},{8,10},{9,11},{10,... | collective-permute-start | bytes 2064392 | tf_op jit(solution)/shard_map/ppermute | solution.py:452
  71.2 37.4 %collective-permute-start.28 = (bf16[3,32,1792]{2,1,0:T(8,128)(2,1)S(1)}, bf16[3,32,1792]{2,1,0:T(8,128)(2,1)S(1)}, u32[]{:S(2)}, u32[]{:S(2)}) collective-permute-start(bf16[3,32,1792]{2,1,0:T(8,128)(2,1)S(1)} %add_convert_fusion.2), channel_id=1, source_target_pairs={{0,2},{1,3},{2,0},{3,1},{4,6},{5,7},{6,4},{7,5},{8,10},{9,11},{10,... | collective-permute-start | bytes 1032200 | tf_op jit(solution)/shard_map/ppermute | solution.py:452
  72.9 15.7 %collective-permute-start.6 = (bf16[3,32,1792]{2,1,0:T(8,128)(2,1)S(1)}, bf16[3,32,1792]{2,1,0:T(8,128)(2,1)S(1)}, u32[]{:S(2)}, u32[]{:S(2)}) collective-permute-start(bf16[3,32,1792]{2,1,0:T(8,128)(2,1)S(1)} %activate.7.refs_2_.refs_18_), channel_id=1, source_target_pairs={{0,1},{1,0},{2,3},{3,2},{4,5},{5,4},{6,7},{7,6},{8,9},{9,8},{10,11... | collective-permute-start | bytes 1032200 | tf_op jit(solution)/shard_map/ppermute | solution.py:456
  85.9 22.1 %collective-permute-start.22 = (bf16[3,64,1792]{2,1,0:T(8,128)(2,1)S(1)}, bf16[3,64,1792]{2,1,0:T(8,128)(2,1)S(1)}, u32[]{:S(2)}, u32[]{:S(2)}) collective-permute-start(bf16[3,64,1792]{2,1,0:T(8,128)(2,1)S(1)} %add_convert_fusion), channel_id=1, source_target_pairs={{0,2},{1,3},{2,0},{3,1},{4,6},{5,7},{6,4},{7,5},{8,10},{9,11},{10,... | collective-permute-start | bytes 2064392 | tf_op jit(solution)/shard_map/ppermute | solution.py:452
  87.9 26.6 %collective-permute-start.12 = (bf16[3,64,1792]{2,1,0:T(8,128)(2,1)S(1)}, bf16[3,64,1792]{2,1,0:T(8,128)(2,1)S(1)}, u32[]{:S(2)}, u32[]{:S(2)}) collective-permute-start(bf16[3,64,1792]{2,1,0:T(8,128)(2,1)S(1)} %activate.8.refs_0_.refs_10_), channel_id=1, source_target_pairs={{0,1},{1,0},{2,3},{3,2},{4,5},{5,4},{6,7},{7,6},{8,9},{9,8},{10,11... | collective-permute-start | bytes 2064392 | tf_op jit(solution)/shard_map/ppermute | solution.py:456
  88.0 26.1 %collective-permute-start.15 = (bf16[3,32,1792]{2,1,0:T(8,128)(2,1)S(1)}, bf16[3,32,1792]{2,1,0:T(8,128)(2,1)S(1)}, u32[]{:S(2)}, u32[]{:S(2)}) collective-permute-start(bf16[3,32,1792]{2,1,0:T(8,128)(2,1)S(1)} %add_convert_fusion.3), channel_id=1, source_target_pairs={{0,2},{1,3},{2,0},{3,1},{4,6},{5,7},{6,4},{7,5},{8,10},{9,11},{10,... | collective-permute-start | bytes 1032200 | tf_op jit(solution)/shard_map/ppermute | solution.py:452
  91.6 22.8 %collective-permute-start.7 = (bf16[1,2,64,1024]{3,2,1,0:T(8,128)(2,1)S(1)}, bf16[1,2,64,1024]{3,2,1,0:T(8,128)(2,1)S(1)}, u32[]{:S(2)}, u32[]{:S(2)}) collective-permute-start(bf16[1,2,64,1024]{3,2,1,0:T(8,128)(2,1)S(1)} %get-tuple-element.44), channel_id=1, source_target_pairs={{0,4},{4,0},{8,12},{12,8},{16,20},{20,16},{24,28},{28,24},{1,5},{5... | collective-permute-start | bytes 786440 | tf_op jit(solution)/shard_map/ppermute | solution.py:448
  108.5 14.1 %collective-permute-start.23 = (bf16[3,64,1792]{2,1,0:T(8,128)(2,1)S(1)}, bf16[3,64,1792]{2,1,0:T(8,128)(2,1)S(1)}, u32[]{:S(2)}, u32[]{:S(2)}) collective-permute-start(bf16[3,64,1792]{2,1,0:T(8,128)(2,1)S(1)} %activate.10.refs_0_.refs_14_), channel_id=1, source_target_pairs={{0,1},{1,0},{2,3},{3,2},{4,5},{5,4},{6,7},{7,6},{8,9},{9,8},{10,11... | collective-permute-start | bytes 2064392 | tf_op jit(solution)/shard_map/ppermute | solution.py:456
  108.7 5.7 %collective-permute-start.29 = (bf16[3,32,1792]{2,1,0:T(8,128)(2,1)S(1)}, bf16[3,32,1792]{2,1,0:T(8,128)(2,1)S(1)}, u32[]{:S(2)}, u32[]{:S(2)}) collective-permute-start(bf16[3,32,1792]{2,1,0:T(8,128)(2,1)S(1)} %activate.11.refs_2_.refs_12_), channel_id=1, source_target_pairs={{0,1},{1,0},{2,3},{3,2},{4,5},{5,4},{6,7},{7,6},{8,9},{9,8},{10,11... | collective-permute-start | bytes 1032200 | tf_op jit(solution)/shard_map/ppermute | solution.py:456
  114.3 4.7 %collective-permute-start.16 = (bf16[3,32,1792]{2,1,0:T(8,128)(2,1)S(1)}, bf16[3,32,1792]{2,1,0:T(8,128)(2,1)S(1)}, u32[]{:S(2)}, u32[]{:S(2)}) collective-permute-start(bf16[3,32,1792]{2,1,0:T(8,128)(2,1)S(1)} %activate.9.refs_2_.refs_16_), channel_id=1, source_target_pairs={{0,1},{1,0},{2,3},{3,2},{4,5},{5,4},{6,7},{7,6},{8,9},{9,8},{10,11... | collective-permute-start | bytes 1032200 | tf_op jit(solution)/shard_map/ppermute | solution.py:456
  117.4 9.8 %collective-permute-start.30 = (bf16[1,2,64,1024]{3,2,1,0:T(8,128)(2,1)S(1)}, bf16[1,2,64,1024]{3,2,1,0:T(8,128)(2,1)S(1)}, u32[]{:S(2)}, u32[]{:S(2)}) collective-permute-start(bf16[1,2,64,1024]{3,2,1,0:T(8,128)(2,1)S(1)} %get-tuple-element.58), channel_id=1, source_target_pairs={{0,4},{4,0},{8,12},{12,8},{16,20},{20,16},{24,28},{28,24},{1,5},{5... | collective-permute-start | bytes 786440 | tf_op jit(solution)/shard_map/ppermute | solution.py:448
  121.9 10.4 %collective-permute-start.17 = (bf16[1,2,64,1024]{3,2,1,0:T(8,128)(2,1)S(1)}, bf16[1,2,64,1024]{3,2,1,0:T(8,128)(2,1)S(1)}, u32[]{:S(2)}, u32[]{:S(2)}) collective-permute-start(bf16[1,2,64,1024]{3,2,1,0:T(8,128)(2,1)S(1)} %get-tuple-element.50), channel_id=1, source_target_pairs={{0,4},{4,0},{8,12},{12,8},{16,20},{20,16},{24,28},{28,24},{1,5},{5... | collective-permute-start | bytes 786440 | tf_op jit(solution)/shard_map/ppermute | solution.py:448
  125.7 12.9 %collective-permute-start.24 = (bf16[1,2,64,1024]{3,2,1,0:T(8,128)(2,1)S(1)}, bf16[1,2,64,1024]{3,2,1,0:T(8,128)(2,1)S(1)}, u32[]{:S(2)}, u32[]{:S(2)}) collective-permute-start(bf16[1,2,64,1024]{3,2,1,0:T(8,128)(2,1)S(1)} %get-tuple-element.54), channel_id=1, source_target_pairs={{0,4},{4,0},{8,12},{12,8},{16,20},{20,16},{24,28},{28,24},{1,5},{5... | collective-permute-start | bytes 786440 | tf_op jit(solution)/shard_map/ppermute | solution.py:448
  127.3 27.8 %collective-permute-start.31 = (bf16[2,64,1024]{2,1,0:T(8,128)(2,1)S(1)}, bf16[2,64,1024]{2,1,0:T(8,128)(2,1)S(1)}, u32[]{:S(2)}, u32[]{:S(2)}) collective-permute-start(bf16[2,64,1024]{2,1,0:T(8,128)(2,1)S(1)} %fusion.2), channel_id=1, source_target_pairs={{0,24},{4,28},{8,0},{12,4},{16,8},{20,12},{24,16},{28,20},{1,25},{... | collective-permute-start | bytes 786440 | tf_op jit(solution)/shard_map/ppermute | solution.py:444
  132.3 22.8 %collective-permute-start.18 = (bf16[2,64,1024]{2,1,0:T(8,128)(2,1)S(1)}, bf16[2,64,1024]{2,1,0:T(8,128)(2,1)S(1)}, u32[]{:S(2)}, u32[]{:S(2)}) collective-permute-start(bf16[2,64,1024]{2,1,0:T(8,128)(2,1)S(1)} %fusion), channel_id=1, source_target_pairs={{0,8},{4,12},{8,16},{12,20},{16,24},{20,28},{24,0},{28,4},{1,9},{5... | collective-permute-start | bytes 786440 | tf_op jit(solution)/shard_map/ppermute | solution.py:444
  138.7 21.0 %collective-permute-start.25 = (bf16[2,64,1024]{2,1,0:T(8,128)(2,1)S(1)}, bf16[2,64,1024]{2,1,0:T(8,128)(2,1)S(1)}, u32[]{:S(2)}, u32[]{:S(2)}) collective-permute-start(bf16[2,64,1024]{2,1,0:T(8,128)(2,1)S(1)} %fusion.1), channel_id=1, source_target_pairs={{0,16},{4,20},{8,24},{12,28},{16,0},{20,4},{24,8},{28,12},{1,17},{... | collective-permute-start | bytes 786440 | tf_op jit(solution)/shard_map/ppermute | solution.py:444

commit v4 on v3

--- a/solution.py
+++ b/solution.py
@@ -173,7 +173,7 @@
     )(where, shard, masks, *weights)
 
 
-def partials(where, shards, weights):
+def partials(where, shards, weights, travels):
     n = len(shards)
     _, rows, feats = shards[0].shape
     half = rows // 2
@@ -203,11 +203,11 @@
             )
             for k, out in enumerate(outs):
                 keep_ref[k, :, part] = out[:own]
-                send_ref[k, :, part] = out[own:]
+                send_ref[k, :, part] = out[own:].astype(travels)
 
         for_steps(steps, step, True)
 
-    out_shape = [jax.ShapeDtypeStruct((3, own, units), F32)] * 2
+    out_shape = [jax.ShapeDtypeStruct((3, own, units), d) for d in (F32, travels)]
     return pl.pallas_call(
         body,
         in_specs=[SMEM] + [VMEM] * (n + 3),
@@ -254,7 +254,7 @@
         far_refs, out_ref = refs[2:-1], refs[-1]
 
         def total(k):
-            value = keep_ref[k] + near_ref[k]
+            value = keep_ref[k] + near_ref[k].astype(F32)
             for ref in far_refs:
                 value = value + ref[k].astype(F32)
             return value
@@ -329,23 +329,14 @@
     )(*pieces, *weights)
 
 
-def weight_grads(where, groups, parts, keeps):
-    flat = [s for g in groups for s in g]
-    pieces = [a for pair in parts for a in pair]
-    n, m = len(flat), len(pieces)
-    _, rows, feats = flat[0].shape
+def gather_rows(where, groups):
+    shards = [s for g in groups for s in g]
+    _, rows, feats = shards[0].shape
     half = rows // 2
-    units = pieces[0].shape[2]
-    tokens = n * rows
-    tile, steps, at = tiles(units)
+    tokens = len(shards) * rows
 
     def body(where_ref, *refs):
-        shards = list(refs[:n])
-        core = where_ref[2]
-        piece_refs = refs[n : n + m]
-        kg, ku, kd = refs[n + m : n + m + 3]
-        grads = refs[n + m + 3 : n + m + 6]
-        lhs, turned, rhs, gate_buf, up_buf, down_buf, sems = refs[n + m + 6 :]
+        pairs, (turned, rhs), lhs = refs[:-3], refs[-3:-1], refs[-1]
 
         def store(second, side):
             row, shard = 0, 0
@@ -353,13 +344,42 @@
                 size = len(group) * half
                 for i in range(len(group)):
                     at_row = pl.ds(row + second * size + i * half, half)
-                    lhs[at_row, :] = shards[shard + i][0, pl.ds(side * half, half), :]
-                    rhs[at_row, :] = shards[shard + i][1, pl.ds(side * half, half), :]
+                    lhs[at_row, :] = pairs[shard + i][0, pl.ds(side * half, half), :]
+                    rhs[at_row, :] = pairs[shard + i][1, pl.ds(side * half, half), :]
                 row += 2 * size
                 shard += len(group)
 
-        split_halves(core, store)
+        split_halves(where_ref[2], store)
         turned[...] = lhs[...].T
+
+    out_shape = [
+        jax.ShapeDtypeStruct((feats, tokens), BF16),
+        jax.ShapeDtypeStruct((tokens, feats), BF16),
+    ]
+    return pl.pallas_call(
+        body,
+        in_specs=[SMEM] + [VMEM] * len(shards),
+        out_specs=[VMEM] * 2,
+        out_shape=out_shape,
+        scratch_shapes=[pltpu.VMEM((tokens, feats), BF16)],
+        cost_estimate=cost(0, *shards, *out_shape),
+        compiler_params=params(8),
+        name="gather_rows",
+    )(where, *shards)
+
+
+def weight_grads(turned, rhs, parts, keeps):
+    pieces = [a for pair in parts for a in pair]
+    m = len(pieces)
+    feats, tokens = turned.shape
+    units = pieces[0].shape[2]
+    tile, steps, at = tiles(units)
+
+    def body(turned_ref, rhs_ref, *refs):
+        piece_refs = refs[:m]
+        kg, ku, kd = refs[m : m + 3]
+        grads = refs[m + 3 : m + 6]
+        gate_buf, up_buf, down_buf, sems = refs[m + 6 :]
 
         def copies(j):
             part = at(j)
@@ -379,11 +399,13 @@
             pre = [
                 jnp.concatenate([p[k, :, part] for p in piece_refs], axis=0) for k in range(3)
             ]
-            for buf, right, mask in ((gate_buf, pre[1], kg), (up_buf, pre[2], ku)):
-                buf[j] = keep_rows(dot_nn(turned[...], right), mask[:, part])
-            down_buf[j] = keep_columns(dot_tn(pre[0], rhs[...]), kd[part, :])
-            for copy in copies(j):
-                copy.start()
+            gate_copy, up_copy, down_copy = copies(j)
+            gate_buf[j] = keep_rows(dot_nn(turned_ref[...], pre[1]), kg[:, part])
+            gate_copy.start()
+            up_buf[j] = keep_rows(dot_nn(turned_ref[...], pre[2]), ku[:, part])
+            up_copy.start()
+            down_buf[j] = keep_columns(dot_tn(pre[0], rhs_ref[...]), kd[part, :])
+            down_copy.start()
 
         def finish(j):
             for copy in copies(j):
@@ -399,22 +421,19 @@
     ]
     return pl.pallas_call(
         body,
-        in_specs=[SMEM] + [VMEM] * (n + m + 3),
+        in_specs=[VMEM] * (m + 5),
         out_specs=[HBM] * 3,
         out_shape=out_shape,
         scratch_shapes=[
-            pltpu.VMEM((tokens, feats), BF16),
-            pltpu.VMEM((feats, tokens), BF16),
-            pltpu.VMEM((tokens, feats), BF16),
             pltpu.VMEM((steps, feats, tile), F32),
             pltpu.VMEM((steps, feats, tile), F32),
             pltpu.VMEM((steps, tile, feats), F32),
             pltpu.SemaphoreType.DMA((3, steps)),
         ],
-        cost_estimate=cost(6 * tokens * feats * units, *flat, *pieces, *out_shape),
+        cost_estimate=cost(6 * tokens * feats * units, turned, rhs, *pieces, *out_shape),
         compiler_params=params(32),
         name="weight_grads",
-    )(where, *flat, *pieces, *keeps)
+    )(turned, rhs, *pieces, *keeps)
 
 
 def per_device(
@@ -461,11 +480,11 @@
 
     far_z = [d for k in range(1, zs // 2 + 1) for d in dict.fromkeys((k, zs - k))]
     held = {(0, 0): pair}
-    for dz in far_z:
+    for k, dz in enumerate(far_z):
         held[dz, 0] = shift_z(pair, dz)
     for dx in range(1, xs):
         held[0, dx] = shift_x(pair, dx)
-    for dz in far_z:
+    for k, dz in enumerate(far_z):
         for dx in range(1, xs):
             held[dz, dx] = shift_x(held[dz, 0], dx)
 
@@ -493,7 +512,7 @@
             keep, send, *rest = first_partials(where, *shards, weights, masks)
             weights, keeps = rest[:3], rest[3:]
         else:
-            keep, send = partials(where, shards, weights)
+            keep, send = partials(where, shards, weights, BF16 if name == "a" else F32)
         near = swap_core(send)
         out = (keep + near).astype(BF16)
         far = [shift_y(out, by) for by in range(1, ys)]
@@ -513,20 +532,17 @@
             [len(group)] * xs,
             weights,
         )
-        sums = outs[0]
+        sums = [outs[0]]
         for dx in far_x:
-            sums = sums + shift_x(outs[dx], -dx)
+            sums.append(shift_x(outs[dx], -dx))
         for k, dz in enumerate(group):
-            value = sums[k]
-            if dz:
-                value = shift_z(value.astype(BF16), -dz)
-            terms.append(value)
-    grads = weight_grads(
-        where,
-        [[held[s] for s in chunk] for chunk in chunks.values()],
-        [parts[name] for name in chunks],
-        keeps,
-    )
+            if not dz:
+                terms.extend(value[k] for value in sums[::-1])
+                continue
+            value = sum(value[k].astype(F32) for value in sums)
+            terms.append(shift_z(value.astype(BF16), -dz))
+    turned, rhs = gather_rows(where, [[held[s] for s in chunk] for chunk in chunks.values()])
+    grads = weight_grads(turned, rhs, [parts[name] for name in chunks], keeps)
     return (*finish(where, terms[::-1]), *grads)
 
 

time: 161 us -> 153 us (0.950)
  starting transfers between devices: 40 us -> 28.8 us
  waiting for transfers between devices: 72.2 us -> 75.3 us
    ppermute x6, starting transfers between devices: 20.1 us -> 9.12 us  [shift_z(): return lax.ppermute(value, 'row', pairs)]
    ppermute x6, waiting for transfers between devices: 12.8 us -> 15.2 us  [shift_z(): return lax.ppermute(value, 'row', pairs)]
    pallas_call x1 -> x2, Pallas kernels: 9.46 us -> 9.72 us  [the longest x1 8.5 us: weight_grads(): pl.pallas_call(body, in_specs=[VMEM] * (m + 5), out_specs=[HBM] * 3, out_...]
  transfers between devices with their start and end apart: 32 -> 32, of which waited for: 9 -> 9; matrix products, arithmetic and copies ran while one was open for 1% -> 1% of each run, Pallas kernels for 27% -> 29%
where the time goes in v4:
time: 153 us
  waiting for transfers between devices  75.3 us (49%)
  Pallas kernels  45.4 us (30%)
  starting transfers between devices  28.8 us (19%)
  other arithmetic  2.5 us (2%)
    ppermute x6, waiting for transfers between devices, shift_y(): return lax.ppermute(value, 'col', pairs)  51 us
    ppermute x6, waiting for transfers between devices, shift_z(): return lax.ppermute(value, 'row', pairs)  15.2 us
    pallas_call x5, Pallas kernels, partials(): pl.pallas_call(body, in_specs=[SMEM] + [VMEM] * (n + 3), out_specs=[VMEM]...  14.9 us
    pallas_call x4, Pallas kernels, products(): pl.pallas_call(body, in_specs=[VMEM] * (n + 3), out_specs=[VMEM] * outs_n...  11.8 us
    ppermute x6, starting transfers between devices, shift_z(): return lax.ppermute(value, 'row', pairs)  9.12 us
    ppermute x8, starting transfers between devices, shift_x(): return lax.ppermute(value, 'row', pairs)  9.08 us
    ppermute x8, waiting for transfers between devices, shift_x(): return lax.ppermute(value, 'row', pairs)  8.97 us
    pallas_call x1, Pallas kernels, weight_grads(): pl.pallas_call(body, in_specs=[VMEM] * (m + 5), out_specs=[HBM] * 3, out_...  8.5 us
  transfers between devices with their start and end apart: 32, of which 9 were waited for; matrix products, arithmetic and copies ran while one was open for 1% of the time, Pallas kernels for 29%

profile of v4, /device:TPU:0, one launch (start us, length us, event | category | flops | bytes accessed | tf_op | source)
XLA Modules:
  0.0 153.0 jit_solution(16675340159758242157)
XLA Ops:
  0.6 1.0 pad_maximum_fusion.pair.refs_0_
  1.6 5.1 %collective-permute-start.9 = (bf16[2,64,1024]{2,1,0:T(8,128)(2,1)S(1)}, bf16[2,64,1024]{2,1,0:T(8,128)(2,1)S(1)}, u32[]{:S(2)}, u32[]{:S(2)}) collective-permute-start(bf16[2,64,1024]{2,1,0:T(8,128)(2,1)S(1)} %pad_maximum_fusion.pair.refs_0_), channel_id=1, source_target_pairs={{0,24},{4,28},{8,0},{12,4},{16,8},{20,12},{24,16},{28,20},{1,25},{... | collective-permute-start | bytes 786440 | tf_op jit(solution)/shard_map/ppermute | solution.py:463
  6.8 1.5 collective-permute-start.3
  8.3 0.8 pad_add_fusion.masks_ref
  9.0 0.1 pad_add_fusion.1.where_ref
  9.1 5.9 %first_partials.1 = (f32[3,32,1792]{2,1,0:T(8,128)S(1)}, f32[3,32,1792]{2,1,0:T(8,128)S(1)}, bf16[1024,1792]{1,0:T(8,128)(2,1)S(1)}, bf16[1024,1792]{1,0:T(8,128...) custom-call(s32[3]{0:T(128)S(1)} %pad_add_fusion.1.where_ref, ...), custom_call_target="tpu_custom_call" | custom-call | flops 704643072 | bytes 23830528 | tf_op jit(solution)/shard_map/first_partials/pallas_call | solution.py:161
  15.0 0.1 collective-permute-start
  15.1 1.1 collective-permute-start.19
  16.2 2.9 %collective-permute-done.8.refs_0_.refs_1_ = bf16[2,64,1024]{2,1,0:T(8,128)(2,1)S(1)} collective-permute-done((bf16[2,64,1024]{2,1,0:T(8,128)(2,1)S(1)}, bf16[2,64,1024]{2,1,0:T(8,128)(2,1)S(1)}, u32[]{:S(2)}, u32[]{:S(2)}) %collective-permute-start.8) | collective-permute-done | bytes 262176 | tf_op jit(solution)/shard_map/ppermute | solution.py:463
  19.1 1.5 collective-permute-start.26
  20.6 0.5 collective-permute-start.13
  21.1 3.0 %partials.5 = (f32[3,32,1792]{2,1,0:T(8,128)S(1)}, f32[3,32,1792]{2,1,0:T(8,128)S(1)}) custom-call(s32[3]{0:T(128)S(1)} %pad_add_fusion.1.where_ref, bf16[2,64,1024]{2,1,0:T(8,128)(2,1)S(1)} %collective-permute-done.3.refs_0_.refs_7_, bf16[1024,1792]{1,0:T(8,128)(2,1)S(1)} %get-tuple-element.40.refs_1_.refs_4_.refs_2_, ...), custom_call_target="tpu_custom_call" | custom-call | flops 704643072 | bytes 12648448 | tf_op jit(solution)/shard_map/partials/pallas_call | solution.py:211
  24.1 0.1 collective-permute-start.4
  24.2 6.1 %collective-permute-done.19.refs_0_.refs_4_ = bf16[2,64,1024]{2,1,0:T(8,128)(2,1)S(1)} collective-permute-done((bf16[2,64,1024]{2,1,0:T(8,128)(2,1)S(1)}, bf16[2,64,1024]{2,1,0:T(8,128)(2,1)S(1)}, u32[]{:S(2)}, u32[]{:S(2)}) %collective-permute-start.19) | collective-permute-done | bytes 262176 | tf_op jit(solution)/shard_map/ppermute | solution.py:463
  30.3 1.2 collective-permute-start.20
  31.6 2.8 %partials.6 = (f32[3,64,1792]{2,1,0:T(8,128)S(1)}, bf16[3,64,1792]{2,1,0:T(8,128)(2,1)S(1)}) custom-call(s32[3]{0:T(128)S(1)} %pad_add_fusion.1.where_ref, bf16[2,64,1024]{2,1,0:T(8,128)(2,1)S(1)} %collective-permute-done.8.refs_0_.refs_1_, bf16[2,64,1024]{2,1,0:T(8,128)(2,1)S(1)} %collective-permute-done.9.refs_1_.refs_2_, ...), custom_call_target="tpu_custom_call" | custom-call | flops 1409286144 | bytes 13598720 | tf_op jit(solution)/shard_map/partials/pallas_call | solution.py:211
  34.4 0.1 collective-permute-start.10
  34.5 3.0 %partials.9 = (f32[3,32,1792]{2,1,0:T(8,128)S(1)}, f32[3,32,1792]{2,1,0:T(8,128)S(1)}) custom-call(s32[3]{0:T(128)S(1)} %pad_add_fusion.1.where_ref, bf16[2,64,1024]{2,1,0:T(8,128)(2,1)S(1)} %collective-permute-done.26.refs_0_.refs_3_, bf16[1024,1792]{1,0:T(8,128)(2,1)S(1)} %get-tuple-element.40.refs_1_.refs_4_.refs_2_, ...), custom_call_target="tpu_custom_call" | custom-call | flops 704643072 | bytes 12648448 | tf_op jit(solution)/shard_map/partials/pallas_call | solution.py:211
  37.5 0.6 collective-permute-start.27
  38.1 3.0 %partials.7 = (f32[3,32,1792]{2,1,0:T(8,128)S(1)}, f32[3,32,1792]{2,1,0:T(8,128)S(1)}) custom-call(s32[3]{0:T(128)S(1)} %pad_add_fusion.1.where_ref, bf16[2,64,1024]{2,1,0:T(8,128)(2,1)S(1)} %collective-permute-done.13.refs_0_.refs_6_, bf16[1024,1792]{1,0:T(8,128)(2,1)S(1)} %get-tuple-element.40.refs_1_.refs_4_.refs_2_, ...), custom_call_target="tpu_custom_call" | custom-call | flops 704643072 | bytes 12648448 | tf_op jit(solution)/shard_map/partials/pallas_call | solution.py:211
  41.1 0.1 collective-permute-start.14
  41.2 3.0 %partials.8 = (f32[3,64,1792]{2,1,0:T(8,128)S(1)}, f32[3,64,1792]{2,1,0:T(8,128)S(1)}) custom-call(s32[3]{0:T(128)S(1)} %pad_add_fusion.1.where_ref, bf16[2,64,1024]{2,1,0:T(8,128)(2,1)S(1)} %collective-permute-done.19.refs_0_.refs_4_, bf16[2,64,1024]{2,1,0:T(8,128)(2,1)S(1)} %collective-permute-done.20.refs_1_.refs_5_, ...), custom_call_target="tpu_custom_call" | custom-call | flops 1409286144 | bytes 14286848 | tf_op jit(solution)/shard_map/partials/pallas_call | solution.py:211
  44.2 0.5 collective-permute-start.21
  44.8 0.1 add_convert_fusion.5
  44.9 1.6 %collective-permute-start.1 = (bf16[3,32,1792]{2,1,0:T(8,128)(2,1)S(1)}, bf16[3,32,1792]{2,1,0:T(8,128)(2,1)S(1)}, u32[]{:S(2)}, u32[]{:S(2)}) collective-permute-start(bf16[3,32,1792]{2,1,0:T(8,128)(2,1)S(1)} %add_convert_fusion.5), channel_id=1, source_target_pairs={{0,2},{1,3},{2,0},{3,1},{4,6},{5,7},{6,4},{7,5},{8,10},{9,11},{10,... | collective-permute-start | bytes 1032200 | tf_op jit(solution)/shard_map/ppermute | solution.py:471
  46.4 0.1 add_convert_fusion.4
  46.5 0.6 collective-permute-start.5
  47.1 0.1 add_convert_fusion.1
  47.2 1.6 %collective-permute-start.11 = (bf16[3,64,1792]{2,1,0:T(8,128)(2,1)S(1)}, bf16[3,64,1792]{2,1,0:T(8,128)(2,1)S(1)}, u32[]{:S(2)}, u32[]{:S(2)}) collective-permute-start(bf16[3,64,1792]{2,1,0:T(8,128)(2,1)S(1)} %add_convert_fusion.1), channel_id=1, source_target_pairs={{0,2},{1,3},{2,0},{3,1},{4,6},{5,7},{6,4},{7,5},{8,10},{9,11},{10,... | collective-permute-start | bytes 2064392 | tf_op jit(solution)/shard_map/ppermute | solution.py:471
  48.8 0.1 add_convert_fusion.2
  48.9 0.6 collective-permute-start.28
  49.5 0.1 add_convert_fusion
  49.6 1.6 %collective-permute-start.22 = (bf16[3,64,1792]{2,1,0:T(8,128)(2,1)S(1)}, bf16[3,64,1792]{2,1,0:T(8,128)(2,1)S(1)}, u32[]{:S(2)}, u32[]{:S(2)}) collective-permute-start(bf16[3,64,1792]{2,1,0:T(8,128)(2,1)S(1)} %add_convert_fusion), channel_id=1, source_target_pairs={{0,2},{1,3},{2,0},{3,1},{4,6},{5,7},{6,4},{7,5},{8,10},{9,11},{10,... | collective-permute-start | bytes 2064392 | tf_op jit(solution)/shard_map/ppermute | solution.py:471
  51.3 26.7 %collective-permute-done.11.refs_2_ = bf16[3,64,1792]{2,1,0:T(8,128)(2,1)S(1)} collective-permute-done((bf16[3,64,1792]{2,1,0:T(8,128)(2,1)S(1)}, bf16[3,64,1792]{2,1,0:T(8,128)(2,1)S(1)}, u32[]{:S(2)}, u32[]{:S(2)}) %collective-permute-start.11) | collective-permute-done | bytes 688160 | tf_op jit(solution)/shard_map/ppermute | solution.py:471
  78.0 1.5 collective-permute-start.15
  79.5 0.4 activate.8.refs_0_.refs_2_
  79.9 0.1 collective-permute-start.12
  80.0 0.2 activate.6.refs_0_
  80.2 0.6 collective-permute-start.2
  80.8 0.2 activate.7.refs_2_.refs_10_
  81.0 19.1 %collective-permute-done.22.refs_2_ = bf16[3,64,1792]{2,1,0:T(8,128)(2,1)S(1)} collective-permute-done((bf16[3,64,1792]{2,1,0:T(8,128)(2,1)S(1)}, bf16[3,64,1792]{2,1,0:T(8,128)(2,1)S(1)}, u32[]{:S(2)}, u32[]{:S(2)}) %collective-permute-start.22) | collective-permute-done | bytes 688160 | tf_op jit(solution)/shard_map/ppermute | solution.py:471
  100.1 0.4 activate.10.refs_0_.refs_6_
  100.5 0.6 collective-permute-start.23
  101.1 0.2 activate.11.refs_2_.refs_4_
  101.3 5.2 %collective-permute-done.15.refs_2_ = bf16[3,32,1792]{2,1,0:T(8,128)(2,1)S(1)} collective-permute-done((bf16[3,32,1792]{2,1,0:T(8,128)(2,1)S(1)}, bf16[3,32,1792]{2,1,0:T(8,128)(2,1)S(1)}, u32[]{:S(2)}, u32[]{:S(2)}) %collective-permute-start.15) | collective-permute-done | bytes 344096 | tf_op jit(solution)/shard_map/ppermute | solution.py:471
  106.5 0.2 activate.9.refs_2_.refs_8_
  106.8 0.6 collective-permute-start.16
  107.3 1.2 gather_rows.1
  108.6 3.0 %products.4 = (f32[1,2,64,1024]{3,2,1,0:T(8,128)S(1)}, bf16[1,2,64,1024]{3,2,1,0:T(8,128)(2,1)S(1)}) custom-call(bf16[3,32,1792]{2,1,0:T(8,128)(2,1)S(1)} %activate.6.refs_0_, bf16[3,32,1792]{2,1,0:T(8,128)(2,1)S(1)} %collective-permute-done.2.refs_1_, bf16[3,32,1792]{2,1,0:T(8,128)(2,1)S(1)} %activate.7.refs_2_.refs_10_, ...), custom_call_target="tpu_custom_call" | custom-call | flops 1409286144 | bytes 13172736 | tf_op jit(solution)/shard_map/products/pallas_call | solution.py:320
  111.5 0.9 collective-permute-start.7
  112.4 2.9 %products.7 = (f32[1,2,64,1024]{3,2,1,0:T(8,128)S(1)}, bf16[1,2,64,1024]{3,2,1,0:T(8,128)(2,1)S(1)}) custom-call(bf16[3,64,1792]{2,1,0:T(8,128)(2,1)S(1)} %activate.8.refs_0_.refs_2_, bf16[3,64,1792]{2,1,0:T(8,128)(2,1)S(1)} %collective-permute-done.12.refs_1_.refs_3_, bf16[3,32,1792]{2,1,0:T(8,128)(2,1)S(1)} %activate.11.refs_2_.refs_4_, ...), custom_call_target="tpu_custom_call" | custom-call | flops 1409286144 | bytes 13860864 | tf_op jit(solution)/shard_map/products/pallas_call | solution.py:320
  115.4 1.3 collective-permute-start.30
  116.7 2.9 %products.5 = (f32[1,2,64,1024]{3,2,1,0:T(8,128)S(1)}, bf16[1,2,64,1024]{3,2,1,0:T(8,128)(2,1)S(1)}) custom-call(bf16[3,64,1792]{2,1,0:T(8,128)(2,1)S(1)} %activate.8.refs_0_.refs_2_, bf16[3,64,1792]{2,1,0:T(8,128)(2,1)S(1)} %collective-permute-done.12.refs_1_.refs_3_, bf16[3,32,1792]{2,1,0:T(8,128)(2,1)S(1)} %activate.9.refs_2_.refs_8_, ...), custom_call_target="tpu_custom_call" | custom-call | flops 1409286144 | bytes 13860864 | tf_op jit(solution)/shard_map/products/pallas_call | solution.py:320
  119.6 0.9 collective-permute-start.17
  120.5 3.0 %products.6 = (f32[1,2,64,1024]{3,2,1,0:T(8,128)S(1)}, bf16[1,2,64,1024]{3,2,1,0:T(8,128)(2,1)S(1)}) custom-call(bf16[3,64,1792]{2,1,0:T(8,128)(2,1)S(1)} %activate.10.refs_0_.refs_6_, bf16[3,64,1792]{2,1,0:T(8,128)(2,1)S(1)} %collective-permute-done.23.refs_1_.refs_7_, bf16[1024,1792]{1,0:T(8,128)(2,1)S(1)} %get-tuple-element.40.refs_1_.refs_4_.refs_2_, ...), custom_call_target="tpu_custom_call" | custom-call | flops 1409286144 | bytes 13172736 | tf_op jit(solution)/shard_map/products/pallas_call | solution.py:320
  123.5 1.3 collective-permute-start.24
  124.8 1.6 %collective-permute-done.30 = bf16[1,2,64,1024]{3,2,1,0:T(8,128)(2,1)S(1)} collective-permute-done((bf16[1,2,64,1024]{3,2,1,0:T(8,128)(2,1)S(1)}, bf16[1,2,64,1024]{3,2,1,0:T(8,128)(2,1)S(1)}, u32[]{:S(2)}, u32[]{:S(2)}) %collective-permute-start.30) | collective-permute-done | bytes 262176 | tf_op jit(solution)/shard_map/ppermute | solution.py:467
  126.5 2.8 %collective-permute-start.31 = (bf16[2,64,1024]{2,1,0:T(8,128)(2,1)S(1)}, bf16[2,64,1024]{2,1,0:T(8,128)(2,1)S(1)}, u32[]{:S(2)}, u32[]{:S(2)}) collective-permute-start(bf16[2,64,1024]{2,1,0:T(8,128)(2,1)S(1)} %fusion.2), channel_id=1, source_target_pairs={{0,24},{4,28},{8,0},{12,4},{16,8},{20,12},{24,16},{28,20},{1,25},{... | collective-permute-start | bytes 786440 | tf_op jit(solution)/shard_map/ppermute | solution.py:463
  129.3 2.8 %collective-permute-done.17 = bf16[1,2,64,1024]{3,2,1,0:T(8,128)(2,1)S(1)} collective-permute-done((bf16[1,2,64,1024]{3,2,1,0:T(8,128)(2,1)S(1)}, bf16[1,2,64,1024]{3,2,1,0:T(8,128)(2,1)S(1)}, u32[]{:S(2)}, u32[]{:S(2)}) %collective-permute-start.17) | collective-permute-done | bytes 262176 | tf_op jit(solution)/shard_map/ppermute | solution.py:467
  132.2 4.5 %collective-permute-done.24 = bf16[1,2,64,1024]{3,2,1,0:T(8,128)(2,1)S(1)} collective-permute-done((bf16[1,2,64,1024]{3,2,1,0:T(8,128)(2,1)S(1)}, bf16[1,2,64,1024]{3,2,1,0:T(8,128)(2,1)S(1)}, u32[]{:S(2)}, u32[]{:S(2)}) %collective-permute-start.24) | collective-permute-done | bytes 262176 | tf_op jit(solution)/shard_map/ppermute | solution.py:467
  136.8 0.1 collective-permute-start.25
  136.8 8.5 %weight_grads.1 = (f32[1024,1792]{1,0:T(8,128)}, f32[1024,1792]{1,0:T(8,128)}, f32[1792,1024]{1,0:T(8,128)}) custom-call(bf16[1024,512]{1,0:T(8,128)(2,1)S(1)} %get-tuple-element.63.turned_ref, bf16[512,1024]{1,0:T(8,128)(2,1)S(1)} %get-tuple-element.64.rhs_ref, bf16[3,32,1792]{2,1,0:T(8,128)(2,1)S(1)} %activate.6.refs_0_, ...), custom_call_target="tpu_custom_call" | custom-call | flops 5637144576 | bytes 29622272 | tf_op jit(solution)/shard_map/weight_grads/pallas_call | solution.py:422
  145.4 6.2 %collective-permute-done.25.refs_3_ = bf16[2,64,1024]{2,1,0:T(8,128)(2,1)S(1)} collective-permute-done((bf16[2,64,1024]{2,1,0:T(8,128)(2,1)S(1)}, bf16[2,64,1024]{2,1,0:T(8,128)(2,1)S(1)}, u32[]{:S(2)}, u32[]{:S(2)}) %collective-permute-start.25) | collective-permute-done | bytes 262176 | tf_op jit(solution)/shard_map/ppermute | solution.py:463
  151.6 1.4 finish.1
  (31 shorter events, 0.4 us)
Async XLA Ops:
  1.6 18.9 %collective-permute-start.9 = (bf16[2,64,1024]{2,1,0:T(8,128)(2,1)S(1)}, bf16[2,64,1024]{2,1,0:T(8,128)(2,1)S(1)}, u32[]{:S(2)}, u32[]{:S(2)}) collective-permute-start(bf16[2,64,1024]{2,1,0:T(8,128)(2,1)S(1)} %pad_maximum_fusion.pair.refs_0_), channel_id=1, source_target_pairs={{0,24},{4,28},{8,0},{12,4},{16,8},{20,12},{24,16},{28,20},{1,25},{... | collective-permute-start | bytes 786440 | tf_op jit(solution)/shard_map/ppermute | solution.py:463
  6.8 12.3 %collective-permute-start.8 = (bf16[2,64,1024]{2,1,0:T(8,128)(2,1)S(1)}, bf16[2,64,1024]{2,1,0:T(8,128)(2,1)S(1)}, u32[]{:S(2)}, u32[]{:S(2)}) collective-permute-start(bf16[2,64,1024]{2,1,0:T(8,128)(2,1)S(1)} %pad_maximum_fusion.pair.refs_0_), channel_id=1, source_target_pairs={{0,8},{4,12},{8,16},{12,20},{16,24},{20,28},{24,0},{28,4},{1,9},{5... | collective-permute-start | bytes 786440 | tf_op jit(solution)/shard_map/ppermute | solution.py:463
  6.8 14.3 %collective-permute-start.3 = (bf16[2,64,1024]{2,1,0:T(8,128)(2,1)S(1)}, bf16[2,64,1024]{2,1,0:T(8,128)(2,1)S(1)}, u32[]{:S(2)}, u32[]{:S(2)}) collective-permute-start(bf16[2,64,1024]{2,1,0:T(8,128)(2,1)S(1)} %pad_maximum_fusion.pair.refs_0_), channel_id=1, source_target_pairs={{0,4},{4,0},{8,12},{12,8},{16,20},{20,16},{24,28},{28,24},{1,5},{5... | collective-permute-start | bytes 786440 | tf_op jit(solution)/shard_map/ppermute | solution.py:467
  15.0 29.2 %collective-permute-start = (f32[3,32,1792]{2,1,0:T(8,128)S(1)}, f32[3,32,1792]{2,1,0:T(8,128)S(1)}, u32[]{:S(2)}, u32[]{:S(2)}) collective-permute-start(f32[3,32,1792]{2,1,0:T(8,128)S(1)} %get-tuple-element.39), channel_id=1, source_target_pairs={{0,1},{1,0},{2,3},{3,2},{4,5},{5,4},{6,7},{7,6},{8,9},{9,8},{10,11... | collective-permute-start | bytes 2064392 | tf_op jit(solution)/shard_map/ppermute | solution.py:475
  15.1 15.2 %collective-permute-start.19 = (bf16[2,64,1024]{2,1,0:T(8,128)(2,1)S(1)}, bf16[2,64,1024]{2,1,0:T(8,128)(2,1)S(1)}, u32[]{:S(2)}, u32[]{:S(2)}) collective-permute-start(bf16[2,64,1024]{2,1,0:T(8,128)(2,1)S(1)} %pad_maximum_fusion.pair.refs_0_), channel_id=1, source_target_pairs={{0,16},{4,20},{8,24},{12,28},{16,0},{20,4},{24,8},{28,12},{1,17},{... | collective-permute-start | bytes 786440 | tf_op jit(solution)/shard_map/ppermute | solution.py:463
  19.1 15.3 %collective-permute-start.26 = (bf16[2,64,1024]{2,1,0:T(8,128)(2,1)S(1)}, bf16[2,64,1024]{2,1,0:T(8,128)(2,1)S(1)}, u32[]{:S(2)}, u32[]{:S(2)}) collective-permute-start(bf16[2,64,1024]{2,1,0:T(8,128)(2,1)S(1)} %collective-permute-done.8.refs_0_.refs_1_), channel_id=1, source_target_pairs={{0,4},{4,0},{8,12},{12,8},{16,20},{20,16},{24,28},{28,24},{1,5},{5... | collective-permute-start | bytes 786440 | tf_op jit(solution)/shard_map/ppermute | solution.py:467
  20.6 17.0 %collective-permute-start.13 = (bf16[2,64,1024]{2,1,0:T(8,128)(2,1)S(1)}, bf16[2,64,1024]{2,1,0:T(8,128)(2,1)S(1)}, u32[]{:S(2)}, u32[]{:S(2)}) collective-permute-start(bf16[2,64,1024]{2,1,0:T(8,128)(2,1)S(1)} %collective-permute-done.9.refs_1_.refs_2_), channel_id=1, source_target_pairs={{0,4},{4,0},{8,12},{12,8},{16,20},{20,16},{24,28},{28,24},{1,5},{5... | collective-permute-start | bytes 786440 | tf_op jit(solution)/shard_map/ppermute | solution.py:467
  24.1 20.7 %collective-permute-start.4 = (f32[3,32,1792]{2,1,0:T(8,128)S(1)}, f32[3,32,1792]{2,1,0:T(8,128)S(1)}, u32[]{:S(2)}, u32[]{:S(2)}) collective-permute-start(f32[3,32,1792]{2,1,0:T(8,128)S(1)} %get-tuple-element.44), channel_id=1, source_target_pairs={{0,1},{1,0},{2,3},{3,2},{4,5},{5,4},{6,7},{7,6},{8,9},{9,8},{10,11... | collective-permute-start | bytes 2064392 | tf_op jit(solution)/shard_map/ppermute | solution.py:475
  30.3 10.8 %collective-permute-start.20 = (bf16[2,64,1024]{2,1,0:T(8,128)(2,1)S(1)}, bf16[2,64,1024]{2,1,0:T(8,128)(2,1)S(1)}, u32[]{:S(2)}, u32[]{:S(2)}) collective-permute-start(bf16[2,64,1024]{2,1,0:T(8,128)(2,1)S(1)} %collective-permute-done.19.refs_0_.refs_4_), channel_id=1, source_target_pairs={{0,4},{4,0},{8,12},{12,8},{16,20},{20,16},{24,28},{28,24},{1,5},{5... | collective-permute-start | bytes 786440 | tf_op jit(solution)/shard_map/ppermute | solution.py:467
  34.4 12.1 %collective-permute-start.10 = (bf16[3,64,1792]{2,1,0:T(8,128)(2,1)S(1)}, bf16[3,64,1792]{2,1,0:T(8,128)(2,1)S(1)}, u32[]{:S(2)}, u32[]{:S(2)}) collective-permute-start(bf16[3,64,1792]{2,1,0:T(8,128)(2,1)S(1)} %get-tuple-element.48), channel_id=1, source_target_pairs={{0,1},{1,0},{2,3},{3,2},{4,5},{5,4},{6,7},{7,6},{8,9},{9,8},{10,11... | collective-permute-start | bytes 2064392 | tf_op jit(solution)/shard_map/ppermute | solution.py:475
  37.5 9.7 %collective-permute-start.27 = (f32[3,32,1792]{2,1,0:T(8,128)S(1)}, f32[3,32,1792]{2,1,0:T(8,128)S(1)}, u32[]{:S(2)}, u32[]{:S(2)}) collective-permute-start(f32[3,32,1792]{2,1,0:T(8,128)S(1)} %get-tuple-element.58), channel_id=1, source_target_pairs={{0,1},{1,0},{2,3},{3,2},{4,5},{5,4},{6,7},{7,6},{8,9},{9,8},{10,11... | collective-permute-start | bytes 2064392 | tf_op jit(solution)/shard_map/ppermute | solution.py:475
  41.1 8.5 %collective-permute-start.14 = (f32[3,32,1792]{2,1,0:T(8,128)S(1)}, f32[3,32,1792]{2,1,0:T(8,128)S(1)}, u32[]{:S(2)}, u32[]{:S(2)}) collective-permute-start(f32[3,32,1792]{2,1,0:T(8,128)S(1)} %get-tuple-element.50), channel_id=1, source_target_pairs={{0,1},{1,0},{2,3},{3,2},{4,5},{5,4},{6,7},{7,6},{8,9},{9,8},{10,11... | collective-permute-start | bytes 2064392 | tf_op jit(solution)/shard_map/ppermute | solution.py:475
  44.2 4.6 %collective-permute-start.21 = (f32[3,64,1792]{2,1,0:T(8,128)S(1)}, f32[3,64,1792]{2,1,0:T(8,128)S(1)}, u32[]{:S(2)}, u32[]{:S(2)}) collective-permute-start(f32[3,64,1792]{2,1,0:T(8,128)S(1)} %get-tuple-element.54), channel_id=1, source_target_pairs={{0,1},{1,0},{2,3},{3,2},{4,5},{5,4},{6,7},{7,6},{8,9},{9,8},{10,11... | collective-permute-start | bytes 4128776 | tf_op jit(solution)/shard_map/ppermute | solution.py:475
  44.9 35.1 %collective-permute-start.1 = (bf16[3,32,1792]{2,1,0:T(8,128)(2,1)S(1)}, bf16[3,32,1792]{2,1,0:T(8,128)(2,1)S(1)}, u32[]{:S(2)}, u32[]{:S(2)}) collective-permute-start(bf16[3,32,1792]{2,1,0:T(8,128)(2,1)S(1)} %add_convert_fusion.5), channel_id=1, source_target_pairs={{0,2},{1,3},{2,0},{3,1},{4,6},{5,7},{6,4},{7,5},{8,10},{9,11},{10,... | collective-permute-start | bytes 1032200 | tf_op jit(solution)/shard_map/ppermute | solution.py:471
  46.5 33.7 %collective-permute-start.5 = (bf16[3,32,1792]{2,1,0:T(8,128)(2,1)S(1)}, bf16[3,32,1792]{2,1,0:T(8,128)(2,1)S(1)}, u32[]{:S(2)}, u32[]{:S(2)}) collective-permute-start(bf16[3,32,1792]{2,1,0:T(8,128)(2,1)S(1)} %add_convert_fusion.4), channel_id=1, source_target_pairs={{0,2},{1,3},{2,0},{3,1},{4,6},{5,7},{6,4},{7,5},{8,10},{9,11},{10,... | collective-permute-start | bytes 1032200 | tf_op jit(solution)/shard_map/ppermute | solution.py:471
  47.2 30.8 %collective-permute-start.11 = (bf16[3,64,1792]{2,1,0:T(8,128)(2,1)S(1)}, bf16[3,64,1792]{2,1,0:T(8,128)(2,1)S(1)}, u32[]{:S(2)}, u32[]{:S(2)}) collective-permute-start(bf16[3,64,1792]{2,1,0:T(8,128)(2,1)S(1)} %add_convert_fusion.1), channel_id=1, source_target_pairs={{0,2},{1,3},{2,0},{3,1},{4,6},{5,7},{6,4},{7,5},{8,10},{9,11},{10,... | collective-permute-start | bytes 2064392 | tf_op jit(solution)/shard_map/ppermute | solution.py:471
  48.9 51.6 %collective-permute-start.28 = (bf16[3,32,1792]{2,1,0:T(8,128)(2,1)S(1)}, bf16[3,32,1792]{2,1,0:T(8,128)(2,1)S(1)}, u32[]{:S(2)}, u32[]{:S(2)}) collective-permute-start(bf16[3,32,1792]{2,1,0:T(8,128)(2,1)S(1)} %add_convert_fusion.2), channel_id=1, source_target_pairs={{0,2},{1,3},{2,0},{3,1},{4,6},{5,7},{6,4},{7,5},{8,10},{9,11},{10,... | collective-permute-start | bytes 1032200 | tf_op jit(solution)/shard_map/ppermute | solution.py:471
  49.6 50.5 %collective-permute-start.22 = (bf16[3,64,1792]{2,1,0:T(8,128)(2,1)S(1)}, bf16[3,64,1792]{2,1,0:T(8,128)(2,1)S(1)}, u32[]{:S(2)}, u32[]{:S(2)}) collective-permute-start(bf16[3,64,1792]{2,1,0:T(8,128)(2,1)S(1)} %add_convert_fusion), channel_id=1, source_target_pairs={{0,2},{1,3},{2,0},{3,1},{4,6},{5,7},{6,4},{7,5},{8,10},{9,11},{10,... | collective-permute-start | bytes 2064392 | tf_op jit(solution)/shard_map/ppermute | solution.py:471
  78.0 28.6 %collective-permute-start.15 = (bf16[3,32,1792]{2,1,0:T(8,128)(2,1)S(1)}, bf16[3,32,1792]{2,1,0:T(8,128)(2,1)S(1)}, u32[]{:S(2)}, u32[]{:S(2)}) collective-permute-start(bf16[3,32,1792]{2,1,0:T(8,128)(2,1)S(1)} %add_convert_fusion.3), channel_id=1, source_target_pairs={{0,2},{1,3},{2,0},{3,1},{4,6},{5,7},{6,4},{7,5},{8,10},{9,11},{10,... | collective-permute-start | bytes 1032200 | tf_op jit(solution)/shard_map/ppermute | solution.py:471
  79.9 32.5 %collective-permute-start.12 = (bf16[3,64,1792]{2,1,0:T(8,128)(2,1)S(1)}, bf16[3,64,1792]{2,1,0:T(8,128)(2,1)S(1)}, u32[]{:S(2)}, u32[]{:S(2)}) collective-permute-start(bf16[3,64,1792]{2,1,0:T(8,128)(2,1)S(1)} %activate.8.refs_0_.refs_2_), channel_id=1, source_target_pairs={{0,1},{1,0},{2,3},{3,2},{4,5},{5,4},{6,7},{7,6},{8,9},{9,8},{10,11... | collective-permute-start | bytes 2064392 | tf_op jit(solution)/shard_map/ppermute | solution.py:475
  80.2 26.5 %collective-permute-start.2 = (bf16[3,32,1792]{2,1,0:T(8,128)(2,1)S(1)}, bf16[3,32,1792]{2,1,0:T(8,128)(2,1)S(1)}, u32[]{:S(2)}, u32[]{:S(2)}) collective-permute-start(bf16[3,32,1792]{2,1,0:T(8,128)(2,1)S(1)} %activate.6.refs_0_), channel_id=1, source_target_pairs={{0,1},{1,0},{2,3},{3,2},{4,5},{5,4},{6,7},{7,6},{8,9},{9,8},{10,11... | collective-permute-start | bytes 1032200 | tf_op jit(solution)/shard_map/ppermute | solution.py:475
  100.1 8.5 %collective-permute-start.6 = (bf16[3,32,1792]{2,1,0:T(8,128)(2,1)S(1)}, bf16[3,32,1792]{2,1,0:T(8,128)(2,1)S(1)}, u32[]{:S(2)}, u32[]{:S(2)}) collective-permute-start(bf16[3,32,1792]{2,1,0:T(8,128)(2,1)S(1)} %activate.7.refs_2_.refs_10_), channel_id=1, source_target_pairs={{0,1},{1,0},{2,3},{3,2},{4,5},{5,4},{6,7},{7,6},{8,9},{9,8},{10,11... | collective-permute-start | bytes 1032200 | tf_op jit(solution)/shard_map/ppermute | solution.py:475
  100.5 20.0 %collective-permute-start.23 = (bf16[3,64,1792]{2,1,0:T(8,128)(2,1)S(1)}, bf16[3,64,1792]{2,1,0:T(8,128)(2,1)S(1)}, u32[]{:S(2)}, u32[]{:S(2)}) collective-permute-start(bf16[3,64,1792]{2,1,0:T(8,128)(2,1)S(1)} %activate.10.refs_0_.refs_6_), channel_id=1, source_target_pairs={{0,1},{1,0},{2,3},{3,2},{4,5},{5,4},{6,7},{7,6},{8,9},{9,8},{10,11... | collective-permute-start | bytes 2064392 | tf_op jit(solution)/shard_map/ppermute | solution.py:475
  106.5 5.9 %collective-permute-start.29 = (bf16[3,32,1792]{2,1,0:T(8,128)(2,1)S(1)}, bf16[3,32,1792]{2,1,0:T(8,128)(2,1)S(1)}, u32[]{:S(2)}, u32[]{:S(2)}) collective-permute-start(bf16[3,32,1792]{2,1,0:T(8,128)(2,1)S(1)} %activate.11.refs_2_.refs_4_), channel_id=1, source_target_pairs={{0,1},{1,0},{2,3},{3,2},{4,5},{5,4},{6,7},{7,6},{8,9},{9,8},{10,11... | collective-permute-start | bytes 1032200 | tf_op jit(solution)/shard_map/ppermute | solution.py:475
  106.8 9.9 %collective-permute-start.16 = (bf16[3,32,1792]{2,1,0:T(8,128)(2,1)S(1)}, bf16[3,32,1792]{2,1,0:T(8,128)(2,1)S(1)}, u32[]{:S(2)}, u32[]{:S(2)}) collective-permute-start(bf16[3,32,1792]{2,1,0:T(8,128)(2,1)S(1)} %activate.9.refs_2_.refs_8_), channel_id=1, source_target_pairs={{0,1},{1,0},{2,3},{3,2},{4,5},{5,4},{6,7},{7,6},{8,9},{9,8},{10,11... | collective-permute-start | bytes 1032200 | tf_op jit(solution)/shard_map/ppermute | solution.py:475
  111.5 33.8 %collective-permute-start.7 = (bf16[1,2,64,1024]{3,2,1,0:T(8,128)(2,1)S(1)}, bf16[1,2,64,1024]{3,2,1,0:T(8,128)(2,1)S(1)}, u32[]{:S(2)}, u32[]{:S(2)}) collective-permute-start(bf16[1,2,64,1024]{3,2,1,0:T(8,128)(2,1)S(1)} %get-tuple-element.46), channel_id=1, source_target_pairs={{0,4},{4,0},{8,12},{12,8},{16,20},{20,16},{24,28},{28,24},{1,5},{5... | collective-permute-start | bytes 786440 | tf_op jit(solution)/shard_map/ppermute | solution.py:467
  115.4 11.0 %collective-permute-start.30 = (bf16[1,2,64,1024]{3,2,1,0:T(8,128)(2,1)S(1)}, bf16[1,2,64,1024]{3,2,1,0:T(8,128)(2,1)S(1)}, u32[]{:S(2)}, u32[]{:S(2)}) collective-permute-start(bf16[1,2,64,1024]{3,2,1,0:T(8,128)(2,1)S(1)} %get-tuple-element.60), channel_id=1, source_target_pairs={{0,4},{4,0},{8,12},{12,8},{16,20},{20,16},{24,28},{28,24},{1,5},{5... | collective-permute-start | bytes 786440 | tf_op jit(solution)/shard_map/ppermute | solution.py:467
  119.6 12.4 %collective-permute-start.17 = (bf16[1,2,64,1024]{3,2,1,0:T(8,128)(2,1)S(1)}, bf16[1,2,64,1024]{3,2,1,0:T(8,128)(2,1)S(1)}, u32[]{:S(2)}, u32[]{:S(2)}) collective-permute-start(bf16[1,2,64,1024]{3,2,1,0:T(8,128)(2,1)S(1)} %get-tuple-element.52), channel_id=1, source_target_pairs={{0,4},{4,0},{8,12},{12,8},{16,20},{20,16},{24,28},{28,24},{1,5},{5... | collective-permute-start | bytes 786440 | tf_op jit(solution)/shard_map/ppermute | solution.py:467
  123.5 13.2 %collective-permute-start.24 = (bf16[1,2,64,1024]{3,2,1,0:T(8,128)(2,1)S(1)}, bf16[1,2,64,1024]{3,2,1,0:T(8,128)(2,1)S(1)}, u32[]{:S(2)}, u32[]{:S(2)}) collective-permute-start(bf16[1,2,64,1024]{3,2,1,0:T(8,128)(2,1)S(1)} %get-tuple-element.56), channel_id=1, source_target_pairs={{0,4},{4,0},{8,12},{12,8},{16,20},{20,16},{24,28},{28,24},{1,5},{5... | collective-permute-start | bytes 786440 | tf_op jit(solution)/shard_map/ppermute | solution.py:467
  126.5 18.9 %collective-permute-start.31 = (bf16[2,64,1024]{2,1,0:T(8,128)(2,1)S(1)}, bf16[2,64,1024]{2,1,0:T(8,128)(2,1)S(1)}, u32[]{:S(2)}, u32[]{:S(2)}) collective-permute-start(bf16[2,64,1024]{2,1,0:T(8,128)(2,1)S(1)} %fusion.2), channel_id=1, source_target_pairs={{0,24},{4,28},{8,0},{12,4},{16,8},{20,12},{24,16},{28,20},{1,25},{... | collective-permute-start | bytes 786440 | tf_op jit(solution)/shard_map/ppermute | solution.py:463
  132.1 13.3 %collective-permute-start.18 = (bf16[2,64,1024]{2,1,0:T(8,128)(2,1)S(1)}, bf16[2,64,1024]{2,1,0:T(8,128)(2,1)S(1)}, u32[]{:S(2)}, u32[]{:S(2)}) collective-permute-start(bf16[2,64,1024]{2,1,0:T(8,128)(2,1)S(1)} %fusion), channel_id=1, source_target_pairs={{0,8},{4,12},{8,16},{12,20},{16,24},{20,28},{24,0},{28,4},{1,9},{5... | collective-permute-start | bytes 786440 | tf_op jit(solution)/shard_map/ppermute | solution.py:463
  136.8 14.8 %collective-permute-start.25 = (bf16[2,64,1024]{2,1,0:T(8,128)(2,1)S(1)}, bf16[2,64,1024]{2,1,0:T(8,128)(2,1)S(1)}, u32[]{:S(2)}, u32[]{:S(2)}) collective-permute-start(bf16[2,64,1024]{2,1,0:T(8,128)(2,1)S(1)} %fusion.1), channel_id=1, source_target_pairs={{0,16},{4,20},{8,24},{12,28},{16,0},{20,4},{24,8},{28,12},{1,17},{... | collective-permute-start | bytes 786440 | tf_op jit(solution)/shard_map/ppermute | solution.py:463

commit v5 on v4

--- a/solution.py
+++ b/solution.py
@@ -523,7 +523,7 @@
     homes = {
         s: (*parts[name], k, half) for name, chunk in chunks.items() for k, s in enumerate(chunk)
     }
-    terms = []
+    terms, relayed = [], None
     for group in groups.values():
         shards = [(dz, dx) for dx in range(xs) for dz in group]
         outs = products(
@@ -540,6 +540,12 @@
                 terms.extend(value[k] for value in sums[::-1])
                 continue
             value = sum(value[k].astype(F32) for value in sums)
+            if dz == zs - 1 and relayed is not None:
+                value = value + relayed
+                relayed = None
+            if zs == 4 and dz == 2:
+                relayed = shift_z(value.astype(BF16), 1)
+                continue
             terms.append(shift_z(value.astype(BF16), -dz))
     turned, rhs = gather_rows(where, [[held[s] for s in chunk] for chunk in chunks.values()])
     grads = weight_grads(turned, rhs, [parts[name] for name in chunks], keeps)

time: 153 us -> 153 us (level)
  waiting for transfers between devices: 75.3 us -> 73.7 us
    ppermute x8, waiting for transfers between devices: 8.97 us -> 4.79 us  [shift_x(): return lax.ppermute(value, 'row', pairs)]
    ppermute x6, waiting for transfers between devices: 15.2 us -> 18.8 us  [shift_z(): return lax.ppermute(value, 'row', pairs)]
    ppermute x6, starting transfers between devices: 9.12 us -> 11.7 us  [shift_z(): return lax.ppermute(value, 'row', pairs)]
  transfers between devices with their start and end apart: 32 -> 32, of which waited for: 9 -> 10; matrix products, arithmetic and copies ran while one was open for 1% -> 1% of each run, Pallas kernels for 29% -> 29%
where the time goes in v5:
time: 153 us; the launch traced here: 152 us
  waiting for transfers between devices  73.7 us (48%)
  Pallas kernels  45.2 us (30%)
  starting transfers between devices  30 us (20%)
  other arithmetic  2.54 us (2%)
    ppermute x6, waiting for transfers between devices, shift_y(): return lax.ppermute(value, 'col', pairs)  50.2 us
    ppermute x6, waiting for transfers between devices, shift_z(): return lax.ppermute(value, 'row', pairs)  18.8 us
    pallas_call x5, Pallas kernels, partials(): pl.pallas_call(body, in_specs=[SMEM] + [VMEM] * (n + 3), out_specs=[VMEM]...  14.9 us
    pallas_call x4, Pallas kernels, products(): pl.pallas_call(body, in_specs=[VMEM] * (n + 3), out_specs=[VMEM] * outs_n...  11.8 us
    ppermute x6, starting transfers between devices, shift_z(): return lax.ppermute(value, 'row', pairs)  11.7 us
    pallas_call x1, Pallas kernels, weight_grads(): pl.pallas_call(body, in_specs=[VMEM] * (m + 5), out_specs=[HBM] * 3, out_...  8.48 us
    ppermute x8, starting transfers between devices, shift_x(): return lax.ppermute(value, 'row', pairs)  7.84 us
    ppermute x6, starting transfers between devices, shift_y(): return lax.ppermute(value, 'col', pairs)  7.35 us
  transfers between devices with their start and end apart: 32, of which 10 were waited for; matrix products, arithmetic and copies ran while one was open for 1% of the time, Pallas kernels for 29%

profile of v5, /device:TPU:0, one launch (start us, length us, event | category | flops | bytes accessed | tf_op | source)
XLA Modules:
  0.0 152.4 jit_solution(14779891877339429077)
XLA Ops:
  0.6 1.0 pad_maximum_fusion.pair.refs_0_
  1.6 4.1 %collective-permute-start.18 = (bf16[2,64,1024]{2,1,0:T(8,128)(2,1)S(1)}, bf16[2,64,1024]{2,1,0:T(8,128)(2,1)S(1)}, u32[]{:S(2)}, u32[]{:S(2)}) collective-permute-start(bf16[2,64,1024]{2,1,0:T(8,128)(2,1)S(1)} %pad_maximum_fusion.pair.refs_0_), channel_id=1, source_target_pairs={{0,16},{4,20},{8,24},{12,28},{16,0},{20,4},{24,8},{28,12},{1,17},{... | collective-permute-start | bytes 786440 | tf_op jit(solution)/shard_map/ppermute | solution.py:463
  5.8 1.6 %collective-permute-start.8 = (bf16[2,64,1024]{2,1,0:T(8,128)(2,1)S(1)}, bf16[2,64,1024]{2,1,0:T(8,128)(2,1)S(1)}, u32[]{:S(2)}, u32[]{:S(2)}) collective-permute-start(bf16[2,64,1024]{2,1,0:T(8,128)(2,1)S(1)} %pad_maximum_fusion.pair.refs_0_), channel_id=1, source_target_pairs={{0,8},{4,12},{8,16},{12,20},{16,24},{20,28},{24,0},{28,4},{1,9},{5... | collective-permute-start | bytes 786440 | tf_op jit(solution)/shard_map/ppermute | solution.py:463
  7.3 0.1 pad_add_fusion.1.where_ref
  7.4 0.8 pad_add_fusion.masks_ref
  8.2 15.1 %collective-permute-done.18.refs_0_.refs_4_ = bf16[2,64,1024]{2,1,0:T(8,128)(2,1)S(1)} collective-permute-done((bf16[2,64,1024]{2,1,0:T(8,128)(2,1)S(1)}, bf16[2,64,1024]{2,1,0:T(8,128)(2,1)S(1)}, u32[]{:S(2)}, u32[]{:S(2)}) %collective-permute-start.18) | collective-permute-done | bytes 262176 | tf_op jit(solution)/shard_map/ppermute | solution.py:463
  23.3 1.5 %collective-permute-start.19 = (bf16[2,64,1024]{2,1,0:T(8,128)(2,1)S(1)}, bf16[2,64,1024]{2,1,0:T(8,128)(2,1)S(1)}, u32[]{:S(2)}, u32[]{:S(2)}) collective-permute-start(bf16[2,64,1024]{2,1,0:T(8,128)(2,1)S(1)} %collective-permute-done.18.refs_0_.refs_4_), channel_id=1, source_target_pairs={{0,4},{4,0},{8,12},{12,8},{16,20},{20,16},{24,28},{28,24},{1,5},{5... | collective-permute-start | bytes 786440 | tf_op jit(solution)/shard_map/ppermute | solution.py:467
  24.8 5.9 %first_partials.1 = (f32[3,32,1792]{2,1,0:T(8,128)S(1)}, f32[3,32,1792]{2,1,0:T(8,128)S(1)}, bf16[1024,1792]{1,0:T(8,128)(2,1)S(1)}, bf16[1024,1792]{1,0:T(8,128...) custom-call(s32[3]{0:T(128)S(1)} %pad_add_fusion.1.where_ref, ...), custom_call_target="tpu_custom_call" | custom-call | flops 704643072 | bytes 23830528 | tf_op jit(solution)/shard_map/first_partials/pallas_call | solution.py:161
  30.8 0.1 collective-permute-start
  30.9 0.6 collective-permute-start.3
  31.5 1.5 %collective-permute-start.26 = (bf16[2,64,1024]{2,1,0:T(8,128)(2,1)S(1)}, bf16[2,64,1024]{2,1,0:T(8,128)(2,1)S(1)}, u32[]{:S(2)}, u32[]{:S(2)}) collective-permute-start(bf16[2,64,1024]{2,1,0:T(8,128)(2,1)S(1)} %collective-permute-done.8.refs_0_.refs_1_), channel_id=1, source_target_pairs={{0,4},{4,0},{8,12},{12,8},{16,20},{20,16},{24,28},{28,24},{1,5},{5... | collective-permute-start | bytes 786440 | tf_op jit(solution)/shard_map/ppermute | solution.py:467
  33.0 2.8 %partials.8 = (f32[3,64,1792]{2,1,0:T(8,128)S(1)}, f32[3,64,1792]{2,1,0:T(8,128)S(1)}) custom-call(s32[3]{0:T(128)S(1)} %pad_add_fusion.1.where_ref, bf16[2,64,1024]{2,1,0:T(8,128)(2,1)S(1)} %collective-permute-done.18.refs_0_.refs_4_, bf16[2,64,1024]{2,1,0:T(8,128)(2,1)S(1)} %collective-permute-done.19.refs_1_.refs_5_, ...), custom_call_target="tpu_custom_call" | custom-call | flops 1409286144 | bytes 14286848 | tf_op jit(solution)/shard_map/partials/pallas_call | solution.py:211
  35.9 0.1 collective-permute-start.20
  35.9 3.6 %collective-permute-done.9.refs_1_.refs_2_ = bf16[2,64,1024]{2,1,0:T(8,128)(2,1)S(1)} collective-permute-done((bf16[2,64,1024]{2,1,0:T(8,128)(2,1)S(1)}, bf16[2,64,1024]{2,1,0:T(8,128)(2,1)S(1)}, u32[]{:S(2)}, u32[]{:S(2)}) %collective-permute-start.9) | collective-permute-done | bytes 262176 | tf_op jit(solution)/shard_map/ppermute | solution.py:463
  39.6 0.5 collective-permute-start.13
  40.1 2.8 %partials.6 = (f32[3,64,1792]{2,1,0:T(8,128)S(1)}, bf16[3,64,1792]{2,1,0:T(8,128)(2,1)S(1)}) custom-call(s32[3]{0:T(128)S(1)} %pad_add_fusion.1.where_ref, bf16[2,64,1024]{2,1,0:T(8,128)(2,1)S(1)} %collective-permute-done.8.refs_0_.refs_1_, bf16[2,64,1024]{2,1,0:T(8,128)(2,1)S(1)} %collective-permute-done.9.refs_1_.refs_2_, ...), custom_call_target="tpu_custom_call" | custom-call | flops 1409286144 | bytes 13598720 | tf_op jit(solution)/shard_map/partials/pallas_call | solution.py:211
  42.9 0.1 collective-permute-start.10
  43.0 3.0 %partials.5 = (f32[3,32,1792]{2,1,0:T(8,128)S(1)}, f32[3,32,1792]{2,1,0:T(8,128)S(1)}) custom-call(s32[3]{0:T(128)S(1)} %pad_add_fusion.1.where_ref, bf16[2,64,1024]{2,1,0:T(8,128)(2,1)S(1)} %collective-permute-done.3.refs_0_.refs_7_, bf16[1024,1792]{1,0:T(8,128)(2,1)S(1)} %get-tuple-element.40.refs_1_.refs_4_.refs_2_, ...), custom_call_target="tpu_custom_call" | custom-call | flops 704643072 | bytes 12648448 | tf_op jit(solution)/shard_map/partials/pallas_call | solution.py:211
  46.0 0.6 collective-permute-start.4
  46.6 3.0 %partials.9 = (f32[3,32,1792]{2,1,0:T(8,128)S(1)}, f32[3,32,1792]{2,1,0:T(8,128)S(1)}) custom-call(s32[3]{0:T(128)S(1)} %pad_add_fusion.1.where_ref, bf16[2,64,1024]{2,1,0:T(8,128)(2,1)S(1)} %collective-permute-done.26.refs_0_.refs_3_, bf16[1024,1792]{1,0:T(8,128)(2,1)S(1)} %get-tuple-element.40.refs_1_.refs_4_.refs_2_, ...), custom_call_target="tpu_custom_call" | custom-call | flops 704643072 | bytes 12648448 | tf_op jit(solution)/shard_map/partials/pallas_call | solution.py:211
  49.6 1.2 collective-permute-done.13.refs_0_.refs_6_
  50.8 3.2 %partials.7 = (f32[3,32,1792]{2,1,0:T(8,128)S(1)}, f32[3,32,1792]{2,1,0:T(8,128)S(1)}) custom-call(s32[3]{0:T(128)S(1)} %pad_add_fusion.1.where_ref, bf16[2,64,1024]{2,1,0:T(8,128)(2,1)S(1)} %collective-permute-done.13.refs_0_.refs_6_, bf16[1024,1792]{1,0:T(8,128)(2,1)S(1)} %get-tuple-element.40.refs_1_.refs_4_.refs_2_, ...), custom_call_target="tpu_custom_call" | custom-call | flops 704643072 | bytes 12648448 | tf_op jit(solution)/shard_map/partials/pallas_call | solution.py:211
  54.0 0.6 collective-permute-start.14
  54.6 0.1 add_convert_fusion.5
  54.7 1.6 %collective-permute-start.1 = (bf16[3,32,1792]{2,1,0:T(8,128)(2,1)S(1)}, bf16[3,32,1792]{2,1,0:T(8,128)(2,1)S(1)}, u32[]{:S(2)}, u32[]{:S(2)}) collective-permute-start(bf16[3,32,1792]{2,1,0:T(8,128)(2,1)S(1)} %add_convert_fusion.5), channel_id=1, source_target_pairs={{0,2},{1,3},{2,0},{3,1},{4,6},{5,7},{6,4},{7,5},{8,10},{9,11},{10,... | collective-permute-start | bytes 1032200 | tf_op jit(solution)/shard_map/ppermute | solution.py:471
  56.3 0.1 add_convert_fusion.1
  56.4 0.6 collective-permute-start.11
  57.0 0.1 add_convert_fusion
  57.1 1.6 %collective-permute-start.21 = (bf16[3,64,1792]{2,1,0:T(8,128)(2,1)S(1)}, bf16[3,64,1792]{2,1,0:T(8,128)(2,1)S(1)}, u32[]{:S(2)}, u32[]{:S(2)}) collective-permute-start(bf16[3,64,1792]{2,1,0:T(8,128)(2,1)S(1)} %add_convert_fusion), channel_id=1, source_target_pairs={{0,2},{1,3},{2,0},{3,1},{4,6},{5,7},{6,4},{7,5},{8,10},{9,11},{10,... | collective-permute-start | bytes 2064392 | tf_op jit(solution)/shard_map/ppermute | solution.py:471
  58.7 0.1 add_convert_fusion.2
  58.8 0.6 collective-permute-start.28
  59.4 21.0 %collective-permute-done.11.refs_2_ = bf16[3,64,1792]{2,1,0:T(8,128)(2,1)S(1)} collective-permute-done((bf16[3,64,1792]{2,1,0:T(8,128)(2,1)S(1)}, bf16[3,64,1792]{2,1,0:T(8,128)(2,1)S(1)}, u32[]{:S(2)}, u32[]{:S(2)}) %collective-permute-start.11) | collective-permute-done | bytes 688160 | tf_op jit(solution)/shard_map/ppermute | solution.py:471
  80.4 1.5 collective-permute-start.15
  82.0 0.4 activate.8.refs_0_.refs_2_
  82.4 12.8 %collective-permute-done.21.refs_2_ = bf16[3,64,1792]{2,1,0:T(8,128)(2,1)S(1)} collective-permute-done((bf16[3,64,1792]{2,1,0:T(8,128)(2,1)S(1)}, bf16[3,64,1792]{2,1,0:T(8,128)(2,1)S(1)}, u32[]{:S(2)}, u32[]{:S(2)}) %collective-permute-start.21) | collective-permute-done | bytes 688160 | tf_op jit(solution)/shard_map/ppermute | solution.py:471
  95.2 0.4 activate.10.refs_0_.refs_6_
  95.6 0.6 collective-permute-start.22
  96.3 6.3 %collective-permute-done.28.refs_2_ = bf16[3,32,1792]{2,1,0:T(8,128)(2,1)S(1)} collective-permute-done((bf16[3,32,1792]{2,1,0:T(8,128)(2,1)S(1)}, bf16[3,32,1792]{2,1,0:T(8,128)(2,1)S(1)}, u32[]{:S(2)}, u32[]{:S(2)}) %collective-permute-start.28) | collective-permute-done | bytes 344096 | tf_op jit(solution)/shard_map/ppermute | solution.py:471
  102.6 1.5 collective-permute-start.5
  104.1 0.2 activate.11.refs_2_.refs_4_
  104.3 5.6 %collective-permute-done.15.refs_2_ = bf16[3,32,1792]{2,1,0:T(8,128)(2,1)S(1)} collective-permute-done((bf16[3,32,1792]{2,1,0:T(8,128)(2,1)S(1)}, bf16[3,32,1792]{2,1,0:T(8,128)(2,1)S(1)}, u32[]{:S(2)}, u32[]{:S(2)}) %collective-permute-start.15) | collective-permute-done | bytes 344096 | tf_op jit(solution)/shard_map/ppermute | solution.py:471
  109.9 0.2 activate.9.refs_2_.refs_8_
  110.2 0.6 collective-permute-start.16
  110.7 1.0 gather_rows.1
  111.7 0.2 activate.6.refs_0_
  112.0 4.4 %collective-permute-done.5.refs_2_ = bf16[3,32,1792]{2,1,0:T(8,128)(2,1)S(1)} collective-permute-done((bf16[3,32,1792]{2,1,0:T(8,128)(2,1)S(1)}, bf16[3,32,1792]{2,1,0:T(8,128)(2,1)S(1)}, u32[]{:S(2)}, u32[]{:S(2)}) %collective-permute-start.5) | collective-permute-done | bytes 344096 | tf_op jit(solution)/shard_map/ppermute | solution.py:471
  116.4 0.2 activate.7.refs_2_.refs_10_
  116.6 0.6 collective-permute-start.6
  117.2 3.0 %products.6 = (f32[1,2,64,1024]{3,2,1,0:T(8,128)S(1)}, bf16[1,2,64,1024]{3,2,1,0:T(8,128)(2,1)S(1)}) custom-call(bf16[3,64,1792]{2,1,0:T(8,128)(2,1)S(1)} %activate.10.refs_0_.refs_6_, bf16[3,64,1792]{2,1,0:T(8,128)(2,1)S(1)} %collective-permute-done.22.refs_1_.refs_7_, bf16[1024,1792]{1,0:T(8,128)(2,1)S(1)} %get-tuple-element.40.refs_1_.refs_4_.refs_2_, ...), custom_call_target="tpu_custom_call" | custom-call | flops 1409286144 | bytes 13172736 | tf_op jit(solution)/shard_map/products/pallas_call | solution.py:320
  120.1 0.5 collective-permute-start.23
  120.7 3.0 %products.7 = (f32[1,2,64,1024]{3,2,1,0:T(8,128)S(1)}, bf16[1,2,64,1024]{3,2,1,0:T(8,128)(2,1)S(1)}) custom-call(bf16[3,64,1792]{2,1,0:T(8,128)(2,1)S(1)} %activate.8.refs_0_.refs_2_, bf16[3,64,1792]{2,1,0:T(8,128)(2,1)S(1)} %collective-permute-done.12.refs_1_.refs_3_, bf16[3,32,1792]{2,1,0:T(8,128)(2,1)S(1)} %activate.11.refs_2_.refs_4_, ...), custom_call_target="tpu_custom_call" | custom-call | flops 1409286144 | bytes 13860864 | tf_op jit(solution)/shard_map/products/pallas_call | solution.py:320
  123.6 1.6 %collective-permute-start.30 = (bf16[1,2,64,1024]{3,2,1,0:T(8,128)(2,1)S(1)}, bf16[1,2,64,1024]{3,2,1,0:T(8,128)(2,1)S(1)}, u32[]{:S(2)}, u32[]{:S(2)}) collective-permute-start(bf16[1,2,64,1024]{3,2,1,0:T(8,128)(2,1)S(1)} %get-tuple-element.60), channel_id=1, source_target_pairs={{0,4},{4,0},{8,12},{12,8},{16,20},{20,16},{24,28},{28,24},{1,5},{5... | collective-permute-start | bytes 786440 | tf_op jit(solution)/shard_map/ppermute | solution.py:467
  125.3 3.0 %products.5 = (f32[1,2,64,1024]{3,2,1,0:T(8,128)S(1)}, bf16[1,2,64,1024]{3,2,1,0:T(8,128)(2,1)S(1)}) custom-call(bf16[3,64,1792]{2,1,0:T(8,128)(2,1)S(1)} %activate.8.refs_0_.refs_2_, bf16[3,64,1792]{2,1,0:T(8,128)(2,1)S(1)} %collective-permute-done.12.refs_1_.refs_3_, bf16[3,32,1792]{2,1,0:T(8,128)(2,1)S(1)} %activate.9.refs_2_.refs_8_, ...), custom_call_target="tpu_custom_call" | custom-call | flops 1409286144 | bytes 13860864 | tf_op jit(solution)/shard_map/products/pallas_call | solution.py:320
  128.2 0.5 collective-permute-start.17
  128.8 0.6 collective-permute-done.23
  129.4 2.0 %collective-permute-start.24 = (bf16[2,64,1024]{2,1,0:T(8,128)(2,1)S(1)}, bf16[2,64,1024]{2,1,0:T(8,128)(2,1)S(1)}, u32[]{:S(2)}, u32[]{:S(2)}) collective-permute-start(bf16[2,64,1024]{2,1,0:T(8,128)(2,1)S(1)} %fusion.1), channel_id=1, source_target_pairs={{0,8},{4,12},{8,16},{12,20},{16,24},{20,28},{24,0},{28,4},{1,9},{5... | collective-permute-start | bytes 786440 | tf_op jit(solution)/shard_map/ppermute | solution.py:463
  131.5 3.0 %products.4 = (f32[1,2,64,1024]{3,2,1,0:T(8,128)S(1)}, bf16[1,2,64,1024]{3,2,1,0:T(8,128)(2,1)S(1)}) custom-call(bf16[3,32,1792]{2,1,0:T(8,128)(2,1)S(1)} %activate.6.refs_0_, bf16[3,32,1792]{2,1,0:T(8,128)(2,1)S(1)} %collective-permute-done.2.refs_1_, bf16[3,32,1792]{2,1,0:T(8,128)(2,1)S(1)} %activate.7.refs_2_.refs_10_, ...), custom_call_target="tpu_custom_call" | custom-call | flops 1409286144 | bytes 13172736 | tf_op jit(solution)/shard_map/products/pallas_call | solution.py:320
  134.4 1.0 collective-permute-start.7
  135.5 2.1 %collective-permute-start.31 = (bf16[2,64,1024]{2,1,0:T(8,128)(2,1)S(1)}, bf16[2,64,1024]{2,1,0:T(8,128)(2,1)S(1)}, u32[]{:S(2)}, u32[]{:S(2)}) collective-permute-start(bf16[2,64,1024]{2,1,0:T(8,128)(2,1)S(1)} %fusion.2), channel_id=1, source_target_pairs={{0,24},{4,28},{8,0},{12,4},{16,8},{20,12},{24,16},{28,20},{1,25},{... | collective-permute-start | bytes 786440 | tf_op jit(solution)/shard_map/ppermute | solution.py:463
  137.6 3.0 %collective-permute-done.17 = bf16[1,2,64,1024]{3,2,1,0:T(8,128)(2,1)S(1)} collective-permute-done((bf16[1,2,64,1024]{3,2,1,0:T(8,128)(2,1)S(1)}, bf16[1,2,64,1024]{3,2,1,0:T(8,128)(2,1)S(1)}, u32[]{:S(2)}, u32[]{:S(2)}) %collective-permute-start.17) | collective-permute-done | bytes 262176 | tf_op jit(solution)/shard_map/ppermute | solution.py:467
  140.6 0.1 fusion
  140.7 1.8 %collective-permute-start.25 = (bf16[2,64,1024]{2,1,0:T(8,128)(2,1)S(1)}, bf16[2,64,1024]{2,1,0:T(8,128)(2,1)S(1)}, u32[]{:S(2)}, u32[]{:S(2)}) collective-permute-start(bf16[2,64,1024]{2,1,0:T(8,128)(2,1)S(1)} %fusion), channel_id=1, source_target_pairs={{0,8},{4,12},{8,16},{12,20},{16,24},{20,28},{24,0},{28,4},{1,9},{5... | collective-permute-start | bytes 786440 | tf_op jit(solution)/shard_map/ppermute | solution.py:463
  142.5 8.5 %weight_grads.1 = (f32[1024,1792]{1,0:T(8,128)}, f32[1024,1792]{1,0:T(8,128)}, f32[1792,1024]{1,0:T(8,128)}) custom-call(bf16[1024,512]{1,0:T(8,128)(2,1)S(1)} %get-tuple-element.63.turned_ref, bf16[512,1024]{1,0:T(8,128)(2,1)S(1)} %get-tuple-element.64.rhs_ref, bf16[3,32,1792]{2,1,0:T(8,128)(2,1)S(1)} %activate.6.refs_0_, ...), custom_call_target="tpu_custom_call" | custom-call | flops 5637144576 | bytes 29622272 | tf_op jit(solution)/shard_map/weight_grads/pallas_call | solution.py:422
  151.0 1.3 finish.1
  (31 shorter events, 0.4 us)
Async XLA Ops:
  1.6 21.7 %collective-permute-start.18 = (bf16[2,64,1024]{2,1,0:T(8,128)(2,1)S(1)}, bf16[2,64,1024]{2,1,0:T(8,128)(2,1)S(1)}, u32[]{:S(2)}, u32[]{:S(2)}) collective-permute-start(bf16[2,64,1024]{2,1,0:T(8,128)(2,1)S(1)} %pad_maximum_fusion.pair.refs_0_), channel_id=1, source_target_pairs={{0,16},{4,20},{8,24},{12,28},{16,0},{20,4},{24,8},{28,12},{1,17},{... | collective-permute-start | bytes 786440 | tf_op jit(solution)/shard_map/ppermute | solution.py:463
  5.8 25.7 %collective-permute-start.8 = (bf16[2,64,1024]{2,1,0:T(8,128)(2,1)S(1)}, bf16[2,64,1024]{2,1,0:T(8,128)(2,1)S(1)}, u32[]{:S(2)}, u32[]{:S(2)}) collective-permute-start(bf16[2,64,1024]{2,1,0:T(8,128)(2,1)S(1)} %pad_maximum_fusion.pair.refs_0_), channel_id=1, source_target_pairs={{0,8},{4,12},{8,16},{12,20},{16,24},{20,28},{24,0},{28,4},{1,9},{5... | collective-permute-start | bytes 786440 | tf_op jit(solution)/shard_map/ppermute | solution.py:463
  23.3 9.7 %collective-permute-start.19 = (bf16[2,64,1024]{2,1,0:T(8,128)(2,1)S(1)}, bf16[2,64,1024]{2,1,0:T(8,128)(2,1)S(1)}, u32[]{:S(2)}, u32[]{:S(2)}) collective-permute-start(bf16[2,64,1024]{2,1,0:T(8,128)(2,1)S(1)} %collective-permute-done.18.refs_0_.refs_4_), channel_id=1, source_target_pairs={{0,4},{4,0},{8,12},{12,8},{16,20},{20,16},{24,28},{28,24},{1,5},{5... | collective-permute-start | bytes 786440 | tf_op jit(solution)/shard_map/ppermute | solution.py:467
  30.8 23.3 %collective-permute-start = (f32[3,32,1792]{2,1,0:T(8,128)S(1)}, f32[3,32,1792]{2,1,0:T(8,128)S(1)}, u32[]{:S(2)}, u32[]{:S(2)}) collective-permute-start(f32[3,32,1792]{2,1,0:T(8,128)S(1)} %get-tuple-element.39), channel_id=1, source_target_pairs={{0,1},{1,0},{2,3},{3,2},{4,5},{5,4},{6,7},{7,6},{8,9},{9,8},{10,11... | collective-permute-start | bytes 2064392 | tf_op jit(solution)/shard_map/ppermute | solution.py:475
  30.9 8.7 %collective-permute-start.9 = (bf16[2,64,1024]{2,1,0:T(8,128)(2,1)S(1)}, bf16[2,64,1024]{2,1,0:T(8,128)(2,1)S(1)}, u32[]{:S(2)}, u32[]{:S(2)}) collective-permute-start(bf16[2,64,1024]{2,1,0:T(8,128)(2,1)S(1)} %pad_maximum_fusion.pair.refs_0_), channel_id=1, source_target_pairs={{0,24},{4,28},{8,0},{12,4},{16,8},{20,12},{24,16},{28,20},{1,25},{... | collective-permute-start | bytes 786440 | tf_op jit(solution)/shard_map/ppermute | solution.py:463
  30.9 11.9 %collective-permute-start.3 = (bf16[2,64,1024]{2,1,0:T(8,128)(2,1)S(1)}, bf16[2,64,1024]{2,1,0:T(8,128)(2,1)S(1)}, u32[]{:S(2)}, u32[]{:S(2)}) collective-permute-start(bf16[2,64,1024]{2,1,0:T(8,128)(2,1)S(1)} %pad_maximum_fusion.pair.refs_0_), channel_id=1, source_target_pairs={{0,4},{4,0},{8,12},{12,8},{16,20},{20,16},{24,28},{28,24},{1,5},{5... | collective-permute-start | bytes 786440 | tf_op jit(solution)/shard_map/ppermute | solution.py:467
  31.5 14.5 %collective-permute-start.26 = (bf16[2,64,1024]{2,1,0:T(8,128)(2,1)S(1)}, bf16[2,64,1024]{2,1,0:T(8,128)(2,1)S(1)}, u32[]{:S(2)}, u32[]{:S(2)}) collective-permute-start(bf16[2,64,1024]{2,1,0:T(8,128)(2,1)S(1)} %collective-permute-done.8.refs_0_.refs_1_), channel_id=1, source_target_pairs={{0,4},{4,0},{8,12},{12,8},{16,20},{20,16},{24,28},{28,24},{1,5},{5... | collective-permute-start | bytes 786440 | tf_op jit(solution)/shard_map/ppermute | solution.py:467
  35.9 20.6 %collective-permute-start.20 = (f32[3,64,1792]{2,1,0:T(8,128)S(1)}, f32[3,64,1792]{2,1,0:T(8,128)S(1)}, u32[]{:S(2)}, u32[]{:S(2)}) collective-permute-start(f32[3,64,1792]{2,1,0:T(8,128)S(1)} %get-tuple-element.54), channel_id=1, source_target_pairs={{0,1},{1,0},{2,3},{3,2},{4,5},{5,4},{6,7},{7,6},{8,9},{9,8},{10,11... | collective-permute-start | bytes 4128776 | tf_op jit(solution)/shard_map/ppermute | solution.py:475
  39.6 11.2 %collective-permute-start.13 = (bf16[2,64,1024]{2,1,0:T(8,128)(2,1)S(1)}, bf16[2,64,1024]{2,1,0:T(8,128)(2,1)S(1)}, u32[]{:S(2)}, u32[]{:S(2)}) collective-permute-start(bf16[2,64,1024]{2,1,0:T(8,128)(2,1)S(1)} %collective-permute-done.9.refs_1_.refs_2_), channel_id=1, source_target_pairs={{0,4},{4,0},{8,12},{12,8},{16,20},{20,16},{24,28},{28,24},{1,5},{5... | collective-permute-start | bytes 786440 | tf_op jit(solution)/shard_map/ppermute | solution.py:467
  42.9 11.8 %collective-permute-start.10 = (bf16[3,64,1792]{2,1,0:T(8,128)(2,1)S(1)}, bf16[3,64,1792]{2,1,0:T(8,128)(2,1)S(1)}, u32[]{:S(2)}, u32[]{:S(2)}) collective-permute-start(bf16[3,64,1792]{2,1,0:T(8,128)(2,1)S(1)} %get-tuple-element.48), channel_id=1, source_target_pairs={{0,1},{1,0},{2,3},{3,2},{4,5},{5,4},{6,7},{7,6},{8,9},{9,8},{10,11... | collective-permute-start | bytes 2064392 | tf_op jit(solution)/shard_map/ppermute | solution.py:475
  46.0 49.6 %collective-permute-start.4 = (f32[3,32,1792]{2,1,0:T(8,128)S(1)}, f32[3,32,1792]{2,1,0:T(8,128)S(1)}, u32[]{:S(2)}, u32[]{:S(2)}) collective-permute-start(f32[3,32,1792]{2,1,0:T(8,128)S(1)} %get-tuple-element.44), channel_id=1, source_target_pairs={{0,1},{1,0},{2,3},{3,2},{4,5},{5,4},{6,7},{7,6},{8,9},{9,8},{10,11... | collective-permute-start | bytes 2064392 | tf_op jit(solution)/shard_map/ppermute | solution.py:475
  50.8 6.3 %collective-permute-start.27 = (f32[3,32,1792]{2,1,0:T(8,128)S(1)}, f32[3,32,1792]{2,1,0:T(8,128)S(1)}, u32[]{:S(2)}, u32[]{:S(2)}) collective-permute-start(f32[3,32,1792]{2,1,0:T(8,128)S(1)} %get-tuple-element.58), channel_id=1, source_target_pairs={{0,1},{1,0},{2,3},{3,2},{4,5},{5,4},{6,7},{7,6},{8,9},{9,8},{10,11... | collective-permute-start | bytes 2064392 | tf_op jit(solution)/shard_map/ppermute | solution.py:475
  54.0 4.7 %collective-permute-start.14 = (f32[3,32,1792]{2,1,0:T(8,128)S(1)}, f32[3,32,1792]{2,1,0:T(8,128)S(1)}, u32[]{:S(2)}, u32[]{:S(2)}) collective-permute-start(f32[3,32,1792]{2,1,0:T(8,128)S(1)} %get-tuple-element.50), channel_id=1, source_target_pairs={{0,1},{1,0},{2,3},{3,2},{4,5},{5,4},{6,7},{7,6},{8,9},{9,8},{10,11... | collective-permute-start | bytes 2064392 | tf_op jit(solution)/shard_map/ppermute | solution.py:475
  54.7 55.5 %collective-permute-start.1 = (bf16[3,32,1792]{2,1,0:T(8,128)(2,1)S(1)}, bf16[3,32,1792]{2,1,0:T(8,128)(2,1)S(1)}, u32[]{:S(2)}, u32[]{:S(2)}) collective-permute-start(bf16[3,32,1792]{2,1,0:T(8,128)(2,1)S(1)} %add_convert_fusion.5), channel_id=1, source_target_pairs={{0,2},{1,3},{2,0},{3,1},{4,6},{5,7},{6,4},{7,5},{8,10},{9,11},{10,... | collective-permute-start | bytes 1032200 | tf_op jit(solution)/shard_map/ppermute | solution.py:471
  56.4 24.0 %collective-permute-start.11 = (bf16[3,64,1792]{2,1,0:T(8,128)(2,1)S(1)}, bf16[3,64,1792]{2,1,0:T(8,128)(2,1)S(1)}, u32[]{:S(2)}, u32[]{:S(2)}) collective-permute-start(bf16[3,64,1792]{2,1,0:T(8,128)(2,1)S(1)} %add_convert_fusion.1), channel_id=1, source_target_pairs={{0,2},{1,3},{2,0},{3,1},{4,6},{5,7},{6,4},{7,5},{8,10},{9,11},{10,... | collective-permute-start | bytes 2064392 | tf_op jit(solution)/shard_map/ppermute | solution.py:471
  57.1 38.1 %collective-permute-start.21 = (bf16[3,64,1792]{2,1,0:T(8,128)(2,1)S(1)}, bf16[3,64,1792]{2,1,0:T(8,128)(2,1)S(1)}, u32[]{:S(2)}, u32[]{:S(2)}) collective-permute-start(bf16[3,64,1792]{2,1,0:T(8,128)(2,1)S(1)} %add_convert_fusion), channel_id=1, source_target_pairs={{0,2},{1,3},{2,0},{3,1},{4,6},{5,7},{6,4},{7,5},{8,10},{9,11},{10,... | collective-permute-start | bytes 2064392 | tf_op jit(solution)/shard_map/ppermute | solution.py:471
  58.8 43.8 %collective-permute-start.28 = (bf16[3,32,1792]{2,1,0:T(8,128)(2,1)S(1)}, bf16[3,32,1792]{2,1,0:T(8,128)(2,1)S(1)}, u32[]{:S(2)}, u32[]{:S(2)}) collective-permute-start(bf16[3,32,1792]{2,1,0:T(8,128)(2,1)S(1)} %add_convert_fusion.2), channel_id=1, source_target_pairs={{0,2},{1,3},{2,0},{3,1},{4,6},{5,7},{6,4},{7,5},{8,10},{9,11},{10,... | collective-permute-start | bytes 1032200 | tf_op jit(solution)/shard_map/ppermute | solution.py:471
  80.4 29.5 %collective-permute-start.15 = (bf16[3,32,1792]{2,1,0:T(8,128)(2,1)S(1)}, bf16[3,32,1792]{2,1,0:T(8,128)(2,1)S(1)}, u32[]{:S(2)}, u32[]{:S(2)}) collective-permute-start(bf16[3,32,1792]{2,1,0:T(8,128)(2,1)S(1)} %add_convert_fusion.3), channel_id=1, source_target_pairs={{0,2},{1,3},{2,0},{3,1},{4,6},{5,7},{6,4},{7,5},{8,10},{9,11},{10,... | collective-permute-start | bytes 1032200 | tf_op jit(solution)/shard_map/ppermute | solution.py:471
  95.2 25.5 %collective-permute-start.12 = (bf16[3,64,1792]{2,1,0:T(8,128)(2,1)S(1)}, bf16[3,64,1792]{2,1,0:T(8,128)(2,1)S(1)}, u32[]{:S(2)}, u32[]{:S(2)}) collective-permute-start(bf16[3,64,1792]{2,1,0:T(8,128)(2,1)S(1)} %activate.8.refs_0_.refs_2_), channel_id=1, source_target_pairs={{0,1},{1,0},{2,3},{3,2},{4,5},{5,4},{6,7},{7,6},{8,9},{9,8},{10,11... | collective-permute-start | bytes 2064392 | tf_op jit(solution)/shard_map/ppermute | solution.py:475
  95.6 20.9 %collective-permute-start.22 = (bf16[3,64,1792]{2,1,0:T(8,128)(2,1)S(1)}, bf16[3,64,1792]{2,1,0:T(8,128)(2,1)S(1)}, u32[]{:S(2)}, u32[]{:S(2)}) collective-permute-start(bf16[3,64,1792]{2,1,0:T(8,128)(2,1)S(1)} %activate.10.refs_0_.refs_6_), channel_id=1, source_target_pairs={{0,1},{1,0},{2,3},{3,2},{4,5},{5,4},{6,7},{7,6},{8,9},{9,8},{10,11... | collective-permute-start | bytes 2064392 | tf_op jit(solution)/shard_map/ppermute | solution.py:475
  102.6 13.8 %collective-permute-start.5 = (bf16[3,32,1792]{2,1,0:T(8,128)(2,1)S(1)}, bf16[3,32,1792]{2,1,0:T(8,128)(2,1)S(1)}, u32[]{:S(2)}, u32[]{:S(2)}) collective-permute-start(bf16[3,32,1792]{2,1,0:T(8,128)(2,1)S(1)} %add_convert_fusion.4), channel_id=1, source_target_pairs={{0,2},{1,3},{2,0},{3,1},{4,6},{5,7},{6,4},{7,5},{8,10},{9,11},{10,... | collective-permute-start | bytes 1032200 | tf_op jit(solution)/shard_map/ppermute | solution.py:471
  109.9 10.2 %collective-permute-start.29 = (bf16[3,32,1792]{2,1,0:T(8,128)(2,1)S(1)}, bf16[3,32,1792]{2,1,0:T(8,128)(2,1)S(1)}, u32[]{:S(2)}, u32[]{:S(2)}) collective-permute-start(bf16[3,32,1792]{2,1,0:T(8,128)(2,1)S(1)} %activate.11.refs_2_.refs_4_), channel_id=1, source_target_pairs={{0,1},{1,0},{2,3},{3,2},{4,5},{5,4},{6,7},{7,6},{8,9},{9,8},{10,11... | collective-permute-start | bytes 1032200 | tf_op jit(solution)/shard_map/ppermute | solution.py:475
  110.2 15.1 %collective-permute-start.16 = (bf16[3,32,1792]{2,1,0:T(8,128)(2,1)S(1)}, bf16[3,32,1792]{2,1,0:T(8,128)(2,1)S(1)}, u32[]{:S(2)}, u32[]{:S(2)}) collective-permute-start(bf16[3,32,1792]{2,1,0:T(8,128)(2,1)S(1)} %activate.9.refs_2_.refs_8_), channel_id=1, source_target_pairs={{0,1},{1,0},{2,3},{3,2},{4,5},{5,4},{6,7},{7,6},{8,9},{9,8},{10,11... | collective-permute-start | bytes 1032200 | tf_op jit(solution)/shard_map/ppermute | solution.py:475
  116.4 15.1 %collective-permute-start.2 = (bf16[3,32,1792]{2,1,0:T(8,128)(2,1)S(1)}, bf16[3,32,1792]{2,1,0:T(8,128)(2,1)S(1)}, u32[]{:S(2)}, u32[]{:S(2)}) collective-permute-start(bf16[3,32,1792]{2,1,0:T(8,128)(2,1)S(1)} %activate.6.refs_0_), channel_id=1, source_target_pairs={{0,1},{1,0},{2,3},{3,2},{4,5},{5,4},{6,7},{7,6},{8,9},{9,8},{10,11... | collective-permute-start | bytes 1032200 | tf_op jit(solution)/shard_map/ppermute | solution.py:475
  116.6 14.9 %collective-permute-start.6 = (bf16[3,32,1792]{2,1,0:T(8,128)(2,1)S(1)}, bf16[3,32,1792]{2,1,0:T(8,128)(2,1)S(1)}, u32[]{:S(2)}, u32[]{:S(2)}) collective-permute-start(bf16[3,32,1792]{2,1,0:T(8,128)(2,1)S(1)} %activate.7.refs_2_.refs_10_), channel_id=1, source_target_pairs={{0,1},{1,0},{2,3},{3,2},{4,5},{5,4},{6,7},{7,6},{8,9},{9,8},{10,11... | collective-permute-start | bytes 1032200 | tf_op jit(solution)/shard_map/ppermute | solution.py:475
  120.1 9.2 %collective-permute-start.23 = (bf16[1,2,64,1024]{3,2,1,0:T(8,128)(2,1)S(1)}, bf16[1,2,64,1024]{3,2,1,0:T(8,128)(2,1)S(1)}, u32[]{:S(2)}, u32[]{:S(2)}) collective-permute-start(bf16[1,2,64,1024]{3,2,1,0:T(8,128)(2,1)S(1)} %get-tuple-element.56), channel_id=1, source_target_pairs={{0,4},{4,0},{8,12},{12,8},{16,20},{20,16},{24,28},{28,24},{1,5},{5... | collective-permute-start | bytes 786440 | tf_op jit(solution)/shard_map/ppermute | solution.py:467
  123.6 11.8 %collective-permute-start.30 = (bf16[1,2,64,1024]{3,2,1,0:T(8,128)(2,1)S(1)}, bf16[1,2,64,1024]{3,2,1,0:T(8,128)(2,1)S(1)}, u32[]{:S(2)}, u32[]{:S(2)}) collective-permute-start(bf16[1,2,64,1024]{3,2,1,0:T(8,128)(2,1)S(1)} %get-tuple-element.60), channel_id=1, source_target_pairs={{0,4},{4,0},{8,12},{12,8},{16,20},{20,16},{24,28},{28,24},{1,5},{5... | collective-permute-start | bytes 786440 | tf_op jit(solution)/shard_map/ppermute | solution.py:467
  128.2 12.4 %collective-permute-start.17 = (bf16[1,2,64,1024]{3,2,1,0:T(8,128)(2,1)S(1)}, bf16[1,2,64,1024]{3,2,1,0:T(8,128)(2,1)S(1)}, u32[]{:S(2)}, u32[]{:S(2)}) collective-permute-start(bf16[1,2,64,1024]{3,2,1,0:T(8,128)(2,1)S(1)} %get-tuple-element.52), channel_id=1, source_target_pairs={{0,4},{4,0},{8,12},{12,8},{16,20},{20,16},{24,28},{28,24},{1,5},{5... | collective-permute-start | bytes 786440 | tf_op jit(solution)/shard_map/ppermute | solution.py:467
  129.4 11.2 %collective-permute-start.24 = (bf16[2,64,1024]{2,1,0:T(8,128)(2,1)S(1)}, bf16[2,64,1024]{2,1,0:T(8,128)(2,1)S(1)}, u32[]{:S(2)}, u32[]{:S(2)}) collective-permute-start(bf16[2,64,1024]{2,1,0:T(8,128)(2,1)S(1)} %fusion.1), channel_id=1, source_target_pairs={{0,8},{4,12},{8,16},{12,20},{16,24},{20,28},{24,0},{28,4},{1,9},{5... | collective-permute-start | bytes 786440 | tf_op jit(solution)/shard_map/ppermute | solution.py:463
  134.4 16.6 %collective-permute-start.7 = (bf16[1,2,64,1024]{3,2,1,0:T(8,128)(2,1)S(1)}, bf16[1,2,64,1024]{3,2,1,0:T(8,128)(2,1)S(1)}, u32[]{:S(2)}, u32[]{:S(2)}) collective-permute-start(bf16[1,2,64,1024]{3,2,1,0:T(8,128)(2,1)S(1)} %get-tuple-element.46), channel_id=1, source_target_pairs={{0,4},{4,0},{8,12},{12,8},{16,20},{20,16},{24,28},{28,24},{1,5},{5... | collective-permute-start | bytes 786440 | tf_op jit(solution)/shard_map/ppermute | solution.py:467
  135.5 15.5 %collective-permute-start.31 = (bf16[2,64,1024]{2,1,0:T(8,128)(2,1)S(1)}, bf16[2,64,1024]{2,1,0:T(8,128)(2,1)S(1)}, u32[]{:S(2)}, u32[]{:S(2)}) collective-permute-start(bf16[2,64,1024]{2,1,0:T(8,128)(2,1)S(1)} %fusion.2), channel_id=1, source_target_pairs={{0,24},{4,28},{8,0},{12,4},{16,8},{20,12},{24,16},{28,20},{1,25},{... | collective-permute-start | bytes 786440 | tf_op jit(solution)/shard_map/ppermute | solution.py:463
  140.7 10.3 %collective-permute-start.25 = (bf16[2,64,1024]{2,1,0:T(8,128)(2,1)S(1)}, bf16[2,64,1024]{2,1,0:T(8,128)(2,1)S(1)}, u32[]{:S(2)}, u32[]{:S(2)}) collective-permute-start(bf16[2,64,1024]{2,1,0:T(8,128)(2,1)S(1)} %fusion), channel_id=1, source_target_pairs={{0,8},{4,12},{8,16},{12,20},{16,24},{20,28},{24,0},{28,4},{1,9},{5... | collective-permute-start | bytes 786440 | tf_op jit(solution)/shard_map/ppermute | solution.py:463
